TPU v7x, 32 devices: a whole 2x2x4 slice. The times are simulated.
32 devices in a mesh: cp: 8 (over z, y), sp: 4 (over x, core).
Axes of the slice: x: 2, y: 2, z: 4, core: 2. Of those that a mesh axis runs over, the one named last changes fastest.
Arguments:
- tokens: bfloat16 [16, 2, 128, 768], P('cp', None, 'sp'), may hold values from -6 to 6
- out_grad: bfloat16 [16, 2, 128, 768], P('cp', None, 'sp'), may hold values from -6 to 6
- time_table: float32 [64, 768], replicated, may hold values from -6 to 6
- time_index: int32 [2, 8], replicated, may hold values from 0 to 63
- span_order: int32 [16], replicated, may hold values from 0 to 15, each once
- block_ids: int32 [2, 2048], replicated, may hold values from 0 to 7, never falling along the last dimension, each value on 1 to 384 neighbouring positions
- w_ada: bfloat16 [768, 4608], P('cp'), may hold values from -0.21875 to 0.21875
- b_ada: bfloat16 [4608], P('cp'), may hold values from -3 to 3
- w_qkv: bfloat16 [768, 2304], P('cp'), may hold values from -0.21875 to 0.21875
- w_out: bfloat16 [768, 768], P('cp'), may hold values from -0.875 to 0.875
- w_up: bfloat16 [768, 3072], P('cp'), may hold values from -0.21875 to 0.21875
- w_down: bfloat16 [3072, 768], P('cp'), may hold values from -0.109375 to 0.109375
Outputs:
- block_out: bfloat16 [16, 2, 128, 768], P('cp', None, 'sp')
- grad_tokens: float32 [16, 2, 128, 768], P('cp', None, 'sp')
- grad_w_ada: float32 [768, 4608], P('cp')
- grad_b_ada: float32 [4608], P('cp')
- grad_w_qkv: float32 [768, 2304], P('cp')
- grad_w_out: float32 [768, 768], P('cp')
- grad_w_up: float32 [768, 3072], P('cp')
- grad_w_down: float32 [3072, 768], P('cp')
Inputs may be any that keep to these rules, and one draw needn't show every extreme that they name: `span_order`: a permutation of the 16 spans of a sequence; slot s lies on index s // 2 of cp. `block_ids`: never falling along a sequence; all 8 blocks occur, each with 1 to 384 tokens.
All inputs are finite; a program needn't handle non-finite values.
Results may differ from a plain program's by a relative error of at most 0.038.
Values may be sent and summed in bfloat16 or wider, within the bound.
No kernel may reach another device: no remote copies, remote signals or barrier semaphores. Data moves between devices by JAX's collectives and lax.ppermute only.
A program may use at most 192 MiB of HBM per device.

v0:
```python
import functools
import math

import jax
import jax.numpy as jnp
from jax import lax
from jax.experimental import pallas as pl
from jax.experimental.pallas import tpu as pltpu
from jax.sharding import PartitionSpec as P

HD = 64
HEADS = 3
GROUP = 3 * HD
EPS = 1e-06
MASKED = -1e30
BF = jnp.bfloat16
F32 = jnp.float32
VM = pl.BlockSpec(memory_space=pltpu.VMEM)
SM = pl.BlockSpec(memory_space=pltpu.SMEM)


def call(kernel, outs, ins, scratch=(), name=None):
    return pl.pallas_call(
        kernel,
        out_shape=[jax.ShapeDtypeStruct(shape, kind) for shape, kind in outs],
        in_specs=[SM] + [VM] * (len(ins) - 1),
        out_specs=[VM] * len(outs),
        scratch_shapes=[pltpu.VMEM(shape, kind) for shape, kind in scratch],
        compiler_params=pltpu.CompilerParams(vmem_limit_bytes=60 * 1024 * 1024),
        name=name,
    )(*ins)


def dot(a, b):
    return lax.dot_general(a, b, (((1,), (0,)), ((), ())), preferred_element_type=F32)


def dot_nt(a, b):
    return lax.dot_general(a, b, (((1,), (1,)), ((), ())), preferred_element_type=F32)


def dot_tn(a, b):
    return lax.dot_general(a, b, (((0,), (0,)), ((), ())), preferred_element_type=F32)


def normalize(x):
    center = x - jnp.mean(x, axis=-1, keepdims=True)
    inv = lax.rsqrt(jnp.mean(center * center, axis=-1, keepdims=True) + EPS)
    return center * inv, inv


def norm_back(m, n, inv):
    return inv * (
        m - jnp.mean(m, axis=-1, keepdims=True) - n * jnp.mean(m * n, axis=-1, keepdims=True)
    )


def onehot(ids_col, count):
    rows = ids_col.shape[0]
    return jnp.where(
        lax.broadcasted_iota(jnp.int32, (rows, count), 1) == ids_col, 1.0, 0.0
    ).astype(BF)


def onehot_t(ids_row, count):
    cols = ids_row.shape[1]
    return jnp.where(
        lax.broadcasted_iota(jnp.int32, (count, cols), 0) == ids_row, 1.0, 0.0
    ).astype(BF)


def turn(x, cosine, sine):
    lane = lax.broadcasted_iota(jnp.int32, cosine.shape, 1) % HD
    parts = []
    for i in range(x.shape[1] // 128):
        piece = x[:, 128 * i : 128 * (i + 1)]
        swapped = jnp.where(
            lane < HD // 2, pltpu.roll(piece, 128 - HD // 2, 1), pltpu.roll(piece, HD // 2, 1)
        )
        parts.append(piece * cosine + swapped * sine)
    return jnp.concatenate(parts, axis=1)


def turn_back(x, cosine, sine):
    lane = lax.broadcasted_iota(jnp.int32, cosine.shape, 1) % HD
    parts = []
    for i in range(x.shape[1] // 128):
        piece = x[:, 128 * i : 128 * (i + 1)]
        other = piece * sine
        swapped = jnp.where(
            lane < HD // 2, pltpu.roll(other, 128 - HD // 2, 1), pltpu.roll(other, HD // 2, 1)
        )
        parts.append(piece * cosine + swapped)
    return jnp.concatenate(parts, axis=1)


def pack_kernel(
    mod_rows, seqs, sc, tok, cond, w_ada, bias, wq, w_up, w_down, w_proj, send, shard
):
    width = tok.shape[-1]
    s = sc[1]
    slots, _, rows, _ = tok.shape
    span = slots * rows
    blocks = mod_rows // seqs
    first = dot(cond[...], w_ada[:, : 2 * width]) + bias[:, : 2 * width]
    at = pl.multiple_of((2 + s) * width, 128)
    rest = (dot(cond[...], w_ada[:, pl.ds(at, width)]) + bias[:, pl.ds(at, width)]).astype(BF)
    for i in range(8):
        seq, hg = i % 2, i // 2
        for slot in range(slots):
            send[i, slot * rows : (slot + 1) * rows, :] = tok[slot, seq]
        mine = first[seq * blocks : (seq + 1) * blocks]
        send[i, span : span + 2 * blocks, :] = jnp.concatenate(
            [mine[:, :width], mine[:, width:]], axis=0
        ).astype(BF)
        send[i, span + 2 * blocks :, :] = jnp.concatenate(
            [
                wq[:, t * width + hg * GROUP : t * width + (hg + 1) * GROUP]
                for t in (0, 1, 2, 2)
            ],
            axis=1,
        )
    inner = w_down.shape[0] // 4
    n_c = w_up.shape[1] // (4 * inner)
    rows = w_up.shape[0]
    shard[rows : rows + inner, :] = w_down[pl.ds(pl.multiple_of(inner * s, 8), inner), :]
    shard[rows + inner : 2 * rows + inner, :] = w_proj[...]
    shard[2 * rows + inner :, :] = rest
    for own in range(4):

        @pl.when(s == own)
        def _(own=own):
            shard[:rows, :] = jnp.concatenate(
                [
                    w_up[:, (4 * c + own) * inner : (4 * c + own + 1) * inner]
                    for c in range(n_c)
                ],
                axis=1,
            )


def qkv_kernel(blocks, span, fast, n_w, *refs):
    sc, tok, mod_one, ids, cos, sin = refs[:6]
    w_refs = refs[6 : 6 + n_w]
    q_out, kv_out, h_out, n_out, w_out_ref, one_out = refs[6 + n_w : 12 + n_w]
    w_scr = refs[12 + n_w]
    width = tok.shape[-1]
    s = sc[1]
    if fast:
        at = span
        one = jnp.zeros((2 * blocks, width), F32)
        for i in range(8):
            one = one + tok[i, at : at + 2 * blocks, :].astype(F32)
        rows = width // 32
        for m in range(4):
            for i in range(8):
                where = pl.multiple_of(4 * rows * i + rows * (s ^ m), 8)
                w_scr[pl.ds(where, rows), :] = w_refs[m][
                    i * rows : (i + 1) * rows, : 3 * GROUP
                ].astype(F32)
        w = w_scr[...].astype(BF)
    else:
        one = mod_one[...].astype(F32)
        w = w_refs[0][...]
    one = one.astype(BF)
    one_out[...] = one
    w_out_ref[...] = w
    x = jnp.concatenate([tok[i, :span, :] for i in range(8)], axis=0).astype(F32)
    n, _ = normalize(x)
    sel = onehot(ids[...], blocks)
    shift = dot(sel, one[:blocks])
    scale = dot(sel, one[blocks:])
    h = (n * (1.0 + scale) + shift).astype(BF)
    h_out[...] = h
    n_out[...] = n.astype(BF)
    p = dot(h, w)
    qk = turn(p[:, : 2 * GROUP], cos[...], sin[...])
    q_out[...] = (qk[:, :GROUP].astype(BF).astype(F32) * (1.0 / math.sqrt(HD))).astype(BF)
    kv_out[...] = jnp.concatenate([qk[:, GROUP:], p[:, 2 * GROUP :]], axis=1).astype(BF)


def attend_small_kernel(
    sc, q, kv0, kv1, kv2, kv3, kid, qid, o_low, o_full, lse, kv, scores, acc, top, low
):
    for m, part in enumerate((kv0, kv1, kv2, kv3)):
        kv[m] = part[...]
    top[...] = jnp.full(top.shape, MASKED, F32)
    low[...] = jnp.zeros(low.shape, F32)
    acc[...] = jnp.zeros(acc.shape, F32)

    def one(m, _):
        allowed = kid[m] <= qid[...]
        for h in range(HEADS):
            st = dot_nt(kv[m, :, h * HD : (h + 1) * HD], q[:, h * HD : (h + 1) * HD])
            st = jnp.where(allowed, st, MASKED)
            scores[m, h] = st
            top[h] = jnp.maximum(top[h], jnp.max(st, axis=0, keepdims=True))
        return 0

    def two(m, _):
        for h in range(HEADS):
            p = jnp.exp(scores[m, h] - top[h])
            low[h] += jnp.sum(p, axis=0, keepdims=True)
            acc[h] += dot_tn(kv[m, :, GROUP + h * HD : GROUP + (h + 1) * HD], p.astype(BF))
        return 0

    lax.fori_loop(0, 4, one, 0)
    lax.fori_loop(0, 4, two, 0)
    for h in range(HEADS):
        o = (acc[h] / low[h]).T
        o_full[:, h * HD : (h + 1) * HD] = o
        o_low[:, h * HD : (h + 1) * HD] = o.astype(BF)
        lse[h : h + 1, :] = top[h] + jnp.log(low[h])


def attend_large_kernel(sc, q, kv0, kv1, kv2, kv3, kid, qid, o_low, o_full, lse, scores):
    count = q.shape[0]
    part = kv0.shape[0]
    kvs = (kv0, kv1, kv2, kv3)
    step = 512
    for h in range(HEADS):
        qh = q[:, h * HD : (h + 1) * HD]

        def one(g, peak, m=0, h=h, qh=qh):
            rows = pl.ds(pl.multiple_of(g * step, step), step)
            st = dot_nt(kvs[m][rows, h * HD : (h + 1) * HD], qh)
            st = jnp.where(kid[m, rows, :] <= qid[...], st, MASKED)
            scores[pl.ds(pl.multiple_of(m * part + g * step, step), step), :] = st
            return jnp.maximum(peak, jnp.max(st, axis=0, keepdims=True))

        peak = jnp.full((1, count), MASKED, F32)
        for m in range(4):
            peak = lax.fori_loop(0, part // step, functools.partial(one, m=m), peak)

        def two(g, carry, m=0, h=h, peak=peak):
            total, acc = carry
            rows = pl.ds(pl.multiple_of(g * step, step), step)
            where = pl.ds(pl.multiple_of(m * part + g * step, step), step)
            p = jnp.exp(scores[where, :] - peak)
            v = kvs[m][rows, GROUP + h * HD : GROUP + (h + 1) * HD]
            return total + jnp.sum(p, axis=0, keepdims=True), acc + dot_tn(v, p.astype(BF))

        carry = (jnp.zeros((1, count), F32), jnp.zeros((HD, count), F32))
        for m in range(4):
            carry = lax.fori_loop(0, part // step, functools.partial(two, m=m), carry)
        total, acc = carry
        o = (acc / total).T
        o_full[:, h * HD : (h + 1) * HD] = o
        o_low[:, h * HD : (h + 1) * HD] = o.astype(BF)
        lse[h : h + 1, :] = peak + jnp.log(total)


def expand_kernel(sc, rest0, rest1, rest2, rest3, ids, g0, g1, g2, g3, mods, dz):
    s = sc[1]
    parts = [r[...] for r in (rest0, rest1, rest2, rest3)]
    for bit in (1, 2):
        parts = [jnp.where((s & bit) != 0, parts[i ^ bit], parts[i]) for i in range(4)]
    slots, seqs, rows, width = g0.shape
    count = slots * seqs * rows
    rest_low = parts[3]
    for i in range(3):
        mods[i] = dot(onehot(ids[:count, :], rest_low.shape[0]), parts[i])
    gate = dot(onehot(ids[...], rest_low.shape[0]), rest_low)
    mods[3] = gate[:count]
    for m, grad in enumerate((g0, g1, g2, g3)):
        for seq in range(seqs):
            for slot in range(slots):
                at = m * count + (seq * slots + slot) * rows
                g = grad[slot, seq].astype(F32)
                dz[at : at + rows, :] = (g * (1.0 + gate[at : at + rows])).astype(BF)


def project_kernel(n_w, sc, attn, tok, mods, weights, y_out, x_out, n_out, inv_out, h_out, w_out):
    width = tok.shape[-1]
    r = sc[0]
    rows = width // n_w
    for k in range(n_w):
        w_out[rows * k : rows * (k + 1), :] = weights[k, 2 * rows : 3 * rows, :]
    full = jnp.concatenate(
        [
            jnp.concatenate([attn[2 * hg + seq] for hg in range(4)], axis=1)
            for seq in range(2)
        ],
        axis=0,
    )
    y = dot(full, w_out[...])
    y_out[...] = y
    slots, seqs, rows, _ = tok.shape
    x = jnp.concatenate(
        [tok[slot, seq] for seq in range(seqs) for slot in range(slots)], axis=0
    ).astype(F32)
    x1 = x + (1.0 + mods[0]) * y
    x_out[...] = x1
    n, inv = normalize(x1)
    n_out[...] = n
    inv_out[...] = inv
    h_out[...] = (n * (1.0 + mods[2]) + mods[1]).astype(BF)


def feed_kernel(
    n_w, sc, h0, h1, h2, h3, dz_in, weights,
    z_keep, z_send, dh_keep, dh_send, h_all, act_out, du_out, up, down,
):
    width = h0.shape[1]
    rows = width // n_w
    for k in range(n_w):
        up[rows * k : rows * (k + 1), :] = weights[k, :rows, :]
        down[rows * k : rows * (k + 1), :] = weights[k, rows : 2 * rows, :]
    h = jnp.concatenate([h0[...], h1[...], h2[...], h3[...]], axis=0)
    dz = dz_in[...]
    part = h0.shape[0]
    u = dot(h, up[...])
    square = u * u
    inner = 0.7978845608028654 * (u + 0.044715 * square * u)
    t = jnp.tanh(inner)
    act = (0.5 * u * (1.0 + t)).astype(BF)
    slope = 0.5 * (1.0 + t) + 0.5 * u * (1.0 - t * t) * (
        0.7978845608028654 * (1.0 + 3.0 * 0.044715 * square)
    )
    du = (dot_nt(dz, down[...]) * slope).astype(BF)
    dh = dot_nt(du, up[...]).astype(BF)
    for m in range(4):
        (dh_keep, dh_send)[m % 2][m // 2] = dh[m * part : (m + 1) * part]
    z = dot(act, down[...]).astype(BF)
    for m in range(4):
        (z_keep, z_send)[m % 2][m // 2] = z[m * part : (m + 1) * part]
    h_all[...] = h
    act_out[...] = act
    du_out[...] = du


def feed_grad_kernel(n_w, sc, h, dz, act, du, grads):
    rows = h.shape[1] // n_w
    up = dot_tn(h[...], du[...]).astype(BF)
    down = dot_tn(act[...], dz[...]).astype(BF)
    for k in range(n_w):
        grads[k, :rows, :] = up[rows * k : rows * (k + 1)]
        grads[k, rows:, :] = down[rows * k : rows * (k + 1)]


def middle_kernel(
    sc, dh_keep, dh_recv, dh_far, mods, n_in, inv, grad, w, dx_out, dh_out, dy_out, d_out
):
    dh = (
        dh_keep[0].astype(F32) + dh_recv[0].astype(F32) + dh_far[...].astype(F32)
    )
    slots, seqs, rows, width = grad.shape
    g = jnp.concatenate(
        [grad[slot, seq] for seq in range(seqs) for slot in range(slots)], axis=0
    ).astype(F32)
    dx = g + norm_back(dh * (1.0 + mods[2]), n_in[...], inv[...])
    dx_out[...] = dx
    dh_out[...] = dh
    dy = (dx * (1.0 + mods[0])).astype(BF)
    dy_out[...] = dy
    d = dot_nt(dy, w[...]).astype(BF)
    span = slots * rows
    for seq in range(seqs):
        for hg in range(4):
            d_out[2 * hg + seq] = d[seq * span : (seq + 1) * span, hg * GROUP : (hg + 1) * GROUP]


def middle_grad_kernel(
    n_p, rows_total, sc, dx, dh, dy, n_in, y, attn, ids_row, s_out, g_keep, g_send, g_scr
):
    sel = onehot_t(ids_row[...], rows_total)
    s_out[0] = dot(sel, (dx[...] * y[...]).astype(BF))
    s_out[1] = dot(sel, dh[...].astype(BF))
    s_out[2] = dot(sel, (dh[...] * n_in[...]).astype(BF))
    full = jnp.concatenate(
        [
            jnp.concatenate([attn[2 * hg + seq] for hg in range(4)], axis=1)
            for seq in range(2)
        ],
        axis=0,
    )
    g_scr[...] = dot_tn(full, dy[...]).astype(BF)
    if n_p == 1:
        g_keep[0] = g_scr[...]
        g_send[...] = jnp.zeros(g_send.shape, BF)
    else:
        core = sc[1] & 1
        half = g_keep.shape[1]
        for i in range(n_p):
            g_keep[i] = g_scr[pl.ds(pl.multiple_of(2 * half * i + half * core, 16), half), :]
            g_send[i] = g_scr[pl.ds(pl.multiple_of(2 * half * i + half * (1 - core), 16), half), :]


def block_kernel(rows_total, sc, z_keep, z_recv, z_far, mods, x1, grad, ids_row, out, s_out):
    z = z_keep[0].astype(F32) + z_recv[0].astype(F32) + z_far[...].astype(F32)
    slots, seqs, rows, width = grad.shape
    g = jnp.concatenate(
        [grad[slot, seq] for seq in range(seqs) for slot in range(slots)], axis=0
    ).astype(F32)
    s_out[...] = dot(onehot_t(ids_row[...], rows_total), (g * z).astype(BF))
    o = (x1[...] + (1.0 + mods[3]) * z).astype(BF)
    for seq in range(seqs):
        for slot in range(slots):
            at = (seq * slots + slot) * rows
            out[slot, seq] = o[at : at + rows]


def row_sums(x):
    return lax.dot_general(
        jnp.ones((8, x.shape[1]), F32), x, (((1,), (1,)), ((), ())),
        precision=lax.Precision.HIGHEST, preferred_element_type=F32,
    )[:1]


def attend_back_small_kernel(
    sc, q, kv0, kv1, kv2, kv3, kid, qid, o_full, lse, do, dq_out, keep, send, kv, out, acc, delta
):
    for m, part in enumerate((kv0, kv1, kv2, kv3)):
        kv[m] = part[...]
    for h in range(HEADS):
        lanes = slice(h * HD, (h + 1) * HD)
        delta[h] = row_sums(do[:, lanes].astype(F32) * o_full[:, lanes])
    acc[...] = jnp.zeros(acc.shape, F32)

    def piece(m, _):
        allowed = kid[m] <= qid[...]
        for h in range(HEADS):
            lanes = slice(h * HD, (h + 1) * HD)
            others = slice(GROUP + h * HD, GROUP + (h + 1) * HD)
            k = kv[m, :, lanes]
            p = jnp.where(allowed, jnp.exp(dot_nt(k, q[:, lanes]) - lse[h : h + 1, :]), 0.0)
            g = (p * (dot_nt(kv[m, :, others], do[:, lanes]) - delta[h])).astype(BF)
            out[m, :, lanes] = dot(g, q[:, lanes]).astype(BF)
            out[m, :, others] = dot(p.astype(BF), do[:, lanes]).astype(BF)
            acc[h] += dot_tn(k, g)
        return 0

    lax.fori_loop(0, 4, piece, 0)
    for h in range(HEADS):
        dq_out[:, h * HD : (h + 1) * HD] = acc[h].T * (1.0 / math.sqrt(HD))
    for m in range(4):
        (keep, send)[m % 2][m // 2] = out[m]


def attend_back_large_kernel(
    sc, q, kv0, kv1, kv2, kv3, kid, qid, o_full, lse, do, dq_out, keep, send, dqs
):
    part = kv0.shape[0]
    step = 512
    for h in range(HEADS):
        lanes = slice(h * HD, (h + 1) * HD)
        qh = q[:, lanes]
        doh = do[:, lanes]
        delta = row_sums(doh.astype(F32) * o_full[:, lanes])
        top = lse[h : h + 1, :]
        dqs[...] = jnp.zeros(dqs.shape, F32)
        for m, kv in enumerate((kv0, kv1, kv2, kv3)):
            out = (keep, send)[m % 2].at[m // 2]

            def loop(g, c, m=m, kv=kv, out=out, qh=qh, doh=doh, delta=delta, top=top, h=h):
                rows = pl.ds(pl.multiple_of(g * step, step), step)
                k = kv[rows, h * HD : (h + 1) * HD]
                v = kv[rows, GROUP + h * HD : GROUP + (h + 1) * HD]
                p = jnp.where(kid[m, rows, :] <= qid[...], jnp.exp(dot_nt(k, qh) - top), 0.0)
                g2 = (p * (dot_nt(v, doh) - delta)).astype(BF)
                out[rows, h * HD : (h + 1) * HD] = dot(g2, qh).astype(BF)
                out[rows, GROUP + h * HD : GROUP + (h + 1) * HD] = dot(p.astype(BF), doh).astype(BF)
                dqs[...] += dot_tn(k, g2)
                return c

            lax.fori_loop(0, part // step, loop, 0)
        dq_out[:, lanes] = dqs[...].T * (1.0 / math.sqrt(HD))


def qkv_back_kernel(
    blocks, fast, sc, dq, dkv_a, dkv_b, dkv_c, w, one, ids_col, cos, sin, m_out, dh_out, d_out
):
    kv = dkv_a[0].astype(F32)
    if fast:
        kv = kv + dkv_b[0].astype(F32) + dkv_c[...].astype(F32)
    kv = kv.astype(BF).astype(F32)
    q = dq[...].astype(BF).astype(F32)
    qk = turn_back(jnp.concatenate([q, kv[:, :GROUP]], axis=1), cos[...], sin[...])
    d = jnp.concatenate([qk, kv[:, GROUP:]], axis=1).astype(BF)
    d_out[...] = d
    dh = dot_nt(d, w[...])
    dh_out[...] = dh.astype(BF)
    scale = dot(onehot(ids_col[...], blocks), one[blocks:])
    m = (dh * (1.0 + scale)).astype(BF)
    part = m.shape[0] // 8
    for i in range(8):
        m_out[i] = m[i * part : (i + 1) * part]


def qkv_grad_kernel(
    blocks, seqs, fast, sc, d, dh, h, n_in, ids_row, s_out, g_keep, g_send, g_scr
):
    sel = onehot_t(ids_row[...], blocks)
    shift_sum = dot(sel, dh[...])
    scale_sum = dot(sel, (dh[...].astype(F32) * n_in[...].astype(F32)).astype(BF))
    seq = sc[2]
    for b in range(seqs):
        s_out[0, b * blocks : (b + 1) * blocks, :] = jnp.where(seq == b, shift_sum, 0.0)
        s_out[1, b * blocks : (b + 1) * blocks, :] = jnp.where(seq == b, scale_sum, 0.0)
    g_scr[...] = dot_tn(h[...], d[...]).astype(BF)
    if fast:
        c = sc[1] & 1
        half = g_keep.shape[1]
        for i in range(8):
            g_keep[i] = g_scr[pl.ds(pl.multiple_of(2 * half * i + half * c, 16), half), :]
            g_send[i] = g_scr[pl.ds(pl.multiple_of(2 * half * i + half * (1 - c), 16), half), :]
    else:
        g_keep[0] = g_scr[...]
        g_send[...] = jnp.zeros(g_send.shape, BF)


def last_kernel(sc, m_in, tok, dx, out):
    slots, seqs, rows, width = tok.shape
    span = slots * rows
    for seq in range(seqs):
        m = m_in[seq].astype(F32)
        for hg in range(1, 4):
            m = m + m_in[2 * hg + seq].astype(F32)
        x = jnp.concatenate([tok[slot, seq] for slot in range(slots)], axis=0).astype(F32)
        n, inv = normalize(x)
        o = dx[seq * span : (seq + 1) * span, :] + norm_back(m, n, inv)
        for slot in range(slots):
            out[slot, seq] = o[slot * rows : (slot + 1) * rows]


def finish_kernel(sc, p0, p1, p2, p3, proj, proj_other, up, down, outw):
    s = sc[1]
    rows = p0.shape[0] // 2
    width = p0.shape[1]
    parts = [p0, p1, p2, p3]
    half = proj.shape[0]
    outw[pl.ds(pl.multiple_of(half * (s & 1), 8), half), :] = proj[...].astype(F32)
    outw[pl.ds(pl.multiple_of(half * (1 - (s & 1)), 8), half), :] = proj_other[...].astype(F32)
    for m in range(4):
        down[pl.ds(pl.multiple_of(rows * (s ^ m), 8), rows), :] = parts[m][rows : 2 * rows, :].astype(F32)
    ups = [p[:rows, :].astype(F32) for p in parts]
    for bit in (1, 2):
        ups = [jnp.where((s & bit) != 0, ups[i ^ bit], ups[i]) for i in range(4)]
    quarter = up.shape[1] // 4 // (width // rows)
    n_c = up.shape[1] // (4 * quarter)
    for c in range(n_c):
        up[:, 4 * quarter * c : 4 * quarter * (c + 1)] = jnp.concatenate(
            [u[:, quarter * c : quarter * (c + 1)] for u in ups], axis=1
        )


def swap(x, axis, k, size):
    return lax.ppermute(x, axis, [(i, i ^ k) for i in range(size)])


def after(x, *others):
    return lax.optimization_barrier((x,) + others)[0]


def gather_sp(x):
    far = swap(x, "sp", 2, 4)
    return [x, swap(x, "sp", 1, 4), far, swap(far, "sp", 1, 4)]


def body(
    tokens, out_grad, time_table, time_index, span_order, block_ids,
    w_ada, b_ada, w_qkv, w_out, w_up, w_down,
):
    slots, seqs, rows, width = tokens.shape
    cp = lax.axis_size("cp")
    fast = cp == 8
    groups = cp // 8
    r = lax.axis_index("cp")
    s = lax.axis_index("sp")
    j = r % 8
    group = r // 8
    seq = j % 2
    hg = j // 2
    span = slots * rows
    span_rows = 4 * rows
    blocks = time_index.shape[1]
    mod_rows = seqs * blocks
    part_rows = width // cp
    total_slots = slots * cp
    hidden = w_up.shape[1]
    count = 8 * span
    sc = jnp.stack([r, s, seq]).astype(jnp.int32)
    exchange_groups = None if fast else [[8 * g + i for i in range(8)] for g in range(groups)]

    def all_to_all(x):
        return lax.all_to_all(
            x, "cp", split_axis=0, concat_axis=0, tiled=True, axis_index_groups=exchange_groups
        )

    spans = span_order.astype(jnp.int32)
    pick = (spans[:, None] == jnp.arange(total_slots, dtype=jnp.int32)[None, :]).astype(BF)
    slot_ids = jnp.einsum(
        "ns,bst->bnt",
        pick,
        block_ids.reshape(seqs, total_slots, span_rows).astype(BF),
        preferred_element_type=F32,
    ).astype(jnp.int32)
    slot_ids = slot_ids.reshape(seqs, total_slots, 4, rows)
    own_seq = lax.dynamic_index_in_dim(slot_ids, seq, 0, keepdims=False)
    key_ids = jnp.stack(
        [
            lax.dynamic_index_in_dim(own_seq, s ^ m, 1, keepdims=False).reshape(-1)
            for m in range(4)
        ]
    )
    query_ids = lax.dynamic_slice_in_dim(key_ids[0], group * count, count, 0)
    here = lax.dynamic_slice_in_dim(slot_ids, slots * r, slots, 1)
    all_ids = jnp.concatenate(
        [
            (
                lax.dynamic_index_in_dim(here, s ^ m, 2, keepdims=False).reshape(seqs, span)
                + blocks * jnp.arange(seqs, dtype=jnp.int32)[:, None]
            ).reshape(-1)
            for m in range(4)
        ]
    )
    token_ids = all_ids[: seqs * span]
    own_spans = lax.dynamic_slice_in_dim(spans, 8 * slots * group, 8 * slots, 0)
    positions = (
        own_spans[:, None] * span_rows + s * rows + jnp.arange(rows, dtype=jnp.int32)[None, :]
    ).reshape(-1)
    lane = jnp.arange(128, dtype=jnp.int32) % HD
    frequency = jnp.exp(
        -math.log(10000.0) * 2.0 * (lane % (HD // 2)).astype(F32) / HD
    )
    angles = positions.astype(F32)[:, None] * frequency[None, :]
    cosine = jnp.cos(angles)
    sine = jnp.where(lane < HD // 2, -1.0, 1.0)[None, :] * jnp.sin(angles)

    pick_time = (
        time_index.reshape(-1)[:, None] == jnp.arange(time_table.shape[0], dtype=jnp.int32)
    ).astype(F32)
    table_part = lax.dynamic_slice_in_dim(time_table, part_rows * r, part_rows, 1)
    cond = jax.nn.silu(
        jnp.dot(pick_time, table_part, precision=lax.Precision.HIGHEST)
    ).astype(BF)
    bias = lax.dynamic_update_slice(
        jnp.zeros((1, 6 * width), F32), b_ada.astype(F32)[None, :], (0, b_ada.shape[0] * r)
    )

    if fast:
        quarter_rows = part_rows // 4
        wq = lax.dynamic_slice(w_qkv, (quarter_rows * s, 0), (quarter_rows, 3 * width))
        extra = 2 * blocks + quarter_rows
    else:
        wq = w_qkv
        extra = 0
    inner = hidden // cp // 4
    if fast:
        send, shard = call(
            functools.partial(pack_kernel, mod_rows, seqs),
            [((8, span + extra, width), BF), ((2 * part_rows + inner + mod_rows, width), BF)],
            [sc, tokens, cond, w_ada, bias, wq, w_up, w_down, w_out],
            name="pack",
        )
    else:
        send = jnp.broadcast_to(
            tokens.transpose(1, 0, 2, 3).reshape(1, seqs, span, width), (4, seqs, span, width)
        ).reshape(8, span, width)
        up_part = lax.dynamic_index_in_dim(
            w_up.reshape(part_rows, cp, 4, inner), s, 2, keepdims=False
        ).reshape(part_rows, cp * inner)
        down_part = lax.dynamic_slice_in_dim(w_down, inner * s, inner, 0)
        shard = jnp.concatenate([up_part, down_part, w_out], axis=0)
    grad_parts = gather_sp(out_grad)
    got = after(all_to_all(send), *grad_parts)
    if fast:
        w_own = got[:, span + extra - quarter_rows :, :].reshape(8 * quarter_rows, width)
        w_list = gather_sp(w_own)
        mod_one = got
    else:
        full_mod = lax.psum(
            jnp.dot(cond, w_ada, preferred_element_type=F32) + bias, "cp"
        )
        first = lax.dynamic_slice_in_dim(full_mod, seq * blocks, blocks, 0)
        mod_one = jnp.concatenate([first[:, :width], first[:, width : 2 * width]], axis=0)
        gathered = lax.all_gather(w_qkv, "cp", axis=0, tiled=True).reshape(width, 3, 4, GROUP)
        w_list = [
            lax.dynamic_index_in_dim(gathered, hg, 2, keepdims=False).reshape(width, 3 * GROUP)
        ]

    n_w = 8 if fast else 1
    weights = lax.all_gather(shard, "cp", axis=0, tiled=False)
    rests = None
    if fast:
        rest = jnp.sum(weights[:, -mod_rows:, :].astype(F32), axis=0).astype(BF)
    if not fast:
        weights = jnp.concatenate(
            [
                weights[:, at : at + part_rows].reshape(width, width)
                for at in (0, part_rows, 2 * part_rows)
            ],
            axis=0,
        )[None]

    mod_kernel_outs = [
        ((count, GROUP), BF),
        ((count, 2 * GROUP), BF),
        ((count, width), BF),
        ((count, width), BF),
        ((width, 3 * GROUP), BF),
        ((2 * blocks, width), BF),
    ]
    q, kv, h_one, n_one, w_heads, one = call(
        functools.partial(qkv_kernel, blocks, span, fast, len(w_list)),
        mod_kernel_outs,
        [sc, got, mod_one, query_ids[:, None], cosine, sine] + w_list,
        scratch=[((width, 3 * GROUP), F32)],
        name="qkv",
    )
    if not fast:
        kv = lax.all_gather(
            kv, "cp", axis=0, tiled=True,
            axis_index_groups=[[8 * g + i for g in range(groups)] for i in range(8)],
        )
    kvs = gather_sp(kv)
    key_col = key_ids[:, :, None]
    query_row = query_ids[None, :]
    part = kv.shape[0]
    wide_kv = ((4, part, 2 * GROUP), BF)
    attn, attn_full, lse = call(
        attend_small_kernel if fast else attend_large_kernel,
        [((count, GROUP), BF), ((count, GROUP), F32), ((8, count), F32)],
        [sc, q] + kvs + [key_col, query_row],
        scratch=[
            wide_kv,
            ((4, HEADS, part, count), F32),
            ((HEADS, HD, count), F32),
            ((HEADS, 1, count), F32),
            ((HEADS, 1, count), F32),
        ]
        if fast
        else [((4 * part, count), F32)],
        name="attend",
    )
    if fast:
        rests = gather_sp(after(rest, attn))
    else:
        tail = full_mod.astype(BF)
        rests = [
            lax.dynamic_slice_in_dim(tail, (2 + (s ^ m)) * width, width, 1) for m in range(4)
        ]
    mods, dz = call(
        expand_kernel,
        [((4, 2 * span, width), F32), ((8 * span, width), BF)],
        [sc] + rests + [all_ids[:, None]] + [after(grad_parts[0], attn)]
        + grad_parts[1:],
        name="expand",
    )
    attn_tok = all_to_all(attn.reshape(8, span, GROUP))
    y, x_mid, n_two, inv_two, h_two, w_out_full = call(
        functools.partial(project_kernel, n_w),
        [
            ((2 * span, width), F32),
            ((2 * span, width), F32),
            ((2 * span, width), F32),
            ((2 * span, 1), F32),
            ((2 * span, width), BF),
            ((width, width), BF),
        ],
        [sc, attn_tok, tokens, mods, weights],
        name="project",
    )
    hs = gather_sp(h_two)
    pair = ((2, 2 * span, width), BF)
    tall = ((8 * span, width), BF)
    z_keep, z_send, dh_keep, dh_send, h_all, act, du = call(
        functools.partial(feed_kernel, n_w),
        [pair, pair, pair, pair, tall, tall, tall],
        [sc] + hs + [dz, weights],
        scratch=[((width, width), BF)] * 2,
        name="feed",
    )
    def reduce_sp(keep, send):
        near = swap(send, "sp", 1, 4)
        both = (keep[1].astype(F32) + near[1].astype(F32)).astype(BF)
        return (keep, near, swap(both, "sp", 2, 4)), both

    dh_parts, dh_both = reduce_sp(dh_keep, dh_send)
    (g_feed,) = call(
        functools.partial(feed_grad_kernel, n_w),
        [((n_w, 2 * width // n_w, width), BF)],
        [sc, h_all, dz, after(act, dh_both), du],
        name="feed_grad",
    )
    if fast:
        feed = lax.psum_scatter(g_feed, "cp", scatter_dimension=0, tiled=False)
    else:
        feed = jnp.concatenate(
            [
                lax.psum_scatter(
                    g_feed[0, at : at + width].astype(F32), "cp", scatter_dimension=0, tiled=True
                )
                for at in (0, width)
            ],
            axis=0,
        )

    token_row = token_ids[None, :]
    g_out = ((8, part_rows // 2, width), BF) if fast else ((1, width, width), BF)
    wide = ((2 * span, width), F32)
    dx_mid, dh_two, dy, d_attn = call(
        middle_kernel,
        [wide, wide, ((2 * span, width), BF), ((8, span, GROUP), BF)],
        [sc] + list(dh_parts)
        + [mods, n_two, after(inv_two, g_feed), out_grad, w_out_full],
        name="middle",
    )
    s_mid, o_keep, o_send = call(
        functools.partial(middle_grad_kernel, n_w, mod_rows),
        [((3, mod_rows, width), F32), g_out, g_out],
        [sc, dx_mid, dh_two, dy, n_two, y, attn_tok, token_row],
        scratch=[((width, width), BF)],
        name="middle_grad",
    )
    d_heads = all_to_all(d_attn).reshape(count, GROUP)
    if fast:
        o_near = swap(after(o_send, d_heads), "sp", 1, 4)
        d_heads = after(d_heads, s_mid, o_send, o_keep)
    z_parts, _ = reduce_sp(after(z_keep, d_heads), after(z_send, d_heads))
    block_out, s_gate = call(
        functools.partial(block_kernel, mod_rows),
        [(tokens.shape, BF), ((mod_rows, width), F32)],
        [sc] + list(z_parts) + [mods, x_mid, out_grad, token_row],
        name="block",
    )
    dkv = ((2, part, 2 * GROUP), BF)
    dq, kv_keep, kv_send = call(
        attend_back_small_kernel if fast else attend_back_large_kernel,
        [((count, GROUP), F32), dkv, dkv],
        [sc, q] + kvs + [key_col, query_row, attn_full, lse, d_heads],
        scratch=[wide_kv, wide_kv, ((HEADS, HD, count), F32), ((HEADS, 1, count), F32)]
        if fast
        else [((HD, count), F32)],
        name="attend_back",
    )
    dkv_list, _ = reduce_sp(kv_keep, kv_send)
    if not fast:
        summed = sum(x.astype(F32) for x in (dkv_list[0][0], dkv_list[1][0], dkv_list[2]))
        summed = lax.psum_scatter(
            summed, "cp", scatter_dimension=0, tiled=True,
            axis_index_groups=[[8 * g + i for g in range(groups)] for i in range(8)],
        ).astype(BF)
        dkv_list = [summed[None], summed[None], summed]
    g_shape = ((8, part_rows // 2, 3 * GROUP), BF) if fast else ((1, width, 3 * GROUP), BF)
    m_one, dh_one, dqkv = call(
        functools.partial(qkv_back_kernel, blocks, fast),
        [((8, span, width), BF), ((count, width), BF), ((count, 3 * GROUP), BF)],
        [sc, dq] + list(dkv_list) + [w_heads, one, query_ids[:, None], cosine, sine],
        name="qkv_back",
    )
    m_tok = all_to_all(m_one)
    s_one, q_keep, q_send = call(
        functools.partial(qkv_grad_kernel, blocks, seqs, fast),
        [((2, mod_rows, width), F32), g_shape, g_shape],
        [sc, dqkv, dh_one, h_one, n_one, query_row],
        scratch=[((width, 3 * GROUP), BF)],
        name="qkv_grad",
    )
    (grad_in,) = call(
        last_kernel, [(tokens.shape, F32)], [sc, m_tok, tokens, dx_mid], name="last"
    )

    def reduce_all(x, wait=None):
        if not fast:
            return lax.psum(x, ("cp", "sp"))
        for axis, k, size in (("sp", 1, 4), ("sp", 2, 4), ("cp", 1, 8), ("cp", 2, 8), ("cp", 4, 8)):
            if k == 4:
                x = after(x, wait)
            low = x.astype(BF)
            x = low.astype(F32) + swap(low, axis, k, size).astype(F32)
        return x

    sums = reduce_all(jnp.concatenate([s_one, s_mid, s_gate[None]], axis=0), m_tok)
    sums = sums.transpose(1, 0, 2).reshape(mod_rows, 6 * width)
    grad_ada = lax.dot_general(
        cond.astype(F32), sums, (((0,), (0,)), ((), ())), precision=lax.Precision.HIGHEST
    )
    grad_bias = lax.dynamic_slice_in_dim(
        jnp.sum(sums, axis=0), b_ada.shape[0] * r, b_ada.shape[0], 0
    )

    if fast:
        half_width = width // 2
        o_sum = (o_keep.astype(F32) + after(o_near, dq).astype(F32)).astype(BF)
        far = s // 2
        mine = lax.dynamic_slice_in_dim(o_sum, half_width * far, half_width, 2)
        theirs = lax.dynamic_slice_in_dim(o_sum, half_width * (1 - far), half_width, 2)
        o_sum = (mine.astype(F32) + swap(theirs, "sp", 2, 4).astype(F32)).astype(BF)
        o_sum = o_sum.reshape(4, 2, part_rows // 2, half_width)
        mine = lax.dynamic_index_in_dim(o_sum, seq, 1, keepdims=False)
        theirs = lax.dynamic_index_in_dim(o_sum, 1 - seq, 1, keepdims=False)
        o_sum = (mine.astype(F32) + swap(theirs, "cp", 1, 8).astype(F32)).astype(BF)
        proj = sum(
            (
                swap(lax.dynamic_index_in_dim(o_sum, hg ^ m, 0, keepdims=False), "cp", 2 * m, 8)
                if m
                else lax.dynamic_index_in_dim(o_sum, hg, 0, keepdims=False)
            ).astype(F32)
            for m in range(4)
        ).astype(BF)
        other = swap(proj, "sp", 2, 4)
        proj = jnp.concatenate(
            [jnp.where(far == 0, proj, other), jnp.where(far == 0, other, proj)], axis=1
        )
        proj_other = swap(proj, "sp", 1, 4)
        near = swap(q_send, "sp", 1, 4)
        sums = (q_keep.astype(F32) + near.astype(F32)).astype(BF).reshape(
            4, 2, part_rows // 2, 3 * GROUP
        )
        ours = lax.dynamic_index_in_dim(sums, seq, 1, keepdims=False)
        theirs = lax.dynamic_index_in_dim(sums, 1 - seq, 1, keepdims=False)
        ours = (ours.astype(F32) + swap(theirs, "cp", 1, 8).astype(F32)).astype(BF)
        found = [
            swap(lax.dynamic_index_in_dim(ours, hg ^ m, 0, keepdims=False), "cp", 2 * m, 8)
            if m
            else lax.dynamic_index_in_dim(ours, hg, 0, keepdims=False)
            for m in range(4)
        ]
        for bit in (1, 2):
            found = [jnp.where((hg & bit) != 0, found[i ^ bit], found[i]) for i in range(4)]
        mine = after(jnp.stack(found), m_tok)
        mine = (mine.astype(F32) + swap(mine, "sp", 2, 4).astype(F32)).astype(BF)
        other = swap(mine, "sp", 1, 4)
        low = jnp.where(s % 2 == 0, mine, other)
        high = jnp.where(s % 2 == 0, other, mine)
        both = jnp.concatenate([low, high], axis=1)
        grad_qkv = (
            both.reshape(4, part_rows, 3, GROUP).transpose(1, 2, 0, 3).reshape(part_rows, 3 * width)
        ).astype(F32)
    else:
        proj = lax.psum_scatter(o_keep[0].astype(F32), "cp", scatter_dimension=0, tiled=True)
        proj_low = lax.psum(proj, "sp")
        own = lax.psum_scatter(q_keep[0].astype(F32), "sp", scatter_dimension=1, tiled=True)
        placed = lax.dynamic_update_slice(
            jnp.zeros((4, width, 3 * GROUP // 4), F32), own[None], (hg, 0, 0)
        )
        placed = lax.psum_scatter(placed, "cp", scatter_dimension=1, tiled=True)
        whole = lax.all_gather(placed, "sp", axis=2, tiled=True)
        grad_qkv = (
            whole.reshape(4, part_rows, 3, GROUP).transpose(1, 2, 0, 3).reshape(part_rows, 3 * width)
        )
    if fast:
        shares = gather_sp(feed.reshape(2 * part_rows, width))
        grad_up, grad_down, grad_out = call(
            finish_kernel,
            [
                ((part_rows, hidden), F32),
                ((hidden // cp, width), F32),
                ((part_rows, width), F32),
            ],
            [sc] + shares + [proj, proj_other],
            name="finish",
        )
    else:
        shares = lax.all_gather(feed, "sp", axis=0, tiled=False)
        grad_up = (
            shares[:, :part_rows]
            .reshape(4, part_rows, cp, inner)
            .transpose(1, 2, 0, 3)
            .reshape(part_rows, hidden)
        )
        grad_down = shares[:, part_rows:].reshape(hidden // cp, width)
        grad_out = proj_low
    return (
        block_out, grad_in, grad_ada, grad_bias, grad_qkv, grad_out, grad_up, grad_down,
    )


def solution(mesh):
    rows = P("cp", None, "sp", None)
    shard = P("cp", None)
    return jax.shard_map(
        body,
        mesh=mesh,
        in_specs=(
            rows, rows, P(), P(), P(), P(), shard, P("cp"), shard, shard, shard, shard,
        ),
        out_specs=(rows, rows, shard, P("cp"), shard, shard, shard, shard),
        check_vma=False,
    )
```

profile of v0, /device:TPU:1, one launch (start us, length us, event | category | flops | bytes accessed | tf_op | source)
XLA Modules:
  0.0 302.7 jit_solution(163113777315931085)
XLA Ops:
  10.0 1.7 multiply_convert_fusion.cond
  12.4 3.2 %pack.1 = (bf16[8,104,768]{2,1,0:T(8,128)(2,1)}, bf16[304,768]{1,0:T(8,128)(2,1)}) custom-call(s32[3]{0:T(128)} %pad_add_fusion.1.sc.refs_0_, bf16[2,2,32,768]{3,2,1,0:T(8,128)(2,1)} %tok.5, bf16[16,96]{1,0:T(8,128)(2,1)} %multiply_convert_fusion.cond, bf16[96,4608]{1,0:T(8,128)(2,1)} %w_ada.1, f32[1,4608]{1,0:T(1,128)} %copy-done.32, ...), custom_call_target="tpu_custom_call" | custom-call | tf_op jit(solution)/shard_map/pack/pallas_call | solution.py:23
  15.7 6.6 %all-to-all-start = ((bf16[8,104,768]{2,1,0:T(8,128)(2,1)}), bf16[8,104,768]{2,1,0:T(8,128)(2,1)S(1)}, u32[]{:S(2)}, u32[]{:S(2)}) async-start(bf16[8,104,768]{2,1,0:T(8,128)(2,1)} %get-tuple-element.67), calls=%async_computation | async-start | bytes 2555904 | tf_op jit(solution)/shard_map/all_to_all | solution.py:586
  22.3 1.2 collective-permute-start.1
  23.5 1.3 collective-permute-start
  25.0 2.9 collective-permute-done.1.g2
  27.9 1.8 collective-permute-start.2
  30.8 36.4 %all-to-all-done.refs_1_.refs_2_ = bf16[8,104,768]{2,1,0:T(8,128)(2,1)S(1)} async-done(((bf16[8,104,768]{2,1,0:T(8,128)(2,1)}), bf16[8,104,768]{2,1,0:T(8,128)(2,1)S(1)}, u32[]{:S(2)}, u32[]{:S(2)}) %all-to-all-start) | async-done | bytes 1277984 | tf_op jit(solution)/shard_map/all_to_all | solution.py:586
  67.2 1.1 collective-permute-start.4
  69.7 2.1 collective-permute-start.3
  71.8 2.3 collective-permute-done.4.refs_8_
  74.1 2.6 collective-permute-start.5
  76.7 1.8 fusion.5
  79.4 5.2 %qkv.1 = (bf16[512,192]{1,0:T(8,128)(2,1)}, bf16[512,384]{1,0:T(8,128)(2,1)}, bf16[512,768]{1,0:T(8,128)(2,1)}, bf16[512,768]{1,0:T(8,128)(2,1)}, bf16[768,576]{1,0:T(8,128)(2,1)}, /*index=5*/bf16[16,768]{1,0:T(8,128)(2,1)}) custom-call(s32[3]{0:T(128)} %pad_add_fusion.1.sc.refs_0_, bf16[8,104,768]{2,1,0:T(8,128)(2,1)} %copy-done.1, ...), custom_call_target="tpu_custom_call" | custom-call | tf_op jit(solution)/shard_map/qkv/pallas_call | solution.py:23
  85.9 9.7 %collective-permute-done.7.kv2 = bf16[512,384]{1,0:T(8,128)(2,1)S(1)} collective-permute-done((bf16[512,384]{1,0:T(8,128)(2,1)}, bf16[512,384]{1,0:T(8,128)(2,1)S(1)}, u32[]{:S(2)}, u32[]{:S(2)}) %collective-permute-start.7) | collective-permute-done | bytes 393248 | tf_op jit(solution)/shard_map/ppermute | solution.py:548
  97.1 1.3 copy.74.kid
  99.4 8.4 %attend.1 = (bf16[512,192]{1,0:T(8,128)(2,1)}, f32[512,192]{1,0:T(8,128)}, f32[8,512]{1,0:T(8,128)}) custom-call(s32[3]{0:T(128)} %pad_add_fusion.1.sc.refs_0_, bf16[512,192]{1,0:T(8,128)(2,1)} %get-tuple-element.69.q, bf16[512,384]{1,0:T(8,128)(2,1)} %get-tuple-element.70.kv0, bf16[512,384]{1,0:T(8,128)(2,1)} %copy-done.8, bf16[512,384]{1,0:T(8,128)(2,1)} %copy-done.7, ...), custom_call_target="tpu_custom_call" | custom-call | tf_op jit(solution)/shard_map/attend/pallas_call | solution.py:23
  107.8 4.6 %all-to-all-start.1 = ((bf16[8,64,192]{2,1,0:T(8,128)(2,1)}), bf16[8,64,192]{2,1,0:T(8,128)(2,1)S(1)}, u32[]{:S(2)}, u32[]{:S(2)}) async-start(bf16[8,64,192]{2,1,0:T(8,128)(2,1)} %bitcast.142), calls=%async_computation.1 | async-start | bytes 524288 | tf_op jit(solution)/shard_map/all_to_all | solution.py:586
  113.4 1.2 collective-permute-start.10
  115.2 1.3 collective-permute-done.10.rest2
  116.5 1.1 collective-permute-start.11
  119.7 3.2 %expand.1 = (f32[4,128,768]{2,1,0:T(8,128)}, bf16[512,768]{1,0:T(8,128)(2,1)}) custom-call(s32[3]{0:T(128)} %pad_add_fusion.1.sc.refs_0_, bf16[16,768]{1,0:T(8,128)(2,1)} %copy-done.31, bf16[16,768]{1,0:T(8,128)(2,1)} %copy-done.37, bf16[16,768]{1,0:T(8,128)(2,1)} %copy-done.36, bf16[16,768]{1,0:T(8,128)(2,1)} %copy-done.38, s32[512,1]{1,0:T(8,128)} %copy.79.ids, ...), custom_call_target="tpu_custom_call" | custom-call | tf_op jit(solution)/shard_map/expand/pallas_call | solution.py:23
  123.6 4.4 %project.1 = (f32[128,768]{1,0:T(8,128)}, f32[128,768]{1,0:T(8,128)}, f32[128,768]{1,0:T(8,128)}, f32[128,1]{1,0:T(8,128)}, bf16[128,768]{1,0:T(8,128)(2,1)}, /*index=5*/bf16[768,768]{1,0:T(8,128)(2,1)}) custom-call(s32[3]{0:T(128)} %pad_add_fusion.1.sc.refs_0_, bf16[8,64,192]{2,1,0:T(8,128)(2,1)} %copy-done.3, bf16[2,2,32,768]{3,2,1,0:T(8,128)(2,1)} %tok.5, ...), custom_call_target="tpu_custom_call" | custom-call | tf_op jit(solution)/shard_map/project/pallas_call | solution.py:23
  128.0 1.1 collective-permute-start.13
  129.4 5.3 %collective-permute-done.13.h2 = bf16[128,768]{1,0:T(8,128)(2,1)S(1)} collective-permute-done((bf16[128,768]{1,0:T(8,128)(2,1)}, bf16[128,768]{1,0:T(8,128)(2,1)S(1)}, u32[]{:S(2)}, u32[]{:S(2)}) %collective-permute-start.13) | collective-permute-done | bytes 196640 | tf_op jit(solution)/shard_map/ppermute | solution.py:548
  137.2 6.5 %feed.1 = (bf16[2,128,768]{2,1,0:T(8,128)(2,1)}, bf16[2,128,768]{2,1,0:T(8,128)(2,1)}, bf16[2,128,768]{2,1,0:T(8,128)(2,1)}, bf16[2,128,768]{2,1,0:T(8,128)(2,1)...) custom-call(s32[3]{0:T(128)} %pad_add_fusion.1.sc.refs_0_, ...), custom_call_target="tpu_custom_call" | custom-call | tf_op jit(solution)/shard_map/feed/pallas_call | solution.py:23
  144.1 1.6 collective-permute-done.15.dh_recv
  145.7 1.1 fusion.6
  146.8 1.2 collective-permute-start.16
  148.0 4.7 %feed_grad.1 = bf16[8,192,768]{2,1,0:T(8,128)(2,1)} custom-call(s32[3]{0:T(128)} %pad_add_fusion.1.sc.refs_0_, bf16[512,768]{1,0:T(8,128)(2,1)} %get-tuple-element.83.h, bf16[512,768]{1,0:T(8,128)(2,1)} %get-tuple-element.77.dz_in.dz, bf16[512,768]{1,0:T(8,128)(2,1)} %get-tuple-element.85.act, bf16[512,768]{1,0:T(8,128)(2,1)} %get-tuple-element.86.du), custom_call_target="tpu_custom_call" | custom-call | tf_op jit(solution)/shard_map/feed_grad/pallas_call | solution.py:23
  153.6 3.8 %middle.1 = (f32[128,768]{1,0:T(8,128)}, f32[128,768]{1,0:T(8,128)}, bf16[128,768]{1,0:T(8,128)(2,1)}, bf16[8,64,192]{2,1,0:T(8,128)(2,1)}) custom-call(s32[3]{0:T(128)} %pad_add_fusion.1.sc.refs_0_, bf16[2,128,768]{2,1,0:T(8,128)(2,1)} %get-tuple-element.79.dh_keep, bf16[2,128,768]{2,1,0:T(8,128)(2,1)} %copy-done.12, bf16[128,768]{1,0:T(8,128)(2,1)} %copy-done.25, ...), custom_call_target="tpu_custom_call" | custom-call | tf_op jit(solution)/shard_map/middle/pallas_call | solution.py:23
  157.4 5.7 %all-to-all-start.2 = ((bf16[8,64,192]{2,1,0:T(8,128)(2,1)}), bf16[8,64,192]{2,1,0:T(8,128)(2,1)S(1)}, u32[]{:S(2)}, u32[]{:S(2)}) async-start(bf16[8,64,192]{2,1,0:T(8,128)(2,1)} %get-tuple-element.89), calls=%async_computation.2 | async-start | bytes 524288 | tf_op jit(solution)/shard_map/all_to_all | solution.py:586
  164.0 3.3 %middle_grad.1 = (f32[3,16,768]{2,1,0:T(8,128)}, bf16[8,48,768]{2,1,0:T(8,128)(2,1)}, bf16[8,48,768]{2,1,0:T(8,128)(2,1)}) custom-call(s32[3]{0:T(128)} %pad_add_fusion.1.sc.refs_0_, f32[128,768]{1,0:T(8,128)} %get-tuple-element.90.dx, f32[128,768]{1,0:T(8,128)} %get-tuple-element.91.dh, bf16[128,768]{1,0:T(8,128)(2,1)} %get-tuple-element.92.dy, ...), custom_call_target="tpu_custom_call" | custom-call | tf_op jit(solution)/shard_map/middle_grad/pallas_call | solution.py:23
  167.3 3.0 all-to-all-done.2
  170.3 2.8 collective-permute-start.17
  173.1 14.0 %attend_back.1 = (f32[512,192]{1,0:T(8,128)}, bf16[2,512,384]{2,1,0:T(8,128)(2,1)}, bf16[2,512,384]{2,1,0:T(8,128)(2,1)}) custom-call(s32[3]{0:T(128)} %pad_add_fusion.1.sc.refs_0_, bf16[512,192]{1,0:T(8,128)(2,1)} %get-tuple-element.69.q, bf16[512,384]{1,0:T(8,128)(2,1)} %get-tuple-element.70.kv0, bf16[512,384]{1,0:T(8,128)(2,1)} %copy-done.8, ...), custom_call_target="tpu_custom_call" | custom-call | tf_op jit(solution)/shard_map/attend_back/pallas_call | solution.py:23
  189.6 1.1 collective-permute-start.18
  191.6 4.8 %collective-permute-done.18.z_far = bf16[128,768]{1,0:T(8,128)(2,1)} collective-permute-done((bf16[128,768]{1,0:T(8,128)(2,1)}, bf16[128,768]{1,0:T(8,128)(2,1)}, u32[]{:S(2)}, u32[]{:S(2)}) %collective-permute-start.18) | collective-permute-done | bytes 196640 | tf_op jit(solution)/shard_map/ppermute | solution.py:548
  196.4 2.8 block.1
  199.3 1.2 collective-permute-start.20
  200.5 2.2 collective-permute-done.37
  202.9 1.1 collective-permute-start.38
  204.0 4.5 %collective-permute-done.38 = bf16[4,48,384]{2,1,0:T(8,128)(2,1)S(1)} collective-permute-done((bf16[4,48,384]{2,1,0:T(8,128)(2,1)S(1)}, bf16[4,48,384]{2,1,0:T(8,128)(2,1)S(1)}, u32[]{:S(2)}, u32[]{:S(2)}) %collective-permute-start.38) | collective-permute-done | bytes 147488 | tf_op jit(solution)/shard_map/ppermute | solution.py:548
  209.8 1.5 collective-permute-start.40
  212.1 5.0 %qkv_back.1 = (bf16[8,64,768]{2,1,0:T(8,128)(2,1)}, bf16[512,768]{1,0:T(8,128)(2,1)}, bf16[512,576]{1,0:T(8,128)(2,1)}) custom-call(s32[3]{0:T(128)} %pad_add_fusion.1.sc.refs_0_, f32[512,192]{1,0:T(8,128)} %get-tuple-element.105.dq, bf16[2,512,384]{2,1,0:T(8,128)(2,1)} %get-tuple-element.106.dkv_a, bf16[2,512,384]{2,1,0:T(8,128)(2,1)} %copy-done.6, ...), custom_call_target="tpu_custom_call" | custom-call | tf_op jit(solution)/shard_map/qkv_back/pallas_call | solution.py:23
  217.1 4.0 %qkv_grad.1 = (f32[2,16,768]{2,1,0:T(8,128)}, bf16[8,48,576]{2,1,0:T(8,128)(2,1)}, bf16[8,48,576]{2,1,0:T(8,128)(2,1)}) custom-call(s32[3]{0:T(128)} %pad_add_fusion.1.sc.refs_0_, bf16[512,576]{1,0:T(8,128)(2,1)} %get-tuple-element.111.d, bf16[512,768]{1,0:T(8,128)(2,1)} %get-tuple-element.112.dh, bf16[512,768]{1,0:T(8,128)(2,1)} %get-tuple-element.113.h, ...), custom_call_target="tpu_custom_call" | custom-call | tf_op jit(solution)/shard_map/qkv_grad/pallas_call | solution.py:23
  222.0 4.1 %collective-permute-start.21 = (bf16[6,16,768]{2,1,0:T(8,128)(2,1)S(1)}, bf16[6,16,768]{2,1,0:T(8,128)(2,1)S(1)}, u32[]{:S(2)}, u32[]{:S(2)}) collective-permute-start(bf16[6,16,768]{2,1,0:T(8,128)(2,1)S(1)} %pad_maximum_fusion.2), channel_id=1, source_target_pairs={{0,1},{1,0},{2,3},{3,2},{4,5},{5,4},{6,7},{7,6},{8,9},{9,8},{10,11... | collective-permute-start | bytes 442376 | tf_op jit(solution)/shard_map/ppermute | solution.py:548
  226.2 1.1 collective-permute-start.42
  229.1 1.2 collective-permute-start.43
  230.3 3.8 %all-to-all-start.3 = ((bf16[8,64,768]{2,1,0:T(8,128)(2,1)}), bf16[8,64,768]{2,1,0:T(8,128)(2,1)S(1)}, u32[]{:S(2)}, u32[]{:S(2)}) async-start(bf16[8,64,768]{2,1,0:T(8,128)(2,1)} %get-tuple-element.110), calls=%async_computation.3 | async-start | bytes 1572864 | tf_op jit(solution)/shard_map/all_to_all | solution.py:586
  234.2 1.2 collective-permute-start.23
  236.0 10.8 %collective-permute-done.23 = bf16[6,16,768]{2,1,0:T(8,128)(2,1)S(1)} collective-permute-done((bf16[6,16,768]{2,1,0:T(8,128)(2,1)S(1)}, bf16[6,16,768]{2,1,0:T(8,128)(2,1)S(1)}, u32[]{:S(2)}, u32[]{:S(2)}) %collective-permute-start.23) | collective-permute-done | bytes 147488 | tf_op jit(solution)/shard_map/ppermute | solution.py:548
  246.9 9.5 %collective-permute-done.27 = bf16[4,48,576]{2,1,0:T(8,128)(2,1)S(1)} collective-permute-done((bf16[4,48,576]{2,1,0:T(8,128)(2,1)S(1)}, bf16[4,48,576]{2,1,0:T(8,128)(2,1)S(1)}, u32[]{:S(2)}, u32[]{:S(2)}) %collective-permute-start.27) | collective-permute-done | bytes 221216 | tf_op jit(solution)/shard_map/ppermute | solution.py:548
  257.0 2.9 collective-permute-start.29
  260.2 1.1 collective-permute-start.25
  261.4 4.9 %collective-permute-done.30 = bf16[48,576]{1,0:T(8,128)(2,1)S(1)} collective-permute-done((bf16[48,576]{1,0:T(8,128)(2,1)S(1)}, bf16[48,576]{1,0:T(8,128)(2,1)S(1)}, u32[]{:S(2)}, u32[]{:S(2)}) %collective-permute-start.30) | collective-permute-done | bytes 55328 | tf_op jit(solution)/shard_map/ppermute | solution.py:548
  266.2 1.4 collective-permute-done.28
  267.7 1.2 collective-permute-start.31
  269.2 2.5 last.1
  271.7 3.8 %collective-permute-done.25 = bf16[6,16,768]{2,1,0:T(8,128)(2,1)S(1)} collective-permute-done((bf16[6,16,768]{2,1,0:T(8,128)(2,1)S(1)}, bf16[6,16,768]{2,1,0:T(8,128)(2,1)S(1)}, u32[]{:S(2)}, u32[]{:S(2)}) %collective-permute-start.25) | collective-permute-done | bytes 147488 | tf_op jit(solution)/shard_map/ppermute | solution.py:548
  277.3 2.1 fusion.27
  283.0 5.1 %collective-permute-done.34.p2 = bf16[192,768]{1,0:T(8,128)(2,1)} collective-permute-done((bf16[192,768]{1,0:T(8,128)(2,1)}, bf16[192,768]{1,0:T(8,128)(2,1)}, u32[]{:S(2)}, u32[]{:S(2)}) %collective-permute-start.34) | collective-permute-done | bytes 294944 | tf_op jit(solution)/shard_map/ppermute | solution.py:548
  290.4 1.7 reshape.194
  292.7 3.2 %finish.1 = (f32[96,3072]{1,0:T(8,128)}, f32[384,768]{1,0:T(8,128)}, f32[96,768]{1,0:T(8,128)}) custom-call(s32[3]{0:T(128)} %pad_add_fusion.1.sc.refs_0_, bf16[192,768]{1,0:T(8,128)(2,1)} %bitcast.140, bf16[192,768]{1,0:T(8,128)(2,1)} %collective-permute-done.33.p1, bf16[192,768]{1,0:T(8,128)(2,1)} %collective-permute-done.34.p2, ...), custom_call_target="tpu_custom_call" | custom-call | tf_op jit(solution)/shard_map/finish/pallas_call | solution.py:23
  (218 shorter events, 38.7 us)
Async XLA Ops:
  7.2 105.3 %all-gather.3.cloned.1.call-start = ((), (), s32[]{:S(2)}) async-start(), calls=%async_computation.6 | async-start | bytes 4202496 | tf_op jit(solution)/shard_map/all_gather | solution.py:683
  15.7 6.6 %copy-start.4 = (bf16[2,2,32,768]{3,2,1,0:T(8,128)(2,1)S(1)}, bf16[2,2,32,768]{3,2,1,0:T(8,128)(2,1)}, u32[]{:S(2)}) copy-start(bf16[2,2,32,768]{3,2,1,0:T(8,128)(2,1)} %grad.3) | copy-start | bytes 589828
  15.7 9.1 %copy-start.41 = (s32[16]{0:T(128)S(1)}, s32[16]{0:T(128)}, u32[]{:S(2)}) copy-start(s32[16]{0:T(128)} %param.16) | copy-start | bytes 196
  15.7 14.0 %copy-start.40 = (s32[2,2048]{1,0:T(2,128)S(1)}, s32[2,2048]{1,0:T(2,128)}, u32[]{:S(2)}) copy-start(s32[2,2048]{1,0:T(2,128)} %param.17) | copy-start | bytes 49156
  15.7 51.5 %all-to-all-start = ((bf16[8,104,768]{2,1,0:T(8,128)(2,1)}), bf16[8,104,768]{2,1,0:T(8,128)(2,1)S(1)}, u32[]{:S(2)}, u32[]{:S(2)}) async-start(bf16[8,104,768]{2,1,0:T(8,128)(2,1)} %get-tuple-element.67), calls=%async_computation | async-start | bytes 2555904 | tf_op jit(solution)/shard_map/all_to_all | solution.py:586
  22.3 5.6 %collective-permute-start.1 = (bf16[2,2,32,768]{3,2,1,0:T(8,128)(2,1)S(1)}, bf16[2,2,32,768]{3,2,1,0:T(8,128)(2,1)S(1)}, u32[]{:S(2)}, u32[]{:S(2)}) collective-permute-start(bf16[2,2,32,768]{3,2,1,0:T(8,128)(2,1)S(1)} %copy-done.4), channel_id=1, source_target_pairs={{0,2},{1,3},{2,0},{3,1},{4,6},{5,7},{6,4},{7,5},{8,10},{9,11},{10,... | collective-permute-start | bytes 589832 | tf_op jit(solution)/shard_map/ppermute | solution.py:548
  23.5 6.2 %collective-permute-start = (bf16[2,2,32,768]{3,2,1,0:T(8,128)(2,1)S(1)}, bf16[2,2,32,768]{3,2,1,0:T(8,128)(2,1)S(1)}, u32[]{:S(2)}, u32[]{:S(2)}) collective-permute-start(bf16[2,2,32,768]{3,2,1,0:T(8,128)(2,1)S(1)} %copy-done.4), channel_id=1, source_target_pairs={{0,1},{1,0},{2,3},{3,2},{4,5},{5,4},{6,7},{7,6},{8,9},{9,8},{10,11... | collective-permute-start | bytes 589832 | tf_op jit(solution)/shard_map/ppermute | solution.py:548
  27.9 70.6 %copy-start.27 = (bf16[2,2,32,768]{3,2,1,0:T(8,128)(2,1)}, bf16[2,2,32,768]{3,2,1,0:T(8,128)(2,1)S(1)}, u32[]{:S(2)}) copy-start(bf16[2,2,32,768]{3,2,1,0:T(8,128)(2,1)S(1)} %collective-permute-done.1.g2) | copy-start | bytes 589828
  27.9 2.9 collective-permute-start.2
  29.7 68.8 %copy-start.28 = (bf16[2,2,32,768]{3,2,1,0:T(8,128)(2,1)}, bf16[2,2,32,768]{3,2,1,0:T(8,128)(2,1)S(1)}, u32[]{:S(2)}) copy-start(bf16[2,2,32,768]{3,2,1,0:T(8,128)(2,1)S(1)} %collective-permute-done.g1) | copy-start | bytes 589828
  30.8 67.7 %copy-start.29 = (bf16[2,2,32,768]{3,2,1,0:T(8,128)(2,1)}, bf16[2,2,32,768]{3,2,1,0:T(8,128)(2,1)S(1)}, u32[]{:S(2)}) copy-start(bf16[2,2,32,768]{3,2,1,0:T(8,128)(2,1)S(1)} %collective-permute-done.2.g3) | copy-start | bytes 589828
  67.2 11.4 %copy-start.1 = (bf16[8,104,768]{2,1,0:T(8,128)(2,1)}, bf16[8,104,768]{2,1,0:T(8,128)(2,1)S(1)}, u32[]{:S(2)}) copy-start(bf16[8,104,768]{2,1,0:T(8,128)(2,1)S(1)} %all-to-all-done.refs_1_.refs_2_) | copy-start | bytes 3833860
  67.2 11.4 %copy-start.10 = (bf16[8,24,768]{2,1,0:T(8,128)(2,1)}, bf16[8,24,768]{2,1,0:T(8,128)(2,1)S(1)}, u32[]{:S(2)}) copy-start(bf16[8,24,768]{2,1,0:T(8,128)(2,1)S(1)} %slice.24) | copy-start | bytes 884740
  67.2 6.9 %collective-permute-start.4 = (bf16[192,768]{1,0:T(8,128)(2,1)S(1)}, bf16[192,768]{1,0:T(8,128)(2,1)S(1)}, u32[]{:S(2)}, u32[]{:S(2)}) collective-permute-start(bf16[192,768]{1,0:T(8,128)(2,1)S(1)} %bitcast.132), channel_id=1, source_target_pairs={{0,2},{1,3},{2,0},{3,1},{4,6},{5,7},{6,4},{7,5},{8,10},{9,11},{10,... | collective-permute-start | bytes 884744 | tf_op jit(solution)/shard_map/ppermute | solution.py:548
  69.7 8.9 %collective-permute-start.3 = (bf16[192,768]{1,0:T(8,128)(2,1)S(1)}, bf16[192,768]{1,0:T(8,128)(2,1)S(1)}, u32[]{:S(2)}, u32[]{:S(2)}) collective-permute-start(bf16[192,768]{1,0:T(8,128)(2,1)S(1)} %bitcast.133), channel_id=1, source_target_pairs={{0,1},{1,0},{2,3},{3,2},{4,5},{5,4},{6,7},{7,6},{8,9},{9,8},{10,11... | collective-permute-start | bytes 884744 | tf_op jit(solution)/shard_map/ppermute | solution.py:548
  74.1 4.4 %collective-permute-start.5 = (bf16[192,768]{1,0:T(8,128)(2,1)S(1)}, bf16[192,768]{1,0:T(8,128)(2,1)S(1)}, u32[]{:S(2)}, u32[]{:S(2)}) collective-permute-start(bf16[192,768]{1,0:T(8,128)(2,1)S(1)} %collective-permute-done.4.refs_8_), channel_id=1, source_target_pairs={{0,1},{1,0},{2,3},{3,2},{4,5},{5,4},{6,7},{7,6},{8,9},{9,8},{10,11... | collective-permute-start | bytes 884744 | tf_op jit(solution)/shard_map/ppermute | solution.py:548
  84.5 11.1 %collective-permute-start.7 = (bf16[512,384]{1,0:T(8,128)(2,1)}, bf16[512,384]{1,0:T(8,128)(2,1)S(1)}, u32[]{:S(2)}, u32[]{:S(2)}) collective-permute-start(bf16[512,384]{1,0:T(8,128)(2,1)} %get-tuple-element.70.kv0), channel_id=1, source_target_pairs={{0,2},{1,3},{2,0},{3,1},{4,6},{5,7},{6,4},{7,5},{8,10},{9,11},{10,... | collective-permute-start | bytes 1179656 | tf_op jit(solution)/shard_map/ppermute | solution.py:548
  85.6 12.9 %collective-permute-start.6 = (bf16[512,384]{1,0:T(8,128)(2,1)}, bf16[512,384]{1,0:T(8,128)(2,1)S(1)}, u32[]{:S(2)}, u32[]{:S(2)}) collective-permute-start(bf16[512,384]{1,0:T(8,128)(2,1)} %get-tuple-element.70.kv0), channel_id=1, source_target_pairs={{0,1},{1,0},{2,3},{3,2},{4,5},{5,4},{6,7},{7,6},{8,9},{9,8},{10,11... | collective-permute-start | bytes 1179656 | tf_op jit(solution)/shard_map/ppermute | solution.py:548
  95.6 2.9 collective-permute-start.8
  107.8 15.1 %all-to-all-start.1 = ((bf16[8,64,192]{2,1,0:T(8,128)(2,1)}), bf16[8,64,192]{2,1,0:T(8,128)(2,1)S(1)}, u32[]{:S(2)}, u32[]{:S(2)}) async-start(bf16[8,64,192]{2,1,0:T(8,128)(2,1)} %bitcast.142), calls=%async_computation.1 | async-start | bytes 524288 | tf_op jit(solution)/shard_map/all_to_all | solution.py:586
  113.4 5.1 %copy-start.31 = (bf16[16,768]{1,0:T(8,128)(2,1)}, bf16[16,768]{1,0:T(8,128)(2,1)S(1)}, u32[]{:S(2)}) copy-start(bf16[16,768]{1,0:T(8,128)(2,1)S(1)} %slice_reduce_fusion.rest0) | copy-start | bytes 73732
  113.4 3.0 %collective-permute-start.10 = (bf16[16,768]{1,0:T(8,128)(2,1)S(1)}, bf16[16,768]{1,0:T(8,128)(2,1)S(1)}, u32[]{:S(2)}, u32[]{:S(2)}) collective-permute-start(bf16[16,768]{1,0:T(8,128)(2,1)S(1)} %slice_reduce_fusion.rest0), channel_id=1, source_target_pairs={{0,2},{1,3},{2,0},{3,1},{4,6},{5,7},{6,4},{7,5},{8,10},{9,11},{10,... | collective-permute-start | bytes 73736 | tf_op jit(solution)/shard_map/ppermute | solution.py:548
  114.6 3.8 %collective-permute-start.9 = (bf16[16,768]{1,0:T(8,128)(2,1)S(1)}, bf16[16,768]{1,0:T(8,128)(2,1)S(1)}, u32[]{:S(2)}, u32[]{:S(2)}) collective-permute-start(bf16[16,768]{1,0:T(8,128)(2,1)S(1)} %slice_reduce_fusion.rest0), channel_id=1, source_target_pairs={{0,1},{1,0},{2,3},{3,2},{4,5},{5,4},{6,7},{7,6},{8,9},{9,8},{10,11... | collective-permute-start | bytes 73736 | tf_op jit(solution)/shard_map/ppermute | solution.py:548
  116.5 2.0 collective-permute-start.11
  128.0 6.7 %collective-permute-start.13 = (bf16[128,768]{1,0:T(8,128)(2,1)}, bf16[128,768]{1,0:T(8,128)(2,1)S(1)}, u32[]{:S(2)}, u32[]{:S(2)}) collective-permute-start(bf16[128,768]{1,0:T(8,128)(2,1)} %get-tuple-element.76.h0), channel_id=1, source_target_pairs={{0,2},{1,3},{2,0},{3,1},{4,6},{5,7},{6,4},{7,5},{8,10},{9,11},{10,... | collective-permute-start | bytes 589832 | tf_op jit(solution)/shard_map/ppermute | solution.py:548
  129.1 6.4 %collective-permute-start.12 = (bf16[128,768]{1,0:T(8,128)(2,1)}, bf16[128,768]{1,0:T(8,128)(2,1)S(1)}, u32[]{:S(2)}, u32[]{:S(2)}) collective-permute-start(bf16[128,768]{1,0:T(8,128)(2,1)} %get-tuple-element.76.h0), channel_id=1, source_target_pairs={{0,1},{1,0},{2,3},{3,2},{4,5},{5,4},{6,7},{7,6},{8,9},{9,8},{10,11... | collective-permute-start | bytes 589832 | tf_op jit(solution)/shard_map/ppermute | solution.py:548
  134.7 1.9 collective-permute-start.14
  143.7 1.9 collective-permute-start.15
  145.6 7.0 %copy-start.12 = (bf16[2,128,768]{2,1,0:T(8,128)(2,1)}, bf16[2,128,768]{2,1,0:T(8,128)(2,1)S(1)}, u32[]{:S(2)}) copy-start(bf16[2,128,768]{2,1,0:T(8,128)(2,1)S(1)} %collective-permute-done.15.dh_recv) | copy-start | bytes 1179652
  146.8 6.2 %collective-permute-start.16 = (bf16[128,768]{1,0:T(8,128)(2,1)S(1)}, bf16[128,768]{1,0:T(8,128)(2,1)S(1)}, u32[]{:S(2)}, u32[]{:S(2)}) collective-permute-start(bf16[128,768]{1,0:T(8,128)(2,1)S(1)} %fusion.6), channel_id=1, source_target_pairs={{0,2},{1,3},{2,0},{3,1},{4,6},{5,7},{6,4},{7,5},{8,10},{9,11},{10,... | collective-permute-start | bytes 589832 | tf_op jit(solution)/shard_map/ppermute | solution.py:548
  157.4 12.9 %all-to-all-start.2 = ((bf16[8,64,192]{2,1,0:T(8,128)(2,1)}), bf16[8,64,192]{2,1,0:T(8,128)(2,1)S(1)}, u32[]{:S(2)}, u32[]{:S(2)}) async-start(bf16[8,64,192]{2,1,0:T(8,128)(2,1)} %get-tuple-element.89), calls=%async_computation.2 | async-start | bytes 524288 | tf_op jit(solution)/shard_map/all_to_all | solution.py:586
  163.1 116.3 %reduce-scatter.2.cloned.1.call-start = ((), (), s32[]{:S(2)}) async-start(), calls=%async_computation.5 | async-start | bytes 2654208 | tf_op jit(solution)/shard_map/reduce_scatter | solution.py:787
  170.3 17.5 %collective-permute-start.17 = (bf16[2,128,768]{2,1,0:T(8,128)(2,1)}, bf16[2,128,768]{2,1,0:T(8,128)(2,1)S(1)}, u32[]{:S(2)}, u32[]{:S(2)}) collective-permute-start(bf16[2,128,768]{2,1,0:T(8,128)(2,1)} %get-tuple-element.100), channel_id=1, source_target_pairs={{0,1},{1,0},{2,3},{3,2},{4,5},{5,4},{6,7},{7,6},{8,9},{9,8},{10,11... | collective-permute-start | bytes 1179656 | tf_op jit(solution)/shard_map/ppermute | solution.py:548
  173.1 17.6 %collective-permute-start.36 = (bf16[8,48,768]{2,1,0:T(8,128)(2,1)}, bf16[8,48,768]{2,1,0:T(8,128)(2,1)S(1)}, u32[]{:S(2)}, u32[]{:S(2)}) collective-permute-start(bf16[8,48,768]{2,1,0:T(8,128)(2,1)} %get-tuple-element.121), channel_id=1, source_target_pairs={{0,1},{1,0},{2,3},{3,2},{4,5},{5,4},{6,7},{7,6},{8,9},{9,8},{10,11... | collective-permute-start | bytes 1769480 | tf_op jit(solution)/shard_map/ppermute | solution.py:548
  187.1 12.1 %collective-permute-start.19 = (bf16[2,512,384]{2,1,0:T(8,128)(2,1)}, bf16[2,512,384]{2,1,0:T(8,128)(2,1)S(1)}, u32[]{:S(2)}, u32[]{:S(2)}) collective-permute-start(bf16[2,512,384]{2,1,0:T(8,128)(2,1)} %get-tuple-element.107), channel_id=1, source_target_pairs={{0,1},{1,0},{2,3},{3,2},{4,5},{5,4},{6,7},{7,6},{8,9},{9,8},{10,11... | collective-permute-start | bytes 2359304 | tf_op jit(solution)/shard_map/ppermute | solution.py:548
  189.6 6.8 %collective-permute-start.18 = (bf16[128,768]{1,0:T(8,128)(2,1)}, bf16[128,768]{1,0:T(8,128)(2,1)}, u32[]{:S(2)}, u32[]{:S(2)}) collective-permute-start(bf16[128,768]{1,0:T(8,128)(2,1)} %fusion.7), channel_id=1, source_target_pairs={{0,2},{1,3},{2,0},{3,1},{4,6},{5,7},{6,4},{7,5},{8,10},{9,11},{10,... | collective-permute-start | bytes 589832 | tf_op jit(solution)/shard_map/ppermute | solution.py:548
  190.9 11.8 %collective-permute-start.37 = (bf16[8,48,384]{2,1,0:T(8,128)(2,1)S(1)}, bf16[8,48,384]{2,1,0:T(8,128)(2,1)S(1)}, u32[]{:S(2)}, u32[]{:S(2)}) collective-permute-start(bf16[8,48,384]{2,1,0:T(8,128)(2,1)S(1)} %constant_dynamic-slice_fusion), channel_id=1, source_target_pairs={{0,2},{1,3},{2,0},{3,1},{4,6},{5,7},{6,4},{7,5},{8,10},{9,11},{10,... | collective-permute-start | bytes 884744 | tf_op jit(solution)/shard_map/ppermute | solution.py:548
  199.2 4.8 %copy-start.35 = (f32[16,768]{1,0:T(8,128)S(1)}, f32[16,768]{1,0:T(8,128)}, u32[]{:S(2)}) copy-start(f32[16,768]{1,0:T(8,128)} %get-tuple-element.116) | copy-start | bytes 147460
  199.3 12.0 %collective-permute-start.20 = (bf16[512,384]{1,0:T(8,128)(2,1)S(1)}, bf16[512,384]{1,0:T(8,128)(2,1)S(1)}, u32[]{:S(2)}, u32[]{:S(2)}) collective-permute-start(bf16[512,384]{1,0:T(8,128)(2,1)S(1)} %fusion.2), channel_id=1, source_target_pairs={{0,2},{1,3},{2,0},{3,1},{4,6},{5,7},{6,4},{7,5},{8,10},{9,11},{10,... | collective-permute-start | bytes 1179656 | tf_op jit(solution)/shard_map/ppermute | solution.py:548
  202.9 5.7 %collective-permute-start.38 = (bf16[4,48,384]{2,1,0:T(8,128)(2,1)S(1)}, bf16[4,48,384]{2,1,0:T(8,128)(2,1)S(1)}, u32[]{:S(2)}, u32[]{:S(2)}) collective-permute-start(bf16[4,48,384]{2,1,0:T(8,128)(2,1)S(1)} %dynamic-slice_bitcast_fusion.1), channel_id=1, source_target_pairs={{0,4},{4,0},{8,12},{12,8},{16,20},{20,16},{24,28},{28,24},{1,5},{5... | collective-permute-start | bytes 442376 | tf_op jit(solution)/shard_map/ppermute | solution.py:548
  208.6 17.5 %collective-permute-start.39 = (bf16[48,384]{1,0:T(8,128)(2,1)S(1)}, bf16[48,384]{1,0:T(8,128)(2,1)S(1)}, u32[]{:S(2)}, u32[]{:S(2)}) collective-permute-start(bf16[48,384]{1,0:T(8,128)(2,1)S(1)} %get-tuple-element.135), channel_id=1, source_target_pairs={{0,8},{4,12},{8,0},{12,4},{16,24},{20,28},{24,16},{28,20},{1,9},{5... | collective-permute-start | bytes 110600 | tf_op jit(solution)/shard_map/ppermute | solution.py:548
  209.4 16.8 %collective-permute-start.41 = (bf16[48,384]{1,0:T(8,128)(2,1)S(1)}, bf16[48,384]{1,0:T(8,128)(2,1)S(1)}, u32[]{:S(2)}, u32[]{:S(2)}) collective-permute-start(bf16[48,384]{1,0:T(8,128)(2,1)S(1)} %get-tuple-element.136), channel_id=1, source_target_pairs={{0,24},{4,28},{8,16},{12,20},{16,8},{20,12},{24,0},{28,4},{1,25},{... | collective-permute-start | bytes 110600 | tf_op jit(solution)/shard_map/ppermute | solution.py:548
  209.8 16.3 %collective-permute-start.40 = (bf16[48,384]{1,0:T(8,128)(2,1)S(1)}, bf16[48,384]{1,0:T(8,128)(2,1)S(1)}, u32[]{:S(2)}, u32[]{:S(2)}) collective-permute-start(bf16[48,384]{1,0:T(8,128)(2,1)S(1)} %get-tuple-element.137), channel_id=1, source_target_pairs={{0,16},{4,20},{8,24},{12,28},{16,0},{20,4},{24,8},{28,12},{1,17},{... | collective-permute-start | bytes 110600 | tf_op jit(solution)/shard_map/ppermute | solution.py:548
  222.0 5.6 %collective-permute-start.21 = (bf16[6,16,768]{2,1,0:T(8,128)(2,1)S(1)}, bf16[6,16,768]{2,1,0:T(8,128)(2,1)S(1)}, u32[]{:S(2)}, u32[]{:S(2)}) collective-permute-start(bf16[6,16,768]{2,1,0:T(8,128)(2,1)S(1)} %pad_maximum_fusion.2), channel_id=1, source_target_pairs={{0,1},{1,0},{2,3},{3,2},{4,5},{5,4},{6,7},{7,6},{8,9},{9,8},{10,11... | collective-permute-start | bytes 442376 | tf_op jit(solution)/shard_map/ppermute | solution.py:548
  226.2 2.9 collective-permute-start.42
  227.3 8.1 %collective-permute-start.26 = (bf16[8,48,576]{2,1,0:T(8,128)(2,1)}, bf16[8,48,576]{2,1,0:T(8,128)(2,1)S(1)}, u32[]{:S(2)}, u32[]{:S(2)}) collective-permute-start(bf16[8,48,576]{2,1,0:T(8,128)(2,1)} %get-tuple-element.119), channel_id=1, source_target_pairs={{0,1},{1,0},{2,3},{3,2},{4,5},{5,4},{6,7},{7,6},{8,9},{9,8},{10,11... | collective-permute-start | bytes 1327112 | tf_op jit(solution)/shard_map/ppermute | solution.py:548
  227.7 7.7 %copy-start.16 = (bf16[8,48,576]{2,1,0:T(8,128)(2,1)S(1)}, bf16[8,48,576]{2,1,0:T(8,128)(2,1)}, u32[]{:S(2)}) copy-start(bf16[8,48,576]{2,1,0:T(8,128)(2,1)} %get-tuple-element.118) | copy-start | bytes 1327108
  227.7 6.5 %collective-permute-start.22 = (bf16[6,16,768]{2,1,0:T(8,128)(2,1)S(1)}, bf16[6,16,768]{2,1,0:T(8,128)(2,1)S(1)}, u32[]{:S(2)}, u32[]{:S(2)}) collective-permute-start(bf16[6,16,768]{2,1,0:T(8,128)(2,1)S(1)} %add_convert_fusion.9), channel_id=1, source_target_pairs={{0,2},{1,3},{2,0},{3,1},{4,6},{5,7},{6,4},{7,5},{8,10},{9,11},{10,... | collective-permute-start | bytes 442376 | tf_op jit(solution)/shard_map/ppermute | solution.py:548
  229.1 6.4 %copy-start.21 = (bf16[48,768]{1,0:T(8,128)(2,1)}, bf16[48,768]{1,0:T(8,128)(2,1)S(1)}, u32[]{:S(2)}) copy-start(bf16[48,768]{1,0:T(8,128)(2,1)S(1)} %pad_maximum_fusion.3.proj) | copy-start | bytes 221188
  229.1 63.0 %collective-permute-start.43 = (bf16[48,768]{1,0:T(8,128)(2,1)S(1)}, bf16[48,768]{1,0:T(8,128)(2,1)S(1)}, u32[]{:S(2)}, u32[]{:S(2)}) collective-permute-start(bf16[48,768]{1,0:T(8,128)(2,1)S(1)} %pad_maximum_fusion.3.proj), channel_id=1, source_target_pairs={{0,1},{1,0},{2,3},{3,2},{4,5},{5,4},{6,7},{7,6},{8,9},{9,8},{10,11... | collective-permute-start | bytes 221192 | tf_op jit(solution)/shard_map/ppermute | solution.py:548
  230.3 29.9 %all-to-all-start.3 = ((bf16[8,64,768]{2,1,0:T(8,128)(2,1)}), bf16[8,64,768]{2,1,0:T(8,128)(2,1)S(1)}, u32[]{:S(2)}, u32[]{:S(2)}) async-start(bf16[8,64,768]{2,1,0:T(8,128)(2,1)} %get-tuple-element.110), calls=%async_computation.3 | async-start | bytes 1572864 | tf_op jit(solution)/shard_map/all_to_all | solution.py:586
  234.2 12.6 %collective-permute-start.23 = (bf16[6,16,768]{2,1,0:T(8,128)(2,1)S(1)}, bf16[6,16,768]{2,1,0:T(8,128)(2,1)S(1)}, u32[]{:S(2)}, u32[]{:S(2)}) collective-permute-start(bf16[6,16,768]{2,1,0:T(8,128)(2,1)S(1)} %add_convert_fusion.8), channel_id=1, source_target_pairs={{0,4},{4,0},{8,12},{12,8},{16,20},{20,16},{24,28},{28,24},{1,5},{5... | collective-permute-start | bytes 442376 | tf_op jit(solution)/shard_map/ppermute | solution.py:548
  235.6 20.9 %collective-permute-start.27 = (bf16[4,48,576]{2,1,0:T(8,128)(2,1)S(1)}, bf16[4,48,576]{2,1,0:T(8,128)(2,1)S(1)}, u32[]{:S(2)}, u32[]{:S(2)}) collective-permute-start(bf16[4,48,576]{2,1,0:T(8,128)(2,1)S(1)} %dynamic-slice_bitcast_fusion), channel_id=1, source_target_pairs={{0,4},{4,0},{8,12},{12,8},{16,20},{20,16},{24,28},{28,24},{1,5},{5... | collective-permute-start | bytes 663560 | tf_op jit(solution)/shard_map/ppermute | solution.py:548
  246.9 13.3 %collective-permute-start.24 = (bf16[6,16,768]{2,1,0:T(8,128)(2,1)S(1)}, bf16[6,16,768]{2,1,0:T(8,128)(2,1)S(1)}, u32[]{:S(2)}, u32[]{:S(2)}) collective-permute-start(bf16[6,16,768]{2,1,0:T(8,128)(2,1)S(1)} %add_convert_fusion.7), channel_id=1, source_target_pairs={{0,8},{4,12},{8,0},{12,4},{16,24},{20,28},{24,16},{28,20},{1,9},{5... | collective-permute-start | bytes 442376 | tf_op jit(solution)/shard_map/ppermute | solution.py:548
  256.5 9.7 %collective-permute-start.30 = (bf16[48,576]{1,0:T(8,128)(2,1)S(1)}, bf16[48,576]{1,0:T(8,128)(2,1)S(1)}, u32[]{:S(2)}, u32[]{:S(2)}) collective-permute-start(bf16[48,576]{1,0:T(8,128)(2,1)S(1)} %get-tuple-element.132), channel_id=1, source_target_pairs={{0,8},{4,12},{8,0},{12,4},{16,24},{20,28},{24,16},{28,20},{1,9},{5... | collective-permute-start | bytes 165896 | tf_op jit(solution)/shard_map/ppermute | solution.py:548
  257.0 9.2 %collective-permute-start.29 = (bf16[48,576]{1,0:T(8,128)(2,1)S(1)}, bf16[48,576]{1,0:T(8,128)(2,1)S(1)}, u32[]{:S(2)}, u32[]{:S(2)}) collective-permute-start(bf16[48,576]{1,0:T(8,128)(2,1)S(1)} %get-tuple-element.133), channel_id=1, source_target_pairs={{0,16},{4,20},{8,24},{12,28},{16,0},{20,4},{24,8},{28,12},{1,17},{... | collective-permute-start | bytes 165896 | tf_op jit(solution)/shard_map/ppermute | solution.py:548
  260.0 7.6 %collective-permute-start.28 = (bf16[48,576]{1,0:T(8,128)(2,1)S(1)}, bf16[48,576]{1,0:T(8,128)(2,1)S(1)}, u32[]{:S(2)}, u32[]{:S(2)}) collective-permute-start(bf16[48,576]{1,0:T(8,128)(2,1)S(1)} %get-tuple-element.134), channel_id=1, source_target_pairs={{0,24},{4,28},{8,16},{12,20},{16,8},{20,12},{24,0},{28,4},{1,25},{... | collective-permute-start | bytes 165896 | tf_op jit(solution)/shard_map/ppermute | solution.py:548
  260.2 9.0 %copy-start.2 = (bf16[8,64,768]{2,1,0:T(8,128)(2,1)}, bf16[8,64,768]{2,1,0:T(8,128)(2,1)S(1)}, u32[]{:S(2)}) copy-start(bf16[8,64,768]{2,1,0:T(8,128)(2,1)S(1)} %all-to-all-done.3.m_in) | copy-start | bytes 2359300
  260.2 15.2 %collective-permute-start.25 = (bf16[6,16,768]{2,1,0:T(8,128)(2,1)S(1)}, bf16[6,16,768]{2,1,0:T(8,128)(2,1)S(1)}, u32[]{:S(2)}, u32[]{:S(2)}) collective-permute-start(bf16[6,16,768]{2,1,0:T(8,128)(2,1)S(1)} %convert_add_fusion.3), channel_id=1, source_target_pairs={{0,16},{4,20},{8,24},{12,28},{16,0},{20,4},{24,8},{28,12},{1,17},{... | collective-permute-start | bytes 442376 | tf_op jit(solution)/shard_map/ppermute | solution.py:548
  267.7 7.8 %collective-permute-start.31 = (bf16[4,48,576]{2,1,0:T(8,128)(2,1)S(1)}, bf16[4,48,576]{2,1,0:T(8,128)(2,1)S(1)}, u32[]{:S(2)}, u32[]{:S(2)}) collective-permute-start(bf16[4,48,576]{2,1,0:T(8,128)(2,1)S(1)} %pad_maximum_fusion.1), channel_id=1, source_target_pairs={{0,2},{1,3},{2,0},{3,1},{4,6},{5,7},{6,4},{7,5},{8,10},{9,11},{10,... | collective-permute-start | bytes 663560 | tf_op jit(solution)/shard_map/ppermute | solution.py:548
  276.2 5.0 %collective-permute-start.32 = (bf16[4,48,576]{2,1,0:T(8,128)(2,1)S(1)}, bf16[4,48,576]{2,1,0:T(8,128)(2,1)S(1)}, u32[]{:S(2)}, u32[]{:S(2)}) collective-permute-start(bf16[4,48,576]{2,1,0:T(8,128)(2,1)S(1)} %copy.85), channel_id=1, source_target_pairs={{0,1},{1,0},{2,3},{3,2},{4,5},{5,4},{6,7},{7,6},{8,9},{9,8},{10,11... | collective-permute-start | bytes 663560 | tf_op jit(solution)/shard_map/ppermute | solution.py:548
  279.4 8.7 %collective-permute-start.34 = (bf16[192,768]{1,0:T(8,128)(2,1)}, bf16[192,768]{1,0:T(8,128)(2,1)}, u32[]{:S(2)}, u32[]{:S(2)}) collective-permute-start(bf16[192,768]{1,0:T(8,128)(2,1)} %bitcast.139), channel_id=1, source_target_pairs={{0,2},{1,3},{2,0},{3,1},{4,6},{5,7},{6,4},{7,5},{8,10},{9,11},{10,... | collective-permute-start | bytes 884744 | tf_op jit(solution)/shard_map/ppermute | solution.py:548
  282.5 9.6 %collective-permute-start.33 = (bf16[192,768]{1,0:T(8,128)(2,1)S(1)}, bf16[192,768]{1,0:T(8,128)(2,1)}, u32[]{:S(2)}, u32[]{:S(2)}) collective-permute-start(bf16[192,768]{1,0:T(8,128)(2,1)S(1)} %bitcast.141), channel_id=1, source_target_pairs={{0,1},{1,0},{2,3},{3,2},{4,5},{5,4},{6,7},{7,6},{8,9},{9,8},{10,11... | collective-permute-start | bytes 884744 | tf_op jit(solution)/shard_map/ppermute | solution.py:548
  288.1 4.0 %collective-permute-start.35 = (bf16[192,768]{1,0:T(8,128)(2,1)}, bf16[192,768]{1,0:T(8,128)(2,1)}, u32[]{:S(2)}, u32[]{:S(2)}) collective-permute-start(bf16[192,768]{1,0:T(8,128)(2,1)} %collective-permute-done.34.p2), channel_id=1, source_target_pairs={{0,1},{1,0},{2,3},{3,2},{4,5},{5,4},{6,7},{7,6},{8,9},{9,8},{10,11... | collective-permute-start | bytes 884744 | tf_op jit(solution)/shard_map/ppermute | solution.py:548
  (28 other events, 43.2 us)
Sparse Core Ops, SparseCore 0:
  15.8 87.9 all-gather.2
  187.9 78.9 reduce-scatter.1
where the time goes:
time: 306 us; the launch traced here: 303 us
  waiting for transfers between devices  113 us (37%)
  Pallas kernels  74 us (24%)
  starting transfers between devices  68.7 us (22%)
  local copies, waits for them, and re-layouts  20.3 us (7%)
  between operations  14.7 us (5%)
  other arithmetic  8.5 us (3%)
  matrix products  3.94 us (1%)
    pallas_call x15, Pallas kernels, call(): pl.pallas_call(kernel, out_shape=[jax.ShapeDtypeStruct(shape, kind) for s...  74 us
    ppermute x44, waiting for transfers between devices, swap(): return lax.ppermute(x, axis, [(i, i ^ k) for i in range(size)])  73.2 us
    ppermute x44, starting transfers between devices, swap(): return lax.ppermute(x, axis, [(i, i ^ k) for i in range(size)])  47.7 us
    all_to_all x4, waiting for transfers between devices, all_to_all(): lax.all_to_all(x, 'cp', split_axis=0, concat_axis=0, tiled=True, axis_ind...  39.4 us
    all_to_all x4, starting transfers between devices, all_to_all(): lax.all_to_all(x, 'cp', split_axis=0, concat_axis=0, tiled=True, axis_ind...  20.7 us
    unnamed x84, local copies, waits for them, and re-layouts  9.05 us
  transfers between devices with their start and end apart: 50, of which 21 were waited for; matrix products, arithmetic and copies ran while one was open for 6% of the time, Pallas kernels for 18%

commit v1 on v0

--- a/solution.py
+++ b/solution.py
@@ -95,7 +95,7 @@
 
 
 def pack_kernel(
-    mod_rows, seqs, sc, tok, cond, w_ada, bias, wq, w_up, w_down, w_proj, send, shard
+    mod_rows, seqs, sc, tok, cond, w_ada, bias, wq, w_up, w_down, send, shard
 ):
     width = tok.shape[-1]
     s = sc[1]
@@ -113,7 +113,8 @@
         send[i, span : span + 2 * blocks, :] = jnp.concatenate(
             [mine[:, :width], mine[:, width:]], axis=0
         ).astype(BF)
-        send[i, span + 2 * blocks :, :] = jnp.concatenate(
+        send[i, span + 2 * blocks : span + 2 * blocks + mod_rows, :] = rest
+        send[i, span + 2 * blocks + mod_rows :, :] = jnp.concatenate(
             [
                 wq[:, t * width + hg * GROUP : t * width + (hg + 1) * GROUP]
                 for t in (0, 1, 2, 2)
@@ -124,8 +125,6 @@
     n_c = w_up.shape[1] // (4 * inner)
     rows = w_up.shape[0]
     shard[rows : rows + inner, :] = w_down[pl.ds(pl.multiple_of(inner * s, 8), inner), :]
-    shard[rows + inner : 2 * rows + inner, :] = w_proj[...]
-    shard[2 * rows + inner :, :] = rest
     for own in range(4):
 
         @pl.when(s == own)
@@ -273,9 +272,14 @@
 def project_kernel(n_w, sc, attn, tok, mods, weights, y_out, x_out, n_out, inv_out, h_out, w_out):
     width = tok.shape[-1]
     r = sc[0]
-    rows = width // n_w
-    for k in range(n_w):
-        w_out[rows * k : rows * (k + 1), :] = weights[k, 2 * rows : 3 * rows, :]
+    if n_w == 1:
+        w_out[...] = weights[0, 0]
+    else:
+        half = weights.shape[2]
+        for k in range(n_w):
+            for c in range(2):
+                at = pl.multiple_of(2 * half * k + half * ((sc[1] & 1) ^ c), 16)
+                w_out[pl.ds(at, half), :] = weights[c, k]
     full = jnp.concatenate(
         [
             jnp.concatenate([attn[2 * hg + seq] for hg in range(4)], axis=1)
@@ -497,8 +501,9 @@
     for b in range(seqs):
         s_out[0, b * blocks : (b + 1) * blocks, :] = jnp.where(seq == b, shift_sum, 0.0)
         s_out[1, b * blocks : (b + 1) * blocks, :] = jnp.where(seq == b, scale_sum, 0.0)
-    g_scr[...] = dot_tn(h[...], d[...]).astype(BF)
-    if fast:
+    g_scr[:, : d.shape[1]] = dot_tn(h[...], d[...]).astype(BF)
+    if fast:
+        g_scr[:, d.shape[1] :] = jnp.zeros((g_scr.shape[0], g_scr.shape[1] - d.shape[1]), BF)
         c = sc[1] & 1
         half = g_keep.shape[1]
         for i in range(8):
@@ -523,14 +528,11 @@
             out[slot, seq] = o[slot * rows : (slot + 1) * rows]
 
 
-def finish_kernel(sc, p0, p1, p2, p3, proj, proj_other, up, down, outw):
+def finish_kernel(sc, p0, p1, p2, p3, up, down):
     s = sc[1]
     rows = p0.shape[0] // 2
     width = p0.shape[1]
     parts = [p0, p1, p2, p3]
-    half = proj.shape[0]
-    outw[pl.ds(pl.multiple_of(half * (s & 1), 8), half), :] = proj[...].astype(F32)
-    outw[pl.ds(pl.multiple_of(half * (1 - (s & 1)), 8), half), :] = proj_other[...].astype(F32)
     for m in range(4):
         down[pl.ds(pl.multiple_of(rows * (s ^ m), 8), rows), :] = parts[m][rows : 2 * rows, :].astype(F32)
     ups = [p[:rows, :].astype(F32) for p in parts]
@@ -541,6 +543,31 @@
     for c in range(n_c):
         up[:, 4 * quarter * c : 4 * quarter * (c + 1)] = jnp.concatenate(
             [u[:, quarter * c : quarter * (c + 1)] for u in ups], axis=1
+        )
+
+
+def finish_qkv_kernel(sc, own, other, out, proj):
+    s = sc[1]
+    hg = sc[0] // 2
+    half = own.shape[2]
+    for c, part in enumerate((own, other)):
+        where = pl.ds(pl.multiple_of(half * ((s & 1) ^ c), 8), half)
+        swapped = (s & 2) != 0
+        low = [jnp.where(swapped, part[1, m].astype(F32), part[0, m].astype(F32)) for m in range(4)]
+        high = [jnp.where(swapped, part[0, m].astype(F32), part[1, m].astype(F32)) for m in range(4)]
+        low_out, high_out = part[0, 4].astype(F32), part[1, 4].astype(F32)
+        proj[where, :] = jnp.concatenate(
+            [jnp.where(swapped, high_out, low_out), jnp.where(swapped, low_out, high_out)], axis=1
+        )
+        for bit in (1, 2):
+            flip = (hg & bit) != 0
+            low = [jnp.where(flip, low[i ^ bit], low[i]) for i in range(4)]
+            high = [jnp.where(flip, high[i ^ bit], high[i]) for i in range(4)]
+        out[where, :] = jnp.concatenate(
+            [x[:, :GROUP] for x in low]
+            + [x[:, GROUP : 2 * GROUP] for x in low]
+            + [x[:, :GROUP] for x in high],
+            axis=1,
         )
 
 
@@ -641,7 +668,7 @@
     if fast:
         quarter_rows = part_rows // 4
         wq = lax.dynamic_slice(w_qkv, (quarter_rows * s, 0), (quarter_rows, 3 * width))
-        extra = 2 * blocks + quarter_rows
+        extra = 2 * blocks + mod_rows + quarter_rows
     else:
         wq = w_qkv
         extra = 0
@@ -649,8 +676,8 @@
     if fast:
         send, shard = call(
             functools.partial(pack_kernel, mod_rows, seqs),
-            [((8, span + extra, width), BF), ((2 * part_rows + inner + mod_rows, width), BF)],
-            [sc, tokens, cond, w_ada, bias, wq, w_up, w_down, w_out],
+            [((8, span + extra, width), BF), ((part_rows + inner, width), BF)],
+            [sc, tokens, cond, w_ada, bias, wq, w_up, w_down],
             name="pack",
         )
     else:
@@ -661,12 +688,16 @@
             w_up.reshape(part_rows, cp, 4, inner), s, 2, keepdims=False
         ).reshape(part_rows, cp * inner)
         down_part = lax.dynamic_slice_in_dim(w_down, inner * s, inner, 0)
-        shard = jnp.concatenate([up_part, down_part, w_out], axis=0)
+        shard = jnp.concatenate([up_part, down_part], axis=0)
     grad_parts = gather_sp(out_grad)
     got = after(all_to_all(send), *grad_parts)
     if fast:
         w_own = got[:, span + extra - quarter_rows :, :].reshape(8 * quarter_rows, width)
-        w_list = gather_sp(w_own)
+        rest = got[:, span + 2 * blocks : span + 2 * blocks + mod_rows, :].astype(F32)
+        w_list = gather_sp(
+            jnp.concatenate([w_own, jnp.sum(rest, axis=0).astype(BF)], axis=0)
+        )
+        rests = [w[8 * quarter_rows :] for w in w_list]
         mod_one = got
     else:
         full_mod = lax.psum(
@@ -680,15 +711,17 @@
         ]
 
     n_w = 8 if fast else 1
-    weights = lax.all_gather(shard, "cp", axis=0, tiled=False)
-    rests = None
-    if fast:
-        rest = jnp.sum(weights[:, -mod_rows:, :].astype(F32), axis=0).astype(BF)
-    if not fast:
+    weights = lax.all_gather(after(shard, got) if fast else shard, "cp", axis=0, tiled=False)
+    if fast:
+        half = part_rows // 2
+        w_own = lax.dynamic_slice_in_dim(w_out, half * (s % 2), half, 0)
+        w_proj = all_to_all(jnp.broadcast_to(after(w_own, got)[None], (8, half, width)))
+    else:
+        w_proj = lax.all_gather(w_out, "cp", axis=0, tiled=True)[None, None]
         weights = jnp.concatenate(
             [
                 weights[:, at : at + part_rows].reshape(width, width)
-                for at in (0, part_rows, 2 * part_rows)
+                for at in (0, part_rows)
             ],
             axis=0,
         )[None]
@@ -714,6 +747,9 @@
             axis_index_groups=[[8 * g + i for g in range(groups)] for i in range(8)],
         )
     kvs = gather_sp(kv)
+    if fast:
+        kvs[0] = after(kvs[0], w_proj)
+        w_proj = jnp.stack([w_proj, swap(w_proj, "sp", 1, 4)])
     key_col = key_ids[:, :, None]
     query_row = query_ids[None, :]
     part = kv.shape[0]
@@ -733,9 +769,7 @@
         else [((4 * part, count), F32)],
         name="attend",
     )
-    if fast:
-        rests = gather_sp(after(rest, attn))
-    else:
+    if not fast:
         tail = full_mod.astype(BF)
         rests = [
             lax.dynamic_slice_in_dim(tail, (2 + (s ^ m)) * width, width, 1) for m in range(4)
@@ -758,7 +792,7 @@
             ((2 * span, width), BF),
             ((width, width), BF),
         ],
-        [sc, attn_tok, tokens, mods, weights],
+        [sc, attn_tok, tokens, mods, w_proj],
         name="project",
     )
     hs = gather_sp(h_two)
@@ -771,16 +805,49 @@
         scratch=[((width, width), BF)] * 2,
         name="feed",
     )
-    def reduce_sp(keep, send):
+    def reduce_sp(keep, send, *wait):
         near = swap(send, "sp", 1, 4)
+        if wait:
+            near = after(near, *wait)
         both = (keep[1].astype(F32) + near[1].astype(F32)).astype(BF)
         return (keep, near, swap(both, "sp", 2, 4)), both
 
     dh_parts, dh_both = reduce_sp(dh_keep, dh_send)
+    token_row = token_ids[None, :]
+    g_out = ((8, part_rows // 2, width), BF) if fast else ((1, width, width), BF)
+    wide = ((2 * span, width), F32)
+    dx_mid, dh_two, dy, d_attn = call(
+        middle_kernel,
+        [wide, wide, ((2 * span, width), BF), ((8, span, GROUP), BF)],
+        [sc] + list(dh_parts)
+        + [mods, n_two, inv_two, out_grad, w_out_full],
+        name="middle",
+    )
+    half_width = width // 2
+    far = s // 2
+
+    def split_far(mine, theirs):
+        part = (mine.astype(F32) + theirs.astype(F32)).astype(BF)
+        return (
+            lax.dynamic_slice_in_dim(part, half_width * far, half_width, 2),
+            lax.dynamic_slice_in_dim(part, half_width * (1 - far), half_width, 2),
+        )
+
+    def split_y(mine, theirs):
+        part = (mine.astype(F32) + theirs.astype(F32)).astype(BF)
+        part = part.reshape((4, 2) + part.shape[1:])
+        return (
+            lax.dynamic_index_in_dim(part, seq, 1, keepdims=False),
+            lax.dynamic_index_in_dim(part, 1 - seq, 1, keepdims=False),
+        )
+
+    d_heads = all_to_all(d_attn).reshape(count, GROUP)
+    if fast:
+        pass
     (g_feed,) = call(
         functools.partial(feed_grad_kernel, n_w),
         [((n_w, 2 * width // n_w, width), BF)],
-        [sc, h_all, dz, after(act, dh_both), du],
+        [sc, h_all, dz, after(act, d_heads), du],
         name="feed_grad",
     )
     if fast:
@@ -796,34 +863,8 @@
             axis=0,
         )
 
-    token_row = token_ids[None, :]
-    g_out = ((8, part_rows // 2, width), BF) if fast else ((1, width, width), BF)
-    wide = ((2 * span, width), F32)
-    dx_mid, dh_two, dy, d_attn = call(
-        middle_kernel,
-        [wide, wide, ((2 * span, width), BF), ((8, span, GROUP), BF)],
-        [sc] + list(dh_parts)
-        + [mods, n_two, after(inv_two, g_feed), out_grad, w_out_full],
-        name="middle",
-    )
-    s_mid, o_keep, o_send = call(
-        functools.partial(middle_grad_kernel, n_w, mod_rows),
-        [((3, mod_rows, width), F32), g_out, g_out],
-        [sc, dx_mid, dh_two, dy, n_two, y, attn_tok, token_row],
-        scratch=[((width, width), BF)],
-        name="middle_grad",
-    )
-    d_heads = all_to_all(d_attn).reshape(count, GROUP)
-    if fast:
-        o_near = swap(after(o_send, d_heads), "sp", 1, 4)
-        d_heads = after(d_heads, s_mid, o_send, o_keep)
-    z_parts, _ = reduce_sp(after(z_keep, d_heads), after(z_send, d_heads))
-    block_out, s_gate = call(
-        functools.partial(block_kernel, mod_rows),
-        [(tokens.shape, BF), ((mod_rows, width), F32)],
-        [sc] + list(z_parts) + [mods, x_mid, out_grad, token_row],
-        name="block",
-    )
+    if fast:
+        d_heads = after(d_heads, g_feed)
     dkv = ((2, part, 2 * GROUP), BF)
     dq, kv_keep, kv_send = call(
         attend_back_small_kernel if fast else attend_back_large_kernel,
@@ -834,6 +875,15 @@
         else [((HD, count), F32)],
         name="attend_back",
     )
+    s_mid, o_keep, o_send = call(
+        functools.partial(middle_grad_kernel, n_w, mod_rows),
+        [((3, mod_rows, width), F32), g_out, g_out],
+        [sc, dx_mid, dh_two, dy, n_two, after(y, dq), attn_tok, token_row],
+        scratch=[((width, width), BF)],
+        name="middle_grad",
+    )
+    if fast:
+        o_near = swap(o_send, "sp", 1, 4)
     dkv_list, _ = reduce_sp(kv_keep, kv_send)
     if not fast:
         summed = sum(x.astype(F32) for x in (dkv_list[0][0], dkv_list[1][0], dkv_list[2]))
@@ -842,7 +892,7 @@
             axis_index_groups=[[8 * g + i for g in range(groups)] for i in range(8)],
         ).astype(BF)
         dkv_list = [summed[None], summed[None], summed]
-    g_shape = ((8, part_rows // 2, 3 * GROUP), BF) if fast else ((1, width, 3 * GROUP), BF)
+    g_shape = ((8, part_rows // 2, width), BF) if fast else ((1, width, 3 * GROUP), BF)
     m_one, dh_one, dqkv = call(
         functools.partial(qkv_back_kernel, blocks, fast),
         [((8, span, width), BF), ((count, width), BF), ((count, 3 * GROUP), BF)],
@@ -850,22 +900,33 @@
         name="qkv_back",
     )
     m_tok = all_to_all(m_one)
+    z_parts, _ = reduce_sp(z_keep, after(z_send, dh_both), m_one)
+    block_out, s_gate = call(
+        functools.partial(block_kernel, mod_rows),
+        [(tokens.shape, BF), ((mod_rows, width), F32)],
+        [sc] + list(z_parts) + [mods, after(x_mid, m_one), out_grad, token_row],
+        name="block",
+    )
     s_one, q_keep, q_send = call(
         functools.partial(qkv_grad_kernel, blocks, seqs, fast),
         [((2, mod_rows, width), F32), g_shape, g_shape],
         [sc, dqkv, dh_one, h_one, n_one, query_row],
-        scratch=[((width, 3 * GROUP), BF)],
+        scratch=[((width, width if fast else 3 * GROUP), BF)],
         name="qkv_grad",
     )
+    shares = gather_sp(feed.reshape(2 * part_rows, width)) if fast else []
     (grad_in,) = call(
-        last_kernel, [(tokens.shape, F32)], [sc, m_tok, tokens, dx_mid], name="last"
+        last_kernel,
+        [(tokens.shape, F32)],
+        [sc, m_tok, tokens, dx_mid],
+        name="last",
     )
 
     def reduce_all(x, wait=None):
         if not fast:
             return lax.psum(x, ("cp", "sp"))
         for axis, k, size in (("sp", 1, 4), ("sp", 2, 4), ("cp", 1, 8), ("cp", 2, 8), ("cp", 4, 8)):
-            if k == 4:
+            if axis == "cp" and k == 2:
                 x = after(x, wait)
             low = x.astype(BF)
             x = low.astype(F32) + swap(low, axis, k, size).astype(F32)
@@ -881,53 +942,28 @@
     )
 
     if fast:
-        half_width = width // 2
-        o_sum = (o_keep.astype(F32) + after(o_near, dq).astype(F32)).astype(BF)
-        far = s // 2
-        mine = lax.dynamic_slice_in_dim(o_sum, half_width * far, half_width, 2)
-        theirs = lax.dynamic_slice_in_dim(o_sum, half_width * (1 - far), half_width, 2)
-        o_sum = (mine.astype(F32) + swap(theirs, "sp", 2, 4).astype(F32)).astype(BF)
-        o_sum = o_sum.reshape(4, 2, part_rows // 2, half_width)
-        mine = lax.dynamic_index_in_dim(o_sum, seq, 1, keepdims=False)
-        theirs = lax.dynamic_index_in_dim(o_sum, 1 - seq, 1, keepdims=False)
-        o_sum = (mine.astype(F32) + swap(theirs, "cp", 1, 8).astype(F32)).astype(BF)
-        proj = sum(
-            (
-                swap(lax.dynamic_index_in_dim(o_sum, hg ^ m, 0, keepdims=False), "cp", 2 * m, 8)
-                if m
-                else lax.dynamic_index_in_dim(o_sum, hg, 0, keepdims=False)
-            ).astype(F32)
-            for m in range(4)
-        ).astype(BF)
-        other = swap(proj, "sp", 2, 4)
-        proj = jnp.concatenate(
-            [jnp.where(far == 0, proj, other), jnp.where(far == 0, other, proj)], axis=1
-        )
-        proj_other = swap(proj, "sp", 1, 4)
-        near = swap(q_send, "sp", 1, 4)
-        sums = (q_keep.astype(F32) + near.astype(F32)).astype(BF).reshape(
-            4, 2, part_rows // 2, 3 * GROUP
-        )
-        ours = lax.dynamic_index_in_dim(sums, seq, 1, keepdims=False)
-        theirs = lax.dynamic_index_in_dim(sums, 1 - seq, 1, keepdims=False)
-        ours = (ours.astype(F32) + swap(theirs, "cp", 1, 8).astype(F32)).astype(BF)
-        found = [
-            swap(lax.dynamic_index_in_dim(ours, hg ^ m, 0, keepdims=False), "cp", 2 * m, 8)
-            if m
-            else lax.dynamic_index_in_dim(ours, hg, 0, keepdims=False)
+        o_mine, o_theirs = split_y(o_keep, after(o_near, dq))
+        o_mine, o_theirs = split_far(o_mine, after(swap(o_theirs, "cp", 1, 8), m_one))
+        mine, theirs = split_far(q_keep, swap(q_send, "sp", 1, 4))
+        got_far = swap(jnp.concatenate([theirs, o_theirs], axis=0), "sp", 2, 4)
+        mine, theirs = split_y(mine, after(got_far, feed)[:8])
+        mine = (mine.astype(F32) + swap(theirs, "cp", 1, 8).astype(F32)).astype(BF)
+        o_mine = (o_mine.astype(F32) + got_far[8:].astype(F32)).astype(BF)
+        pick = [
+            jnp.stack([lax.dynamic_index_in_dim(x, hg ^ m, 0, keepdims=False) for x in (mine, o_mine)])
             for m in range(4)
         ]
-        for bit in (1, 2):
-            found = [jnp.where((hg & bit) != 0, found[i ^ bit], found[i]) for i in range(4)]
-        mine = after(jnp.stack(found), m_tok)
-        mine = (mine.astype(F32) + swap(mine, "sp", 2, 4).astype(F32)).astype(BF)
-        other = swap(mine, "sp", 1, 4)
-        low = jnp.where(s % 2 == 0, mine, other)
-        high = jnp.where(s % 2 == 0, other, mine)
-        both = jnp.concatenate([low, high], axis=1)
-        grad_qkv = (
-            both.reshape(4, part_rows, 3, GROUP).transpose(1, 2, 0, 3).reshape(part_rows, 3 * width)
-        ).astype(F32)
+        parts = [pick[0]] + [swap(pick[m], "cp", 2 * m, 8) for m in (1, 2, 3)]
+        proj = sum(p[1].astype(F32) for p in parts).astype(BF)
+        found = after(jnp.stack([p[0] for p in parts] + [proj]), m_tok)
+        found = jnp.stack([found, swap(found, "sp", 2, 4)])
+        found = [found, swap(found, "sp", 1, 4)]
+        grad_qkv, grad_out = call(
+            finish_qkv_kernel,
+            [((part_rows, 3 * width), F32), ((part_rows, width), F32)],
+            [sc] + found,
+            name="finish_qkv",
+        )
     else:
         proj = lax.psum_scatter(o_keep[0].astype(F32), "cp", scatter_dimension=0, tiled=True)
         proj_low = lax.psum(proj, "sp")
@@ -941,15 +977,13 @@
             whole.reshape(4, part_rows, 3, GROUP).transpose(1, 2, 0, 3).reshape(part_rows, 3 * width)
         )
     if fast:
-        shares = gather_sp(feed.reshape(2 * part_rows, width))
-        grad_up, grad_down, grad_out = call(
+        grad_up, grad_down = call(
             finish_kernel,
             [
                 ((part_rows, hidden), F32),
                 ((hidden // cp, width), F32),
-                ((part_rows, width), F32),
             ],
-            [sc] + shares + [proj, proj_other],
+            [sc] + shares,
             name="finish",
         )
     else:

time: 306 us -> 284 us (0.928)
  waiting for transfers between devices: 113 us -> 79.6 us
  blocking collectives: 0 us -> 12 us
    ppermute x44 -> x37, waiting for transfers between devices: 73.2 us -> 49.8 us  [swap(): return lax.ppermute(x, axis, [(i, i ^ k) for i in range(size)])]
    all_to_all x0 -> x1, blocking collectives: none -> 12 us  [all_to_all(): lax.all_to_all(x, 'cp', split_axis=0, concat_axis=0, tiled=True, axis_ind...]
    all_to_all x4, waiting for transfers between devices: 39.4 us -> 29.7 us  [all_to_all(): lax.all_to_all(x, 'cp', split_axis=0, concat_axis=0, tiled=True, axis_ind...]
    slice x0 -> x3, local copies, waits for them, and re-layouts: none -> 4.02 us  [body(): rests = [w[8 * quarter_rows:] for w in w_list]]
    pallas_call x15 -> x16, Pallas kernels: 74 us -> 75.2 us  [call(): pl.pallas_call(kernel, out_shape=[jax.ShapeDtypeStruct(shape, kind) for s...]
    unnamed x84 -> x83, local copies, waits for them, and re-layouts: 9.05 us -> 8.04 us
    ppermute x44 -> x37, starting transfers between devices: 47.7 us -> 48.1 us  [swap(): return lax.ppermute(x, axis, [(i, i ^ k) for i in range(size)])]
  transfers between devices with their start and end apart: 50 -> 43, of which waited for: 21 -> 17; matrix products, arithmetic and copies ran while one was open for 6% -> 7% of each run, Pallas kernels for 18% -> 19%
where the time goes in v1:
time: 284 us; the launch traced here: 283 us
  waiting for transfers between devices  79.6 us (28%)
  Pallas kernels  75.2 us (26%)
  starting transfers between devices  67 us (24%)
  local copies, waits for them, and re-layouts  20.5 us (7%)
  between operations  14.7 us (5%)
  blocking collectives  12 us (4%)
  other arithmetic  9.84 us (3%)
  matrix products  3.93 us (1%)
    pallas_call x16, Pallas kernels, call(): pl.pallas_call(kernel, out_shape=[jax.ShapeDtypeStruct(shape, kind) for s...  75.2 us
    ppermute x37, waiting for transfers between devices, swap(): return lax.ppermute(x, axis, [(i, i ^ k) for i in range(size)])  49.8 us
    ppermute x37, starting transfers between devices, swap(): return lax.ppermute(x, axis, [(i, i ^ k) for i in range(size)])  48.1 us
    all_to_all x4, waiting for transfers between devices, all_to_all(): lax.all_to_all(x, 'cp', split_axis=0, concat_axis=0, tiled=True, axis_ind...  29.7 us
    all_to_all x4, starting transfers between devices, all_to_all(): lax.all_to_all(x, 'cp', split_axis=0, concat_axis=0, tiled=True, axis_ind...  18.6 us
    all_to_all x1, blocking collectives, all_to_all(): lax.all_to_all(x, 'cp', split_axis=0, concat_axis=0, tiled=True, axis_ind...  12 us
    unnamed x83, local copies, waits for them, and re-layouts  8.04 us
  transfers between devices with their start and end apart: 43, of which 17 were waited for; matrix products, arithmetic and copies ran while one was open for 7% of the time, Pallas kernels for 19%

profile of v1, /device:TPU:1, one launch (start us, length us, event | category | flops | bytes accessed | tf_op | source)
XLA Modules:
  0.0 282.7 jit_solution(12540596249954694931)
XLA Ops:
  10.0 1.6 multiply_convert_fusion.cond
  12.4 3.2 %pack.1 = (bf16[8,120,768]{2,1,0:T(8,128)(2,1)}, bf16[192,768]{1,0:T(8,128)(2,1)}) custom-call(s32[3]{0:T(128)} %pad_add_fusion.1.sc.refs_0_, bf16[2,2,32,768]{3,2,1,0:T(8,128)(2,1)} %tok.5, bf16[16,96]{1,0:T(8,128)(2,1)} %multiply_convert_fusion.cond, bf16[96,4608]{1,0:T(8,128)(2,1)} %w_ada.1, f32[1,4608]{1,0:T(1,128)} %copy-done.34, ...), custom_call_target="tpu_custom_call" | custom-call | tf_op jit(solution)/shard_map/pack/pallas_call | solution.py:23
  15.6 6.6 %all-to-all-start = ((bf16[8,120,768]{2,1,0:T(8,128)(2,1)}), bf16[8,120,768]{2,1,0:T(8,128)(2,1)S(1)}, u32[]{:S(2)}, u32[]{:S(2)}) async-start(bf16[8,120,768]{2,1,0:T(8,128)(2,1)} %get-tuple-element.72), calls=%async_computation | async-start | bytes 2949120 | tf_op jit(solution)/shard_map/all_to_all | solution.py:613
  22.3 1.2 collective-permute-start.1
  23.5 1.3 collective-permute-start
  24.8 3.1 %collective-permute-done.1.g2 = bf16[2,2,32,768]{3,2,1,0:T(8,128)(2,1)S(1)} collective-permute-done((bf16[2,2,32,768]{3,2,1,0:T(8,128)(2,1)S(1)}, bf16[2,2,32,768]{3,2,1,0:T(8,128)(2,1)S(1)}, u32[]{:S(2)}, u32[]{:S(2)}) %collective-permute-start.1) | collective-permute-done | bytes 196640 | tf_op jit(solution)/shard_map/ppermute | solution.py:575
  27.8 1.8 collective-permute-start.2
  30.8 25.4 %all-to-all-done.refs_1_.refs_2_ = bf16[8,120,768]{2,1,0:T(8,128)(2,1)S(1)} async-done(((bf16[8,120,768]{2,1,0:T(8,128)(2,1)}), bf16[8,120,768]{2,1,0:T(8,128)(2,1)S(1)}, u32[]{:S(2)}, u32[]{:S(2)}) %all-to-all-start) | async-done | bytes 1474592 | tf_op jit(solution)/shard_map/all_to_all | solution.py:613
  56.7 1.1 collective-permute-start.4
  58.7 4.7 %all-to-all-start.1 = ((bf16[8,48,768]{2,1,0:T(8,128)(2,1)}), bf16[8,48,768]{2,1,0:T(8,128)(2,1)S(1)}, u32[]{:S(2)}, u32[]{:S(2)}) async-start(bf16[8,48,768]{2,1,0:T(8,128)(2,1)} %broadcast_in_dim.56), calls=%async_computation.1 | async-start | bytes 1179648 | tf_op jit(solution)/shard_map/all_to_all | solution.py:613
  66.7 1.8 fusion.5
  69.4 5.3 %qkv.1 = (bf16[512,192]{1,0:T(8,128)(2,1)}, bf16[512,384]{1,0:T(8,128)(2,1)}, bf16[512,768]{1,0:T(8,128)(2,1)}, bf16[512,768]{1,0:T(8,128)(2,1)}, bf16[768,576]{1,0:T(8,128)(2,1)}, /*index=5*/bf16[16,768]{1,0:T(8,128)(2,1)}) custom-call(s32[3]{0:T(128)} %pad_add_fusion.1.sc.refs_0_, bf16[8,120,768]{2,1,0:T(8,128)(2,1)} %copy-done.1, ...), custom_call_target="tpu_custom_call" | custom-call | tf_op jit(solution)/shard_map/qkv/pallas_call | solution.py:23
  74.7 1.1 collective-permute-start.7
  76.1 9.7 %collective-permute-done.7.kv2 = bf16[512,384]{1,0:T(8,128)(2,1)S(1)} collective-permute-done((bf16[512,384]{1,0:T(8,128)(2,1)}, bf16[512,384]{1,0:T(8,128)(2,1)S(1)}, u32[]{:S(2)}, u32[]{:S(2)}) %collective-permute-start.7) | collective-permute-done | bytes 393248 | tf_op jit(solution)/shard_map/ppermute | solution.py:575
  86.5 3.3 %collective-permute-start.9 = (bf16[8,48,768]{2,1,0:T(8,128)(2,1)S(1)}, bf16[8,48,768]{2,1,0:T(8,128)(2,1)S(1)}, u32[]{:S(2)}, u32[]{:S(2)}) collective-permute-start(bf16[8,48,768]{2,1,0:T(8,128)(2,1)S(1)} %all-to-all-done.1), channel_id=1, source_target_pairs={{0,1},{1,0},{2,3},{3,2},{4,5},{5,4},{6,7},{7,6},{8,9},{9,8},{10,11... | collective-permute-start | bytes 1769480 | tf_op jit(solution)/shard_map/ppermute | solution.py:575
  90.6 1.4 copy.35.kid
  92.9 8.4 %attend.1 = (bf16[512,192]{1,0:T(8,128)(2,1)}, f32[512,192]{1,0:T(8,128)}, f32[8,512]{1,0:T(8,128)}) custom-call(s32[3]{0:T(128)} %pad_add_fusion.1.sc.refs_0_, bf16[512,192]{1,0:T(8,128)(2,1)} %get-tuple-element.74.q, bf16[512,384]{1,0:T(8,128)(2,1)} %get-tuple-element.77.kv0, bf16[512,384]{1,0:T(8,128)(2,1)} %copy-done.8, bf16[512,384]{1,0:T(8,128)(2,1)} %copy-done.7, ...), custom_call_target="tpu_custom_call" | custom-call | tf_op jit(solution)/shard_map/attend/pallas_call | solution.py:23
  101.3 3.5 %all-to-all-start.2 = ((bf16[8,64,192]{2,1,0:T(8,128)(2,1)}), bf16[8,64,192]{2,1,0:T(8,128)(2,1)S(1)}, u32[]{:S(2)}, u32[]{:S(2)}) async-start(bf16[8,64,192]{2,1,0:T(8,128)(2,1)} %bitcast.108), calls=%async_computation.2 | async-start | bytes 524288 | tf_op jit(solution)/shard_map/all_to_all | solution.py:613
  106.0 1.3 slice.77.rest2
  107.3 1.3 slice.76.rest1
  108.6 1.3 slice.78.rest3
  110.0 3.2 %expand.1 = (f32[4,128,768]{2,1,0:T(8,128)}, bf16[512,768]{1,0:T(8,128)(2,1)}) custom-call(s32[3]{0:T(128)} %pad_add_fusion.1.sc.refs_0_, bf16[16,768]{1,0:T(8,128)(2,1)} %copy-done.25, bf16[16,768]{1,0:T(8,128)(2,1)} %slice.76.rest1, bf16[16,768]{1,0:T(8,128)(2,1)} %slice.77.rest2, bf16[16,768]{1,0:T(8,128)(2,1)} %slice.78.rest3, s32[512,1]{1,0:T(8,128)} %copy.40.ids, ...), custom_call_target="tpu_custom_call" | custom-call | tf_op jit(solution)/shard_map/expand/pallas_call | solution.py:23
  113.2 1.1 pad_maximum_fusion.weights
  114.3 4.3 %all-to-all-done.2.attn = bf16[8,64,192]{2,1,0:T(8,128)(2,1)S(1)} async-done(((bf16[8,64,192]{2,1,0:T(8,128)(2,1)}), bf16[8,64,192]{2,1,0:T(8,128)(2,1)S(1)}, u32[]{:S(2)}, u32[]{:S(2)}) %all-to-all-start.2) | async-done | bytes 196640 | tf_op jit(solution)/shard_map/all_to_all | solution.py:613
  119.3 3.5 %project.1 = (f32[128,768]{1,0:T(8,128)}, f32[128,768]{1,0:T(8,128)}, f32[128,768]{1,0:T(8,128)}, f32[128,1]{1,0:T(8,128)}, bf16[128,768]{1,0:T(8,128)(2,1)}, /*index=5*/bf16[768,768]{1,0:T(8,128)(2,1)}) custom-call(s32[3]{0:T(128)} %pad_add_fusion.1.sc.refs_0_, bf16[8,64,192]{2,1,0:T(8,128)(2,1)} %copy-done.3, bf16[2,2,32,768]{3,2,1,0:T(8,128)(2,1)} %tok.5, ...), custom_call_target="tpu_custom_call" | custom-call | tf_op jit(solution)/shard_map/project/pallas_call | solution.py:23
  123.6 2.3 collective-permute-start.10
  125.8 1.7 collective-permute-done.11.h2
  127.6 3.0 %collective-permute-start.12 = (bf16[128,768]{1,0:T(8,128)(2,1)S(1)}, bf16[128,768]{1,0:T(8,128)(2,1)S(1)}, u32[]{:S(2)}, u32[]{:S(2)}) collective-permute-start(bf16[128,768]{1,0:T(8,128)(2,1)S(1)} %collective-permute-done.11.h2), channel_id=1, source_target_pairs={{0,1},{1,0},{2,3},{3,2},{4,5},{5,4},{6,7},{7,6},{8,9},{9,8},{10,11... | collective-permute-start | bytes 589832 | tf_op jit(solution)/shard_map/ppermute | solution.py:575
  132.3 6.1 %feed.1 = (bf16[2,128,768]{2,1,0:T(8,128)(2,1)}, bf16[2,128,768]{2,1,0:T(8,128)(2,1)}, bf16[2,128,768]{2,1,0:T(8,128)(2,1)}, bf16[2,128,768]{2,1,0:T(8,128)(2,1)...) custom-call(s32[3]{0:T(128)} %pad_add_fusion.1.sc.refs_0_, ...), custom_call_target="tpu_custom_call" | custom-call | tf_op jit(solution)/shard_map/feed/pallas_call | solution.py:23
  138.7 1.6 collective-permute-done.13.dh_recv
  140.3 1.1 fusion.6
  142.4 5.2 %collective-permute-done.15.dh_far = bf16[128,768]{1,0:T(8,128)(2,1)S(1)} collective-permute-done((bf16[128,768]{1,0:T(8,128)(2,1)S(1)}, bf16[128,768]{1,0:T(8,128)(2,1)S(1)}, u32[]{:S(2)}, u32[]{:S(2)}) %collective-permute-start.15) | collective-permute-done | bytes 196640 | tf_op jit(solution)/shard_map/ppermute | solution.py:575
  148.3 3.7 %middle.1 = (f32[128,768]{1,0:T(8,128)}, f32[128,768]{1,0:T(8,128)}, bf16[128,768]{1,0:T(8,128)(2,1)}, bf16[8,64,192]{2,1,0:T(8,128)(2,1)}) custom-call(s32[3]{0:T(128)} %pad_add_fusion.1.sc.refs_0_, bf16[2,128,768]{2,1,0:T(8,128)(2,1)} %get-tuple-element.87.dh_keep, bf16[2,128,768]{2,1,0:T(8,128)(2,1)} %copy-done.12, bf16[128,768]{1,0:T(8,128)(2,1)} %copy-done.29, ...), custom_call_target="tpu_custom_call" | custom-call | tf_op jit(solution)/shard_map/middle/pallas_call | solution.py:23
  152.0 12.0 %all_to_all.25 = bf16[8,64,192]{2,1,0:T(8,128)(2,1)} all-to-all(bf16[8,64,192]{2,1,0:T(8,128)(2,1)} %get-tuple-element.95), channel_id=1, replica_groups=mesh['cp'=8,'sp'=4] {'cp'}, dimensions={0} | all-to-all | bytes 393216 | tf_op jit(solution)/shard_map/all_to_all | solution.py:613
  164.0 4.7 %feed_grad.1 = bf16[8,192,768]{2,1,0:T(8,128)(2,1)} custom-call(s32[3]{0:T(128)} %pad_add_fusion.1.sc.refs_0_, bf16[512,768]{1,0:T(8,128)(2,1)} %get-tuple-element.96.h, bf16[512,768]{1,0:T(8,128)(2,1)} %get-tuple-element.82.dz_in.dz, bf16[512,768]{1,0:T(8,128)(2,1)} %get-tuple-element.98.act, bf16[512,768]{1,0:T(8,128)(2,1)} %get-tuple-element.99.du), custom_call_target="tpu_custom_call" | custom-call | tf_op jit(solution)/shard_map/feed_grad/pallas_call | solution.py:23
  168.8 14.0 %attend_back.1 = (f32[512,192]{1,0:T(8,128)}, bf16[2,512,384]{2,1,0:T(8,128)(2,1)}, bf16[2,512,384]{2,1,0:T(8,128)(2,1)}) custom-call(s32[3]{0:T(128)} %pad_add_fusion.1.sc.refs_0_, bf16[512,192]{1,0:T(8,128)(2,1)} %get-tuple-element.74.q, bf16[512,384]{1,0:T(8,128)(2,1)} %get-tuple-element.77.kv0, bf16[512,384]{1,0:T(8,128)(2,1)} %copy-done.8, ...), custom_call_target="tpu_custom_call" | custom-call | tf_op jit(solution)/shard_map/attend_back/pallas_call | solution.py:23
  182.8 2.8 %collective-permute-start.16 = (bf16[2,512,384]{2,1,0:T(8,128)(2,1)}, bf16[2,512,384]{2,1,0:T(8,128)(2,1)S(1)}, u32[]{:S(2)}, u32[]{:S(2)}) collective-permute-start(bf16[2,512,384]{2,1,0:T(8,128)(2,1)} %get-tuple-element.103), channel_id=1, source_target_pairs={{0,1},{1,0},{2,3},{3,2},{4,5},{5,4},{6,7},{7,6},{8,9},{9,8},{10,11... | collective-permute-start | bytes 2359304 | tf_op jit(solution)/shard_map/ppermute | solution.py:575
  186.3 3.3 %middle_grad.1 = (f32[3,16,768]{2,1,0:T(8,128)}, bf16[8,48,768]{2,1,0:T(8,128)(2,1)}, bf16[8,48,768]{2,1,0:T(8,128)(2,1)}) custom-call(s32[3]{0:T(128)} %pad_add_fusion.1.sc.refs_0_, f32[128,768]{1,0:T(8,128)} %get-tuple-element.111.dx, f32[128,768]{1,0:T(8,128)} %get-tuple-element.117.dh, bf16[128,768]{1,0:T(8,128)(2,1)} %get-tuple-element.118.dy, ...), custom_call_target="tpu_custom_call" | custom-call | tf_op jit(solution)/shard_map/middle_grad/pallas_call | solution.py:23
  192.0 1.1 collective-permute-start.26
  193.1 7.8 %collective-permute-done.17.dkv_c = bf16[512,384]{1,0:T(8,128)(2,1)} collective-permute-done((bf16[512,384]{1,0:T(8,128)(2,1)}, bf16[512,384]{1,0:T(8,128)(2,1)}, u32[]{:S(2)}, u32[]{:S(2)}) %collective-permute-start.17) | collective-permute-done | bytes 393248 | tf_op jit(solution)/shard_map/ppermute | solution.py:575
  200.9 5.0 %qkv_back.1 = (bf16[8,64,768]{2,1,0:T(8,128)(2,1)}, bf16[512,768]{1,0:T(8,128)(2,1)}, bf16[512,576]{1,0:T(8,128)(2,1)}) custom-call(s32[3]{0:T(128)} %pad_add_fusion.1.sc.refs_0_, f32[512,192]{1,0:T(8,128)} %get-tuple-element.101.dq, bf16[2,512,384]{2,1,0:T(8,128)(2,1)} %get-tuple-element.102.dkv_a, bf16[2,512,384]{2,1,0:T(8,128)(2,1)} %copy-done.6, ...), custom_call_target="tpu_custom_call" | custom-call | tf_op jit(solution)/shard_map/qkv_back/pallas_call | solution.py:23
  206.8 3.8 %all-to-all-start.4 = ((bf16[8,64,768]{2,1,0:T(8,128)(2,1)}), bf16[8,64,768]{2,1,0:T(8,128)(2,1)S(1)}, u32[]{:S(2)}, u32[]{:S(2)}) async-start(bf16[8,64,768]{2,1,0:T(8,128)(2,1)} %get-tuple-element.106), calls=%async_computation.4 | async-start | bytes 1572864 | tf_op jit(solution)/shard_map/all_to_all | solution.py:613
  210.6 4.1 %qkv_grad.1 = (f32[2,16,768]{2,1,0:T(8,128)}, bf16[8,48,768]{2,1,0:T(8,128)(2,1)}, bf16[8,48,768]{2,1,0:T(8,128)(2,1)}) custom-call(s32[3]{0:T(128)} %pad_add_fusion.1.sc.refs_0_, bf16[512,576]{1,0:T(8,128)(2,1)} %get-tuple-element.112.d, bf16[512,768]{1,0:T(8,128)(2,1)} %get-tuple-element.113.dh, bf16[512,768]{1,0:T(8,128)(2,1)} %get-tuple-element.114.h, ...), custom_call_target="tpu_custom_call" | custom-call | tf_op jit(solution)/shard_map/qkv_grad/pallas_call | solution.py:23
  215.6 1.8 collective-permute-start.24
  218.1 2.7 block.1
  221.9 1.2 collective-permute-done.19
  223.2 1.5 collective-permute-start.20
  225.1 3.6 %collective-permute-done.20 = bf16[6,16,768]{2,1,0:T(8,128)(2,1)S(1)} collective-permute-done((bf16[6,16,768]{2,1,0:T(8,128)(2,1)S(1)}, bf16[6,16,768]{2,1,0:T(8,128)(2,1)S(1)}, u32[]{:S(2)}, u32[]{:S(2)}) %collective-permute-start.20) | collective-permute-done | bytes 147488 | tf_op jit(solution)/shard_map/ppermute | solution.py:575
  228.7 1.5 collective-permute-start.21
  230.2 2.9 %collective-permute-done.21 = bf16[6,16,768]{2,1,0:T(8,128)(2,1)S(1)} collective-permute-done((bf16[6,16,768]{2,1,0:T(8,128)(2,1)S(1)}, bf16[6,16,768]{2,1,0:T(8,128)(2,1)S(1)}, u32[]{:S(2)}, u32[]{:S(2)}) %collective-permute-start.21) | collective-permute-done | bytes 147488 | tf_op jit(solution)/shard_map/ppermute | solution.py:575
  233.2 4.9 %collective-permute-done.27 = bf16[12,48,384]{2,1,0:T(8,128)(2,1)S(1)} collective-permute-done((bf16[12,48,384]{2,1,0:T(8,128)(2,1)S(1)}, bf16[12,48,384]{2,1,0:T(8,128)(2,1)S(1)}, u32[]{:S(2)}, u32[]{:S(2)}) %collective-permute-start.27) | collective-permute-done | bytes 442400 | tf_op jit(solution)/shard_map/ppermute | solution.py:575
  238.3 1.5 collective-permute-start.22
  239.8 2.5 last.1
  242.4 1.2 collective-permute-start.28
  243.7 2.1 collective-permute-start.23
  245.8 1.5 collective-permute-start.35
  248.2 1.9 collective-permute-start.30
  251.2 5.8 %collective-permute-done.30 = bf16[2,48,384]{2,1,0:T(8,128)(2,1)S(1)} collective-permute-done((bf16[2,48,384]{2,1,0:T(8,128)(2,1)S(1)}, bf16[2,48,384]{2,1,0:T(8,128)(2,1)S(1)}, u32[]{:S(2)}, u32[]{:S(2)}) %collective-permute-start.30) | collective-permute-done | bytes 73760 | tf_op jit(solution)/shard_map/ppermute | solution.py:575
  257.1 1.3 collective-permute-start.32
  258.4 2.9 %collective-permute-start.34 = (bf16[192,768]{1,0:T(8,128)(2,1)S(1)}, bf16[192,768]{1,0:T(8,128)(2,1)S(1)}, u32[]{:S(2)}, u32[]{:S(2)}) collective-permute-start(bf16[192,768]{1,0:T(8,128)(2,1)S(1)} %bitcast.106), channel_id=1, source_target_pairs={{0,1},{1,0},{2,3},{3,2},{4,5},{5,4},{6,7},{7,6},{8,9},{9,8},{10,11... | collective-permute-start | bytes 884744 | tf_op jit(solution)/shard_map/ppermute | solution.py:575
  261.6 3.8 %collective-permute-start.33 = (bf16[2,5,48,384]{3,2,1,0:T(8,128)(2,1)S(1)}, bf16[2,5,48,384]{3,2,1,0:T(8,128)(2,1)S(1)}, u32[]{:S(2)}, u32[]{:S(2)}) collective-permute-start(bf16[2,5,48,384]{3,2,1,0:T(8,128)(2,1)S(1)} %pad_maximum_fusion.2.own), channel_id=1, source_target_pairs={{0,1},{1,0},{2,3},{3,2},{4,5},{5,4},{6,7},{7,6},{8,9},{9,8},{10,11... | collective-permute-start | bytes 1105928 | tf_op jit(solution)/shard_map/ppermute | solution.py:575
  266.2 2.1 fusion.25
  269.7 3.1 %finish.1 = (f32[96,3072]{1,0:T(8,128)}, f32[384,768]{1,0:T(8,128)}) custom-call(s32[3]{0:T(128)} %pad_add_fusion.1.sc.refs_0_, bf16[192,768]{1,0:T(8,128)(2,1)} %bitcast.104, bf16[192,768]{1,0:T(8,128)(2,1)} %copy-done.23, bf16[192,768]{1,0:T(8,128)(2,1)} %copy-done.22, bf16[192,768]{1,0:T(8,128)(2,1)} %copy-done.24), custom_call_target="tpu_custom_call" | custom-call | tf_op jit(solution)/shard_map/finish/pallas_call | solution.py:23
  273.5 2.4 finish_qkv.1
  (205 shorter events, 31.7 us)
Async XLA Ops:
  15.6 6.7 %copy-start.4 = (bf16[2,2,32,768]{3,2,1,0:T(8,128)(2,1)S(1)}, bf16[2,2,32,768]{3,2,1,0:T(8,128)(2,1)}, u32[]{:S(2)}) copy-start(bf16[2,2,32,768]{3,2,1,0:T(8,128)(2,1)} %grad.3) | copy-start | bytes 589828
  15.6 40.8 %copy-start.39 = (s32[16]{0:T(128)S(1)}, s32[16]{0:T(128)}, u32[]{:S(2)}) copy-start(s32[16]{0:T(128)} %param.16) | copy-start | bytes 196
  15.6 40.9 %copy-start.36 = (bf16[96,768]{1,0:T(8,128)(2,1)S(1)}, bf16[96,768]{1,0:T(8,128)(2,1)}, u32[]{:S(2)}) copy-start(bf16[96,768]{1,0:T(8,128)(2,1)} %param.21) | copy-start | bytes 442372
  15.6 40.9 %copy-start.38 = (s32[2,2048]{1,0:T(2,128)S(1)}, s32[2,2048]{1,0:T(2,128)}, u32[]{:S(2)}) copy-start(s32[2,2048]{1,0:T(2,128)} %param.17) | copy-start | bytes 49156
  15.6 40.7 %all-to-all-start = ((bf16[8,120,768]{2,1,0:T(8,128)(2,1)}), bf16[8,120,768]{2,1,0:T(8,128)(2,1)S(1)}, u32[]{:S(2)}, u32[]{:S(2)}) async-start(bf16[8,120,768]{2,1,0:T(8,128)(2,1)} %get-tuple-element.72), calls=%async_computation | async-start | bytes 2949120 | tf_op jit(solution)/shard_map/all_to_all | solution.py:613
  22.2 109.4 %all-gather.3.cloned.1.call-start = ((), (), s32[]{:S(2)}) async-start(), calls=%async_computation.7 | async-start | bytes 2654208 | tf_op jit(solution)/shard_map/all_gather | solution.py:714
  22.3 5.6 %collective-permute-start.1 = (bf16[2,2,32,768]{3,2,1,0:T(8,128)(2,1)S(1)}, bf16[2,2,32,768]{3,2,1,0:T(8,128)(2,1)S(1)}, u32[]{:S(2)}, u32[]{:S(2)}) collective-permute-start(bf16[2,2,32,768]{3,2,1,0:T(8,128)(2,1)S(1)} %copy-done.4), channel_id=1, source_target_pairs={{0,2},{1,3},{2,0},{3,1},{4,6},{5,7},{6,4},{7,5},{8,10},{9,11},{10,... | collective-permute-start | bytes 589832 | tf_op jit(solution)/shard_map/ppermute | solution.py:575
  23.5 6.1 %collective-permute-start = (bf16[2,2,32,768]{3,2,1,0:T(8,128)(2,1)S(1)}, bf16[2,2,32,768]{3,2,1,0:T(8,128)(2,1)S(1)}, u32[]{:S(2)}, u32[]{:S(2)}) collective-permute-start(bf16[2,2,32,768]{3,2,1,0:T(8,128)(2,1)S(1)} %copy-done.4), channel_id=1, source_target_pairs={{0,1},{1,0},{2,3},{3,2},{4,5},{5,4},{6,7},{7,6},{8,9},{9,8},{10,11... | collective-permute-start | bytes 589832 | tf_op jit(solution)/shard_map/ppermute | solution.py:575
  27.8 3.0 %collective-permute-start.2 = (bf16[2,2,32,768]{3,2,1,0:T(8,128)(2,1)S(1)}, bf16[2,2,32,768]{3,2,1,0:T(8,128)(2,1)}, u32[]{:S(2)}, u32[]{:S(2)}) collective-permute-start(bf16[2,2,32,768]{3,2,1,0:T(8,128)(2,1)S(1)} %collective-permute-done.1.g2), channel_id=1, source_target_pairs={{0,1},{1,0},{2,3},{3,2},{4,5},{5,4},{6,7},{7,6},{8,9},{9,8},{10,11... | collective-permute-start | bytes 589832 | tf_op jit(solution)/shard_map/ppermute | solution.py:575
  56.3 2.4 copy-start.1
  56.7 11.9 %copy-start.11 = (bf16[208,768]{1,0:T(8,128)(2,1)}, bf16[208,768]{1,0:T(8,128)(2,1)S(1)}, u32[]{:S(2)}) copy-start(bf16[208,768]{1,0:T(8,128)(2,1)S(1)} %pad_maximum_fusion.3.refs_6_) | copy-start | bytes 958468
  56.7 9.1 %collective-permute-start.4 = (bf16[208,768]{1,0:T(8,128)(2,1)S(1)}, bf16[208,768]{1,0:T(8,128)(2,1)S(1)}, u32[]{:S(2)}, u32[]{:S(2)}) collective-permute-start(bf16[208,768]{1,0:T(8,128)(2,1)S(1)} %pad_maximum_fusion.3.refs_6_), channel_id=1, source_target_pairs={{0,2},{1,3},{2,0},{3,1},{4,6},{5,7},{6,4},{7,5},{8,10},{9,11},{10,... | collective-permute-start | bytes 958472 | tf_op jit(solution)/shard_map/ppermute | solution.py:575
  58.7 27.8 %all-to-all-start.1 = ((bf16[8,48,768]{2,1,0:T(8,128)(2,1)}), bf16[8,48,768]{2,1,0:T(8,128)(2,1)S(1)}, u32[]{:S(2)}, u32[]{:S(2)}) async-start(bf16[8,48,768]{2,1,0:T(8,128)(2,1)} %broadcast_in_dim.56), calls=%async_computation.1 | async-start | bytes 1179648 | tf_op jit(solution)/shard_map/all_to_all | solution.py:613
  64.7 3.8 %collective-permute-start.3 = (bf16[208,768]{1,0:T(8,128)(2,1)S(1)}, bf16[208,768]{1,0:T(8,128)(2,1)S(1)}, u32[]{:S(2)}, u32[]{:S(2)}) collective-permute-start(bf16[208,768]{1,0:T(8,128)(2,1)S(1)} %pad_maximum_fusion.3.refs_6_), channel_id=1, source_target_pairs={{0,1},{1,0},{2,3},{3,2},{4,5},{5,4},{6,7},{7,6},{8,9},{9,8},{10,11... | collective-permute-start | bytes 958472 | tf_op jit(solution)/shard_map/ppermute | solution.py:575
  65.8 2.8 copy-start.17
  65.8 2.8 collective-permute-start.5
  74.7 11.1 %collective-permute-start.7 = (bf16[512,384]{1,0:T(8,128)(2,1)}, bf16[512,384]{1,0:T(8,128)(2,1)S(1)}, u32[]{:S(2)}, u32[]{:S(2)}) collective-permute-start(bf16[512,384]{1,0:T(8,128)(2,1)} %get-tuple-element.77.kv0), channel_id=1, source_target_pairs={{0,2},{1,3},{2,0},{3,1},{4,6},{5,7},{6,4},{7,5},{8,10},{9,11},{10,... | collective-permute-start | bytes 1179656 | tf_op jit(solution)/shard_map/ppermute | solution.py:575
  75.8 16.2 %collective-permute-start.6 = (bf16[512,384]{1,0:T(8,128)(2,1)}, bf16[512,384]{1,0:T(8,128)(2,1)S(1)}, u32[]{:S(2)}, u32[]{:S(2)}) collective-permute-start(bf16[512,384]{1,0:T(8,128)(2,1)} %get-tuple-element.77.kv0), channel_id=1, source_target_pairs={{0,1},{1,0},{2,3},{3,2},{4,5},{5,4},{6,7},{7,6},{8,9},{9,8},{10,11... | collective-permute-start | bytes 1179656 | tf_op jit(solution)/shard_map/ppermute | solution.py:575
  85.8 6.2 %copy-start.7 = (bf16[512,384]{1,0:T(8,128)(2,1)}, bf16[512,384]{1,0:T(8,128)(2,1)S(1)}, u32[]{:S(2)}) copy-start(bf16[512,384]{1,0:T(8,128)(2,1)S(1)} %collective-permute-done.7.kv2) | copy-start | bytes 1179652
  85.8 6.2 %collective-permute-start.8 = (bf16[512,384]{1,0:T(8,128)(2,1)S(1)}, bf16[512,384]{1,0:T(8,128)(2,1)S(1)}, u32[]{:S(2)}, u32[]{:S(2)}) collective-permute-start(bf16[512,384]{1,0:T(8,128)(2,1)S(1)} %collective-permute-done.7.kv2), channel_id=1, source_target_pairs={{0,1},{1,0},{2,3},{3,2},{4,5},{5,4},{6,7},{7,6},{8,9},{9,8},{10,11... | collective-permute-start | bytes 1179656 | tf_op jit(solution)/shard_map/ppermute | solution.py:575
  86.5 26.7 %collective-permute-start.9 = (bf16[8,48,768]{2,1,0:T(8,128)(2,1)S(1)}, bf16[8,48,768]{2,1,0:T(8,128)(2,1)S(1)}, u32[]{:S(2)}, u32[]{:S(2)}) collective-permute-start(bf16[8,48,768]{2,1,0:T(8,128)(2,1)S(1)} %all-to-all-done.1), channel_id=1, source_target_pairs={{0,1},{1,0},{2,3},{3,2},{4,5},{5,4},{6,7},{7,6},{8,9},{9,8},{10,11... | collective-permute-start | bytes 1769480 | tf_op jit(solution)/shard_map/ppermute | solution.py:575
  89.8 2.2 copy-start.35
  101.3 17.3 %all-to-all-start.2 = ((bf16[8,64,192]{2,1,0:T(8,128)(2,1)}), bf16[8,64,192]{2,1,0:T(8,128)(2,1)S(1)}, u32[]{:S(2)}, u32[]{:S(2)}) async-start(bf16[8,64,192]{2,1,0:T(8,128)(2,1)} %bitcast.108), calls=%async_computation.2 | async-start | bytes 524288 | tf_op jit(solution)/shard_map/all_to_all | solution.py:613
  104.8 137.4 %reduce-scatter.2.cloned.1.call-start = ((), (), s32[]{:S(2)}) async-start(), calls=%async_computation.6 | async-start | bytes 2654208 | tf_op jit(solution)/shard_map/reduce_scatter | solution.py:854
  122.8 4.7 %collective-permute-start.11 = (bf16[128,768]{1,0:T(8,128)(2,1)}, bf16[128,768]{1,0:T(8,128)(2,1)S(1)}, u32[]{:S(2)}, u32[]{:S(2)}) collective-permute-start(bf16[128,768]{1,0:T(8,128)(2,1)} %get-tuple-element.81.h0), channel_id=1, source_target_pairs={{0,2},{1,3},{2,0},{3,1},{4,6},{5,7},{6,4},{7,5},{8,10},{9,11},{10,... | collective-permute-start | bytes 589832 | tf_op jit(solution)/shard_map/ppermute | solution.py:575
  123.6 7.0 %collective-permute-start.10 = (bf16[128,768]{1,0:T(8,128)(2,1)}, bf16[128,768]{1,0:T(8,128)(2,1)S(1)}, u32[]{:S(2)}, u32[]{:S(2)}) collective-permute-start(bf16[128,768]{1,0:T(8,128)(2,1)} %get-tuple-element.81.h0), channel_id=1, source_target_pairs={{0,1},{1,0},{2,3},{3,2},{4,5},{5,4},{6,7},{7,6},{8,9},{9,8},{10,11... | collective-permute-start | bytes 589832 | tf_op jit(solution)/shard_map/ppermute | solution.py:575
  127.6 4.0 %copy-start.26 = (bf16[128,768]{1,0:T(8,128)(2,1)}, bf16[128,768]{1,0:T(8,128)(2,1)S(1)}, u32[]{:S(2)}) copy-start(bf16[128,768]{1,0:T(8,128)(2,1)S(1)} %collective-permute-done.11.h2) | copy-start | bytes 589828
  127.6 4.0 %collective-permute-start.12 = (bf16[128,768]{1,0:T(8,128)(2,1)S(1)}, bf16[128,768]{1,0:T(8,128)(2,1)S(1)}, u32[]{:S(2)}, u32[]{:S(2)}) collective-permute-start(bf16[128,768]{1,0:T(8,128)(2,1)S(1)} %collective-permute-done.11.h2), channel_id=1, source_target_pairs={{0,1},{1,0},{2,3},{3,2},{4,5},{5,4},{6,7},{7,6},{8,9},{9,8},{10,11... | collective-permute-start | bytes 589832 | tf_op jit(solution)/shard_map/ppermute | solution.py:575
  138.4 1.9 collective-permute-start.13
  140.3 7.3 %copy-start.12 = (bf16[2,128,768]{2,1,0:T(8,128)(2,1)}, bf16[2,128,768]{2,1,0:T(8,128)(2,1)S(1)}, u32[]{:S(2)}) copy-start(bf16[2,128,768]{2,1,0:T(8,128)(2,1)S(1)} %collective-permute-done.13.dh_recv) | copy-start | bytes 1179652
  141.4 6.2 %collective-permute-start.15 = (bf16[128,768]{1,0:T(8,128)(2,1)S(1)}, bf16[128,768]{1,0:T(8,128)(2,1)S(1)}, u32[]{:S(2)}, u32[]{:S(2)}) collective-permute-start(bf16[128,768]{1,0:T(8,128)(2,1)S(1)} %fusion.6), channel_id=1, source_target_pairs={{0,2},{1,3},{2,0},{3,1},{4,6},{5,7},{6,4},{7,5},{8,10},{9,11},{10,... | collective-permute-start | bytes 589832 | tf_op jit(solution)/shard_map/ppermute | solution.py:575
  182.7 6.9 %copy-start.5 = (bf16[2,512,384]{2,1,0:T(8,128)(2,1)S(1)}, bf16[2,512,384]{2,1,0:T(8,128)(2,1)}, u32[]{:S(2)}) copy-start(bf16[2,512,384]{2,1,0:T(8,128)(2,1)} %get-tuple-element.102.dkv_a) | copy-start | bytes 2359300
  182.8 6.9 %collective-permute-start.16 = (bf16[2,512,384]{2,1,0:T(8,128)(2,1)}, bf16[2,512,384]{2,1,0:T(8,128)(2,1)S(1)}, u32[]{:S(2)}, u32[]{:S(2)}) collective-permute-start(bf16[2,512,384]{2,1,0:T(8,128)(2,1)} %get-tuple-element.103), channel_id=1, source_target_pairs={{0,1},{1,0},{2,3},{3,2},{4,5},{5,4},{6,7},{7,6},{8,9},{9,8},{10,11... | collective-permute-start | bytes 2359304 | tf_op jit(solution)/shard_map/ppermute | solution.py:575
  189.6 2.2 copy-start.16
  189.6 2.2 collective-permute-start.25
  189.7 2.3 copy-start.6
  190.5 10.4 %collective-permute-start.17 = (bf16[512,384]{1,0:T(8,128)(2,1)}, bf16[512,384]{1,0:T(8,128)(2,1)}, u32[]{:S(2)}, u32[]{:S(2)}) collective-permute-start(bf16[512,384]{1,0:T(8,128)(2,1)} %fusion.2), channel_id=1, source_target_pairs={{0,2},{1,3},{2,0},{3,1},{4,6},{5,7},{6,4},{7,5},{8,10},{9,11},{10,... | collective-permute-start | bytes 1179656 | tf_op jit(solution)/shard_map/ppermute | solution.py:575
  190.5 15.4 %collective-permute-start.14 = (bf16[2,128,768]{2,1,0:T(8,128)(2,1)}, bf16[2,128,768]{2,1,0:T(8,128)(2,1)S(1)}, u32[]{:S(2)}, u32[]{:S(2)}) collective-permute-start(bf16[2,128,768]{2,1,0:T(8,128)(2,1)} %get-tuple-element.89), channel_id=1, source_target_pairs={{0,1},{1,0},{2,3},{3,2},{4,5},{5,4},{6,7},{7,6},{8,9},{9,8},{10,11... | collective-permute-start | bytes 1179656 | tf_op jit(solution)/shard_map/ppermute | solution.py:575
  192.0 23.6 %collective-permute-start.26 = (bf16[4,48,768]{2,1,0:T(8,128)(2,1)S(1)}, bf16[4,48,768]{2,1,0:T(8,128)(2,1)S(1)}, u32[]{:S(2)}, u32[]{:S(2)}) collective-permute-start(bf16[4,48,768]{2,1,0:T(8,128)(2,1)S(1)} %dynamic-slice_bitcast_fusion), channel_id=1, source_target_pairs={{0,4},{4,0},{8,12},{12,8},{16,20},{20,16},{24,28},{28,24},{1,5},{5... | collective-permute-start | bytes 884744 | tf_op jit(solution)/shard_map/ppermute | solution.py:575
  200.9 5.0 %copy-start.13 = (bf16[2,128,768]{2,1,0:T(8,128)(2,1)S(1)}, bf16[2,128,768]{2,1,0:T(8,128)(2,1)}, u32[]{:S(2)}) copy-start(bf16[2,128,768]{2,1,0:T(8,128)(2,1)} %get-tuple-element.85.z_keep) | copy-start | bytes 1179652
  200.9 5.8 %copy-start.33 = (f32[3,16,768]{2,1,0:T(8,128)S(1)}, f32[3,16,768]{2,1,0:T(8,128)}, u32[]{:S(2)}) copy-start(f32[3,16,768]{2,1,0:T(8,128)} %get-tuple-element.121) | copy-start | bytes 442372
  206.7 10.7 %collective-permute-start.18 = (bf16[128,768]{1,0:T(8,128)(2,1)}, bf16[128,768]{1,0:T(8,128)(2,1)S(1)}, u32[]{:S(2)}, u32[]{:S(2)}) collective-permute-start(bf16[128,768]{1,0:T(8,128)(2,1)} %fusion.7), channel_id=1, source_target_pairs={{0,2},{1,3},{2,0},{3,1},{4,6},{5,7},{6,4},{7,5},{8,10},{9,11},{10,... | collective-permute-start | bytes 589832 | tf_op jit(solution)/shard_map/ppermute | solution.py:575
  206.8 31.4 %all-to-all-start.4 = ((bf16[8,64,768]{2,1,0:T(8,128)(2,1)}), bf16[8,64,768]{2,1,0:T(8,128)(2,1)S(1)}, u32[]{:S(2)}, u32[]{:S(2)}) async-start(bf16[8,64,768]{2,1,0:T(8,128)(2,1)} %get-tuple-element.106), calls=%async_computation.4 | async-start | bytes 1572864 | tf_op jit(solution)/shard_map/all_to_all | solution.py:613
  215.6 9.1 %collective-permute-start.24 = (bf16[8,48,768]{2,1,0:T(8,128)(2,1)}, bf16[8,48,768]{2,1,0:T(8,128)(2,1)S(1)}, u32[]{:S(2)}, u32[]{:S(2)}) collective-permute-start(bf16[8,48,768]{2,1,0:T(8,128)(2,1)} %get-tuple-element.125), channel_id=1, source_target_pairs={{0,1},{1,0},{2,3},{3,2},{4,5},{5,4},{6,7},{7,6},{8,9},{9,8},{10,11... | collective-permute-start | bytes 1769480 | tf_op jit(solution)/shard_map/ppermute | solution.py:575
  220.8 3.9 %copy-start.15 = (bf16[8,48,768]{2,1,0:T(8,128)(2,1)S(1)}, bf16[8,48,768]{2,1,0:T(8,128)(2,1)}, u32[]{:S(2)}) copy-start(bf16[8,48,768]{2,1,0:T(8,128)(2,1)} %get-tuple-element.124) | copy-start | bytes 1769476
  221.7 1.4 collective-permute-start.19
  223.2 5.5 %collective-permute-start.20 = (bf16[6,16,768]{2,1,0:T(8,128)(2,1)S(1)}, bf16[6,16,768]{2,1,0:T(8,128)(2,1)S(1)}, u32[]{:S(2)}, u32[]{:S(2)}) collective-permute-start(bf16[6,16,768]{2,1,0:T(8,128)(2,1)S(1)} %add_convert_fusion.9), channel_id=1, source_target_pairs={{0,2},{1,3},{2,0},{3,1},{4,6},{5,7},{6,4},{7,5},{8,10},{9,11},{10,... | collective-permute-start | bytes 442376 | tf_op jit(solution)/shard_map/ppermute | solution.py:575
  225.0 13.2 %collective-permute-start.27 = (bf16[12,48,384]{2,1,0:T(8,128)(2,1)S(1)}, bf16[12,48,384]{2,1,0:T(8,128)(2,1)S(1)}, u32[]{:S(2)}, u32[]{:S(2)}) collective-permute-start(bf16[12,48,384]{2,1,0:T(8,128)(2,1)S(1)} %pad_maximum_fusion.1), channel_id=1, source_target_pairs={{0,2},{1,3},{2,0},{3,1},{4,6},{5,7},{6,4},{7,5},{8,10},{9,11},{10,... | collective-permute-start | bytes 1327112 | tf_op jit(solution)/shard_map/ppermute | solution.py:575
  228.7 4.5 %collective-permute-start.21 = (bf16[6,16,768]{2,1,0:T(8,128)(2,1)S(1)}, bf16[6,16,768]{2,1,0:T(8,128)(2,1)S(1)}, u32[]{:S(2)}, u32[]{:S(2)}) collective-permute-start(bf16[6,16,768]{2,1,0:T(8,128)(2,1)S(1)} %add_convert_fusion.8), channel_id=1, source_target_pairs={{0,4},{4,0},{8,12},{12,8},{16,20},{20,16},{24,28},{28,24},{1,5},{5... | collective-permute-start | bytes 442376 | tf_op jit(solution)/shard_map/ppermute | solution.py:575
  238.3 5.4 %collective-permute-start.22 = (bf16[6,16,768]{2,1,0:T(8,128)(2,1)S(1)}, bf16[6,16,768]{2,1,0:T(8,128)(2,1)S(1)}, u32[]{:S(2)}, u32[]{:S(2)}) collective-permute-start(bf16[6,16,768]{2,1,0:T(8,128)(2,1)S(1)} %convert_add_fusion.3), channel_id=1, source_target_pairs={{0,8},{4,12},{8,0},{12,4},{16,24},{20,28},{24,16},{28,20},{1,9},{5... | collective-permute-start | bytes 442376 | tf_op jit(solution)/shard_map/ppermute | solution.py:575
  242.3 3.5 %copy-start.21 = (bf16[1,192,768]{2,1,0:T(8,128)(2,1)S(1)}, bf16[1,192,768]{2,1,0:T(8,128)(2,1)}, u32[]{:S(2)}) copy-start(bf16[1,192,768]{2,1,0:T(8,128)(2,1)} %reduce-scatter.2.cloned.1.call-done) | copy-start | bytes 884740
  242.4 4.9 %collective-permute-start.28 = (bf16[4,48,384]{2,1,0:T(8,128)(2,1)S(1)}, bf16[4,48,384]{2,1,0:T(8,128)(2,1)S(1)}, u32[]{:S(2)}, u32[]{:S(2)}) collective-permute-start(bf16[4,48,384]{2,1,0:T(8,128)(2,1)S(1)} %dynamic-slice_bitcast_fusion.1), channel_id=1, source_target_pairs={{0,4},{4,0},{8,12},{12,8},{16,20},{20,16},{24,28},{28,24},{1,5},{5... | collective-permute-start | bytes 442376 | tf_op jit(solution)/shard_map/ppermute | solution.py:575
  243.7 14.7 %collective-permute-start.23 = (bf16[6,16,768]{2,1,0:T(8,128)(2,1)S(1)}, bf16[6,16,768]{2,1,0:T(8,128)(2,1)S(1)}, u32[]{:S(2)}, u32[]{:S(2)}) collective-permute-start(bf16[6,16,768]{2,1,0:T(8,128)(2,1)S(1)} %add_convert_fusion.7), channel_id=1, source_target_pairs={{0,16},{4,20},{8,24},{12,28},{16,0},{20,4},{24,8},{28,12},{1,17},{... | collective-permute-start | bytes 442376 | tf_op jit(solution)/shard_map/ppermute | solution.py:575
  245.8 15.5 %collective-permute-start.35 = (bf16[192,768]{1,0:T(8,128)(2,1)S(1)}, bf16[192,768]{1,0:T(8,128)(2,1)S(1)}, u32[]{:S(2)}, u32[]{:S(2)}) collective-permute-start(bf16[192,768]{1,0:T(8,128)(2,1)S(1)} %bitcast.105), channel_id=1, source_target_pairs={{0,2},{1,3},{2,0},{3,1},{4,6},{5,7},{6,4},{7,5},{8,10},{9,11},{10,... | collective-permute-start | bytes 884744 | tf_op jit(solution)/shard_map/ppermute | solution.py:575
  247.4 3.8 %collective-permute-start.29 = (bf16[2,48,384]{2,1,0:T(8,128)(2,1)S(1)}, bf16[2,48,384]{2,1,0:T(8,128)(2,1)S(1)}, u32[]{:S(2)}, u32[]{:S(2)}) collective-permute-start(bf16[2,48,384]{2,1,0:T(8,128)(2,1)S(1)} %pad_maximum_fusion.5), channel_id=1, source_target_pairs={{0,8},{4,12},{8,0},{12,4},{16,24},{20,28},{24,16},{28,20},{1,9},{5... | collective-permute-start | bytes 221192 | tf_op jit(solution)/shard_map/ppermute | solution.py:575
  248.2 8.8 %collective-permute-start.30 = (bf16[2,48,384]{2,1,0:T(8,128)(2,1)S(1)}, bf16[2,48,384]{2,1,0:T(8,128)(2,1)S(1)}, u32[]{:S(2)}, u32[]{:S(2)}) collective-permute-start(bf16[2,48,384]{2,1,0:T(8,128)(2,1)S(1)} %pad_maximum_fusion.6), channel_id=1, source_target_pairs={{0,16},{4,20},{8,24},{12,28},{16,0},{20,4},{24,8},{28,12},{1,17},{... | collective-permute-start | bytes 221192 | tf_op jit(solution)/shard_map/ppermute | solution.py:575
  250.1 6.9 %collective-permute-start.31 = (bf16[2,48,384]{2,1,0:T(8,128)(2,1)S(1)}, bf16[2,48,384]{2,1,0:T(8,128)(2,1)S(1)}, u32[]{:S(2)}, u32[]{:S(2)}) collective-permute-start(bf16[2,48,384]{2,1,0:T(8,128)(2,1)S(1)} %pad_maximum_fusion.7), channel_id=1, source_target_pairs={{0,24},{4,28},{8,16},{12,20},{16,8},{20,12},{24,0},{28,4},{1,25},{... | collective-permute-start | bytes 221192 | tf_op jit(solution)/shard_map/ppermute | solution.py:575
  257.1 9.1 %copy-start.37 = (bf16[16,96]{1,0:T(8,128)(2,1)S(1)}, bf16[16,96]{1,0:T(8,128)(2,1)}, u32[]{:S(2)}) copy-start(bf16[16,96]{1,0:T(8,128)(2,1)} %multiply_convert_fusion.cond) | copy-start | bytes 9220
  257.1 4.5 %collective-permute-start.32 = (bf16[5,48,384]{2,1,0:T(8,128)(2,1)S(1)}, bf16[5,48,384]{2,1,0:T(8,128)(2,1)S(1)}, u32[]{:S(2)}, u32[]{:S(2)}) collective-permute-start(bf16[5,48,384]{2,1,0:T(8,128)(2,1)S(1)} %fusion.8), channel_id=1, source_target_pairs={{0,2},{1,3},{2,0},{3,1},{4,6},{5,7},{6,4},{7,5},{8,10},{9,11},{10,... | collective-permute-start | bytes 552968 | tf_op jit(solution)/shard_map/ppermute | solution.py:575
  258.4 9.8 %collective-permute-start.34 = (bf16[192,768]{1,0:T(8,128)(2,1)S(1)}, bf16[192,768]{1,0:T(8,128)(2,1)S(1)}, u32[]{:S(2)}, u32[]{:S(2)}) collective-permute-start(bf16[192,768]{1,0:T(8,128)(2,1)S(1)} %bitcast.106), channel_id=1, source_target_pairs={{0,1},{1,0},{2,3},{3,2},{4,5},{5,4},{6,7},{7,6},{8,9},{9,8},{10,11... | collective-permute-start | bytes 884744 | tf_op jit(solution)/shard_map/ppermute | solution.py:575
  261.3 6.9 %copy-start.22 = (bf16[192,768]{1,0:T(8,128)(2,1)}, bf16[192,768]{1,0:T(8,128)(2,1)S(1)}, u32[]{:S(2)}) copy-start(bf16[192,768]{1,0:T(8,128)(2,1)S(1)} %collective-permute-done.35.p2) | copy-start | bytes 884740
  261.3 7.0 %collective-permute-start.36 = (bf16[192,768]{1,0:T(8,128)(2,1)S(1)}, bf16[192,768]{1,0:T(8,128)(2,1)S(1)}, u32[]{:S(2)}, u32[]{:S(2)}) collective-permute-start(bf16[192,768]{1,0:T(8,128)(2,1)S(1)} %collective-permute-done.35.p2), channel_id=1, source_target_pairs={{0,1},{1,0},{2,3},{3,2},{4,5},{5,4},{6,7},{7,6},{8,9},{9,8},{10,11... | collective-permute-start | bytes 884744 | tf_op jit(solution)/shard_map/ppermute | solution.py:575
  261.6 6.7 %copy-start.10 = (bf16[2,5,48,384]{3,2,1,0:T(8,128)(2,1)}, bf16[2,5,48,384]{3,2,1,0:T(8,128)(2,1)S(1)}, u32[]{:S(2)}) copy-start(bf16[2,5,48,384]{3,2,1,0:T(8,128)(2,1)S(1)} %pad_maximum_fusion.2.own) | copy-start | bytes 1105924
  261.6 11.2 %collective-permute-start.33 = (bf16[2,5,48,384]{3,2,1,0:T(8,128)(2,1)S(1)}, bf16[2,5,48,384]{3,2,1,0:T(8,128)(2,1)S(1)}, u32[]{:S(2)}, u32[]{:S(2)}) collective-permute-start(bf16[2,5,48,384]{3,2,1,0:T(8,128)(2,1)S(1)} %pad_maximum_fusion.2.own), channel_id=1, source_target_pairs={{0,1},{1,0},{2,3},{3,2},{4,5},{5,4},{6,7},{7,6},{8,9},{9,8},{10,11... | collective-permute-start | bytes 1105928 | tf_op jit(solution)/shard_map/ppermute | solution.py:575
  (19 other events, 18.4 us)
Sparse Core Ops, SparseCore 0:
  56.4 65.1 all-gather.2
  168.9 71.9 reduce-scatter.1

commit v2 on v1

--- a/solution.py
+++ b/solution.py
@@ -102,6 +102,10 @@
     slots, _, rows, _ = tok.shape
     span = slots * rows
     blocks = mod_rows // seqs
+    count = wq.shape[0] // 4
+    quarter = wq[:count, :]
+    for own in range(1, 4):
+        quarter = jnp.where(s == own, wq[own * count : (own + 1) * count, :], quarter)
     first = dot(cond[...], w_ada[:, : 2 * width]) + bias[:, : 2 * width]
     at = pl.multiple_of((2 + s) * width, 128)
     rest = (dot(cond[...], w_ada[:, pl.ds(at, width)]) + bias[:, pl.ds(at, width)]).astype(BF)
@@ -116,7 +120,7 @@
         send[i, span + 2 * blocks : span + 2 * blocks + mod_rows, :] = rest
         send[i, span + 2 * blocks + mod_rows :, :] = jnp.concatenate(
             [
-                wq[:, t * width + hg * GROUP : t * width + (hg + 1) * GROUP]
+                quarter[:, t * width + hg * GROUP : t * width + (hg + 1) * GROUP]
                 for t in (0, 1, 2, 2)
             ],
             axis=1,
@@ -203,8 +207,8 @@
             acc[h] += dot_tn(kv[m, :, GROUP + h * HD : GROUP + (h + 1) * HD], p.astype(BF))
         return 0
 
-    lax.fori_loop(0, 4, one, 0)
-    lax.fori_loop(0, 4, two, 0)
+    lax.fori_loop(0, 4, one, 0, unroll=2)
+    lax.fori_loop(0, 4, two, 0, unroll=2)
     for h in range(HEADS):
         o = (acc[h] / low[h]).T
         o_full[:, h * HD : (h + 1) * HD] = o
@@ -434,7 +438,7 @@
             acc[h] += dot_tn(k, g)
         return 0
 
-    lax.fori_loop(0, 4, piece, 0)
+    lax.fori_loop(0, 4, piece, 0, unroll=2)
     for h in range(HEADS):
         dq_out[:, h * HD : (h + 1) * HD] = acc[h].T * (1.0 / math.sqrt(HD))
     for m in range(4):
@@ -579,8 +583,10 @@
     return lax.optimization_barrier((x,) + others)[0]
 
 
-def gather_sp(x):
+def gather_sp(x, ready=None):
     far = swap(x, "sp", 2, 4)
+    if ready is not None:
+        far = after(far, ready)
     return [x, swap(x, "sp", 1, 4), far, swap(far, "sp", 1, 4)]
 
 
@@ -667,7 +673,7 @@
 
     if fast:
         quarter_rows = part_rows // 4
-        wq = lax.dynamic_slice(w_qkv, (quarter_rows * s, 0), (quarter_rows, 3 * width))
+        wq = w_qkv
         extra = 2 * blocks + mod_rows + quarter_rows
     else:
         wq = w_qkv
@@ -746,11 +752,11 @@
             kv, "cp", axis=0, tiled=True,
             axis_index_groups=[[8 * g + i for g in range(groups)] for i in range(8)],
         )
-    kvs = gather_sp(kv)
+    key_col = key_ids[:, :, None]
+    kvs = gather_sp(kv, key_col)
     if fast:
         kvs[0] = after(kvs[0], w_proj)
         w_proj = jnp.stack([w_proj, swap(w_proj, "sp", 1, 4)])
-    key_col = key_ids[:, :, None]
     query_row = query_ids[None, :]
     part = kv.shape[0]
     wide_kv = ((4, part, 2 * GROUP), BF)

time: 284 us -> 282 us (level)
    unnamed x83 -> x87, local copies, waits for them, and re-layouts: 8.04 us -> 9.29 us
where the time goes in v2:
time: 282 us; the launch traced here: 281 us
  waiting for transfers between devices  81.2 us (29%)
  Pallas kernels  74.3 us (26%)
  starting transfers between devices  64.7 us (23%)
  local copies, waits for them, and re-layouts  22 us (8%)
  between operations  14.7 us (5%)
  blocking collectives  12 us (4%)
  other arithmetic  9.01 us (3%)
  matrix products  3.11 us (1%)
    pallas_call x16, Pallas kernels, call(): pl.pallas_call(kernel, out_shape=[jax.ShapeDtypeStruct(shape, kind) for s...  74.3 us
    ppermute x37, waiting for transfers between devices, swap(): return lax.ppermute(x, axis, [(i, i ^ k) for i in range(size)])  51.5 us
    ppermute x37, starting transfers between devices, swap(): return lax.ppermute(x, axis, [(i, i ^ k) for i in range(size)])  45.6 us
    all_to_all x4, waiting for transfers between devices, all_to_all(): lax.all_to_all(x, 'cp', split_axis=0, concat_axis=0, tiled=True, axis_ind...  29.7 us
    all_to_all x4, starting transfers between devices, all_to_all(): lax.all_to_all(x, 'cp', split_axis=0, concat_axis=0, tiled=True, axis_ind...  18.8 us
    all_to_all x1, blocking collectives, all_to_all(): lax.all_to_all(x, 'cp', split_axis=0, concat_axis=0, tiled=True, axis_ind...  12 us
    unnamed x87, local copies, waits for them, and re-layouts  9.29 us
  transfers between devices with their start and end apart: 43, of which 17 were waited for; matrix products, arithmetic and copies ran while one was open for 7% of the time, Pallas kernels for 19%

profile of v2, /device:TPU:1, one launch (start us, length us, event | category | flops | bytes accessed | tf_op | source)
XLA Modules:
  0.0 281.1 jit_solution(6575913534545201901)
XLA Ops:
  10.9 3.3 %pack.1 = (bf16[8,120,768]{2,1,0:T(8,128)(2,1)}, bf16[192,768]{1,0:T(8,128)(2,1)}) custom-call(s32[3]{0:T(128)} %pad_add_fusion.1.sc.refs_0_, bf16[2,2,32,768]{3,2,1,0:T(8,128)(2,1)} %tok.5, bf16[16,96]{1,0:T(8,128)(2,1)} %multiply_convert_fusion.cond, bf16[96,4608]{1,0:T(8,128)(2,1)} %w_ada.1, f32[1,4608]{1,0:T(1,128)} %copy-done.36, bf16[96,2304]{1,0:T(8,128)(2,1)} %wq.1, ...), custom_call_target="tpu_custom_call" | custom-call | tf_op jit(solution)/shard_map/pack/pallas_call | solution.py:23
  14.2 6.7 %all-to-all-start = ((bf16[8,120,768]{2,1,0:T(8,128)(2,1)}), bf16[8,120,768]{2,1,0:T(8,128)(2,1)S(1)}, u32[]{:S(2)}, u32[]{:S(2)}) async-start(bf16[8,120,768]{2,1,0:T(8,128)(2,1)} %get-tuple-element.73), calls=%async_computation | async-start | bytes 2949120 | tf_op jit(solution)/shard_map/all_to_all | solution.py:619
  20.9 1.2 collective-permute-start.1
  22.1 1.3 collective-permute-start
  23.4 3.1 %collective-permute-done.1.g2 = bf16[2,2,32,768]{3,2,1,0:T(8,128)(2,1)S(1)} collective-permute-done((bf16[2,2,32,768]{3,2,1,0:T(8,128)(2,1)S(1)}, bf16[2,2,32,768]{3,2,1,0:T(8,128)(2,1)S(1)}, u32[]{:S(2)}, u32[]{:S(2)}) %collective-permute-start.1) | collective-permute-done | bytes 196640 | tf_op jit(solution)/shard_map/ppermute | solution.py:579
  26.5 1.8 collective-permute-start.2
  29.5 25.4 %all-to-all-done.refs_1_.refs_2_ = bf16[8,120,768]{2,1,0:T(8,128)(2,1)S(1)} async-done(((bf16[8,120,768]{2,1,0:T(8,128)(2,1)}), bf16[8,120,768]{2,1,0:T(8,128)(2,1)S(1)}, u32[]{:S(2)}, u32[]{:S(2)}) %all-to-all-start) | async-done | bytes 1474592 | tf_op jit(solution)/shard_map/all_to_all | solution.py:619
  55.4 1.1 collective-permute-start.4
  57.4 4.7 %all-to-all-start.1 = ((bf16[8,48,768]{2,1,0:T(8,128)(2,1)}), bf16[8,48,768]{2,1,0:T(8,128)(2,1)S(1)}, u32[]{:S(2)}, u32[]{:S(2)}) async-start(bf16[8,48,768]{2,1,0:T(8,128)(2,1)} %broadcast_in_dim.56), calls=%async_computation.1 | async-start | bytes 1179648 | tf_op jit(solution)/shard_map/all_to_all | solution.py:619
  65.4 1.8 fusion.5
  68.1 5.3 %qkv.1 = (bf16[512,192]{1,0:T(8,128)(2,1)}, bf16[512,384]{1,0:T(8,128)(2,1)}, bf16[512,768]{1,0:T(8,128)(2,1)}, bf16[512,768]{1,0:T(8,128)(2,1)}, bf16[768,576]{1,0:T(8,128)(2,1)}, /*index=5*/bf16[16,768]{1,0:T(8,128)(2,1)}) custom-call(s32[3]{0:T(128)} %pad_add_fusion.1.sc.refs_0_, bf16[8,120,768]{2,1,0:T(8,128)(2,1)} %copy-done.1, ...), custom_call_target="tpu_custom_call" | custom-call | tf_op jit(solution)/shard_map/qkv/pallas_call | solution.py:23
  73.4 1.1 collective-permute-start.7
  75.2 9.3 %collective-permute-done.7.kv2 = bf16[512,384]{1,0:T(8,128)(2,1)S(1)} collective-permute-done((bf16[512,384]{1,0:T(8,128)(2,1)}, bf16[512,384]{1,0:T(8,128)(2,1)S(1)}, u32[]{:S(2)}, u32[]{:S(2)}) %collective-permute-start.7) | collective-permute-done | bytes 393248 | tf_op jit(solution)/shard_map/ppermute | solution.py:579
  85.2 3.3 %collective-permute-start.9 = (bf16[8,48,768]{2,1,0:T(8,128)(2,1)S(1)}, bf16[8,48,768]{2,1,0:T(8,128)(2,1)S(1)}, u32[]{:S(2)}, u32[]{:S(2)}) collective-permute-start(bf16[8,48,768]{2,1,0:T(8,128)(2,1)S(1)} %all-to-all-done.1), channel_id=1, source_target_pairs={{0,1},{1,0},{2,3},{3,2},{4,5},{5,4},{6,7},{7,6},{8,9},{9,8},{10,11... | collective-permute-start | bytes 1769480 | tf_op jit(solution)/shard_map/ppermute | solution.py:579
  88.4 1.3 copy.35.kid
  92.0 7.9 %attend.1 = (bf16[512,192]{1,0:T(8,128)(2,1)}, f32[512,192]{1,0:T(8,128)}, f32[8,512]{1,0:T(8,128)}) custom-call(s32[3]{0:T(128)} %pad_add_fusion.1.sc.refs_0_, bf16[512,192]{1,0:T(8,128)(2,1)} %get-tuple-element.75.q, bf16[512,384]{1,0:T(8,128)(2,1)} %get-tuple-element.78.kv0, bf16[512,384]{1,0:T(8,128)(2,1)} %copy-done.8, bf16[512,384]{1,0:T(8,128)(2,1)} %copy-done.7, ...), custom_call_target="tpu_custom_call" | custom-call | tf_op jit(solution)/shard_map/attend/pallas_call | solution.py:23
  99.9 3.7 %all-to-all-start.2 = ((bf16[8,64,192]{2,1,0:T(8,128)(2,1)}), bf16[8,64,192]{2,1,0:T(8,128)(2,1)S(1)}, u32[]{:S(2)}, u32[]{:S(2)}) async-start(bf16[8,64,192]{2,1,0:T(8,128)(2,1)} %bitcast.108), calls=%async_computation.2 | async-start | bytes 524288 | tf_op jit(solution)/shard_map/all_to_all | solution.py:619
  104.7 1.3 slice.77.rest2
  106.0 1.3 slice.76.rest1
  107.3 1.4 slice.78.rest3
  108.7 3.2 %expand.1 = (f32[4,128,768]{2,1,0:T(8,128)}, bf16[512,768]{1,0:T(8,128)(2,1)}) custom-call(s32[3]{0:T(128)} %pad_add_fusion.1.sc.refs_0_, bf16[16,768]{1,0:T(8,128)(2,1)} %copy-done.26, bf16[16,768]{1,0:T(8,128)(2,1)} %slice.76.rest1, bf16[16,768]{1,0:T(8,128)(2,1)} %slice.77.rest2, bf16[16,768]{1,0:T(8,128)(2,1)} %slice.78.rest3, s32[512,1]{1,0:T(8,128)} %copy.40.ids, ...), custom_call_target="tpu_custom_call" | custom-call | tf_op jit(solution)/shard_map/expand/pallas_call | solution.py:23
  111.9 1.1 pad_maximum_fusion.weights
  113.0 4.3 %all-to-all-done.2.attn = bf16[8,64,192]{2,1,0:T(8,128)(2,1)S(1)} async-done(((bf16[8,64,192]{2,1,0:T(8,128)(2,1)}), bf16[8,64,192]{2,1,0:T(8,128)(2,1)S(1)}, u32[]{:S(2)}, u32[]{:S(2)}) %all-to-all-start.2) | async-done | bytes 196640 | tf_op jit(solution)/shard_map/all_to_all | solution.py:619
  118.0 3.5 %project.1 = (f32[128,768]{1,0:T(8,128)}, f32[128,768]{1,0:T(8,128)}, f32[128,768]{1,0:T(8,128)}, f32[128,1]{1,0:T(8,128)}, bf16[128,768]{1,0:T(8,128)(2,1)}, /*index=5*/bf16[768,768]{1,0:T(8,128)(2,1)}) custom-call(s32[3]{0:T(128)} %pad_add_fusion.1.sc.refs_0_, bf16[8,64,192]{2,1,0:T(8,128)(2,1)} %copy-done.3, bf16[2,2,32,768]{3,2,1,0:T(8,128)(2,1)} %tok.5, ...), custom_call_target="tpu_custom_call" | custom-call | tf_op jit(solution)/shard_map/project/pallas_call | solution.py:23
  121.5 2.0 collective-permute-start.10
  123.5 2.7 collective-permute-done.11.h2
  126.3 3.0 %collective-permute-start.12 = (bf16[128,768]{1,0:T(8,128)(2,1)S(1)}, bf16[128,768]{1,0:T(8,128)(2,1)S(1)}, u32[]{:S(2)}, u32[]{:S(2)}) collective-permute-start(bf16[128,768]{1,0:T(8,128)(2,1)S(1)} %collective-permute-done.11.h2), channel_id=1, source_target_pairs={{0,1},{1,0},{2,3},{3,2},{4,5},{5,4},{6,7},{7,6},{8,9},{9,8},{10,11... | collective-permute-start | bytes 589832 | tf_op jit(solution)/shard_map/ppermute | solution.py:579
  129.2 1.1 collective-permute-done.12.h3
  130.9 6.1 %feed.1 = (bf16[2,128,768]{2,1,0:T(8,128)(2,1)}, bf16[2,128,768]{2,1,0:T(8,128)(2,1)}, bf16[2,128,768]{2,1,0:T(8,128)(2,1)}, bf16[2,128,768]{2,1,0:T(8,128)(2,1)...) custom-call(s32[3]{0:T(128)} %pad_add_fusion.1.sc.refs_0_, ...), custom_call_target="tpu_custom_call" | custom-call | tf_op jit(solution)/shard_map/feed/pallas_call | solution.py:23
  137.4 1.6 collective-permute-done.13.dh_recv
  138.9 1.1 fusion.6
  140.1 6.1 %collective-permute-done.15.dh_far = bf16[128,768]{1,0:T(8,128)(2,1)S(1)} collective-permute-done((bf16[128,768]{1,0:T(8,128)(2,1)S(1)}, bf16[128,768]{1,0:T(8,128)(2,1)S(1)}, u32[]{:S(2)}, u32[]{:S(2)}) %collective-permute-start.15) | collective-permute-done | bytes 196640 | tf_op jit(solution)/shard_map/ppermute | solution.py:579
  146.9 3.7 %middle.1 = (f32[128,768]{1,0:T(8,128)}, f32[128,768]{1,0:T(8,128)}, bf16[128,768]{1,0:T(8,128)(2,1)}, bf16[8,64,192]{2,1,0:T(8,128)(2,1)}) custom-call(s32[3]{0:T(128)} %pad_add_fusion.1.sc.refs_0_, bf16[2,128,768]{2,1,0:T(8,128)(2,1)} %get-tuple-element.89.dh_keep, bf16[2,128,768]{2,1,0:T(8,128)(2,1)} %copy-done.12, bf16[128,768]{1,0:T(8,128)(2,1)} %copy-done.30, ...), custom_call_target="tpu_custom_call" | custom-call | tf_op jit(solution)/shard_map/middle/pallas_call | solution.py:23
  150.6 12.0 %all_to_all.25 = bf16[8,64,192]{2,1,0:T(8,128)(2,1)} all-to-all(bf16[8,64,192]{2,1,0:T(8,128)(2,1)} %get-tuple-element.97), channel_id=1, replica_groups=mesh['cp'=8,'sp'=4] {'cp'}, dimensions={0} | all-to-all | bytes 393216 | tf_op jit(solution)/shard_map/all_to_all | solution.py:619
  162.7 4.7 %feed_grad.1 = bf16[8,192,768]{2,1,0:T(8,128)(2,1)} custom-call(s32[3]{0:T(128)} %pad_add_fusion.1.sc.refs_0_, bf16[512,768]{1,0:T(8,128)(2,1)} %get-tuple-element.98.h, bf16[512,768]{1,0:T(8,128)(2,1)} %get-tuple-element.84.dz_in.dz, bf16[512,768]{1,0:T(8,128)(2,1)} %get-tuple-element.100.act, bf16[512,768]{1,0:T(8,128)(2,1)} %get-tuple-element.101.du), custom_call_target="tpu_custom_call" | custom-call | tf_op jit(solution)/shard_map/feed_grad/pallas_call | solution.py:23
  167.3 13.7 %attend_back.1 = (f32[512,192]{1,0:T(8,128)}, bf16[2,512,384]{2,1,0:T(8,128)(2,1)}, bf16[2,512,384]{2,1,0:T(8,128)(2,1)}) custom-call(s32[3]{0:T(128)} %pad_add_fusion.1.sc.refs_0_, bf16[512,192]{1,0:T(8,128)(2,1)} %get-tuple-element.75.q, bf16[512,384]{1,0:T(8,128)(2,1)} %get-tuple-element.78.kv0, bf16[512,384]{1,0:T(8,128)(2,1)} %copy-done.8, ...), custom_call_target="tpu_custom_call" | custom-call | tf_op jit(solution)/shard_map/attend_back/pallas_call | solution.py:23
  181.1 2.8 %collective-permute-start.16 = (bf16[2,512,384]{2,1,0:T(8,128)(2,1)}, bf16[2,512,384]{2,1,0:T(8,128)(2,1)S(1)}, u32[]{:S(2)}, u32[]{:S(2)}) collective-permute-start(bf16[2,512,384]{2,1,0:T(8,128)(2,1)} %get-tuple-element.105), channel_id=1, source_target_pairs={{0,1},{1,0},{2,3},{3,2},{4,5},{5,4},{6,7},{7,6},{8,9},{9,8},{10,11... | collective-permute-start | bytes 2359304 | tf_op jit(solution)/shard_map/ppermute | solution.py:579
  184.6 3.3 %middle_grad.1 = (f32[3,16,768]{2,1,0:T(8,128)}, bf16[8,48,768]{2,1,0:T(8,128)(2,1)}, bf16[8,48,768]{2,1,0:T(8,128)(2,1)}) custom-call(s32[3]{0:T(128)} %pad_add_fusion.1.sc.refs_0_, f32[128,768]{1,0:T(8,128)} %get-tuple-element.113.dx, f32[128,768]{1,0:T(8,128)} %get-tuple-element.119.dh, bf16[128,768]{1,0:T(8,128)(2,1)} %get-tuple-element.120.dy, ...), custom_call_target="tpu_custom_call" | custom-call | tf_op jit(solution)/shard_map/middle_grad/pallas_call | solution.py:23
  190.3 1.1 collective-permute-start.26
  191.4 7.8 %collective-permute-done.17.dkv_c = bf16[512,384]{1,0:T(8,128)(2,1)S(1)} collective-permute-done((bf16[512,384]{1,0:T(8,128)(2,1)}, bf16[512,384]{1,0:T(8,128)(2,1)S(1)}, u32[]{:S(2)}, u32[]{:S(2)}) %collective-permute-start.17) | collective-permute-done | bytes 393248 | tf_op jit(solution)/shard_map/ppermute | solution.py:579
  199.9 5.0 %qkv_back.1 = (bf16[8,64,768]{2,1,0:T(8,128)(2,1)}, bf16[512,768]{1,0:T(8,128)(2,1)}, bf16[512,576]{1,0:T(8,128)(2,1)}) custom-call(s32[3]{0:T(128)} %pad_add_fusion.1.sc.refs_0_, f32[512,192]{1,0:T(8,128)} %get-tuple-element.103.dq, bf16[2,512,384]{2,1,0:T(8,128)(2,1)} %get-tuple-element.104.dkv_a, bf16[2,512,384]{2,1,0:T(8,128)(2,1)} %copy-done.6, ...), custom_call_target="tpu_custom_call" | custom-call | tf_op jit(solution)/shard_map/qkv_back/pallas_call | solution.py:23
  205.7 3.8 %all-to-all-start.4 = ((bf16[8,64,768]{2,1,0:T(8,128)(2,1)}), bf16[8,64,768]{2,1,0:T(8,128)(2,1)S(1)}, u32[]{:S(2)}, u32[]{:S(2)}) async-start(bf16[8,64,768]{2,1,0:T(8,128)(2,1)} %get-tuple-element.108), calls=%async_computation.4 | async-start | bytes 1572864 | tf_op jit(solution)/shard_map/all_to_all | solution.py:619
  209.5 4.1 %qkv_grad.1 = (f32[2,16,768]{2,1,0:T(8,128)}, bf16[8,48,768]{2,1,0:T(8,128)(2,1)}, bf16[8,48,768]{2,1,0:T(8,128)(2,1)}) custom-call(s32[3]{0:T(128)} %pad_add_fusion.1.sc.refs_0_, bf16[512,576]{1,0:T(8,128)(2,1)} %get-tuple-element.114.d, bf16[512,768]{1,0:T(8,128)(2,1)} %get-tuple-element.115.dh, bf16[512,768]{1,0:T(8,128)(2,1)} %get-tuple-element.116.h, ...), custom_call_target="tpu_custom_call" | custom-call | tf_op jit(solution)/shard_map/qkv_grad/pallas_call | solution.py:23
  214.4 1.4 collective-permute-start.24
  216.5 2.7 block.1
  220.4 1.2 collective-permute-done.19
  221.6 1.2 collective-permute-start.20
  223.5 3.5 %collective-permute-done.20 = bf16[6,16,768]{2,1,0:T(8,128)(2,1)S(1)} collective-permute-done((bf16[6,16,768]{2,1,0:T(8,128)(2,1)S(1)}, bf16[6,16,768]{2,1,0:T(8,128)(2,1)S(1)}, u32[]{:S(2)}, u32[]{:S(2)}) %collective-permute-start.20) | collective-permute-done | bytes 147488 | tf_op jit(solution)/shard_map/ppermute | solution.py:579
  227.0 1.6 collective-permute-start.21
  228.6 3.1 %collective-permute-done.21 = bf16[6,16,768]{2,1,0:T(8,128)(2,1)S(1)} collective-permute-done((bf16[6,16,768]{2,1,0:T(8,128)(2,1)S(1)}, bf16[6,16,768]{2,1,0:T(8,128)(2,1)S(1)}, u32[]{:S(2)}, u32[]{:S(2)}) %collective-permute-start.21) | collective-permute-done | bytes 147488 | tf_op jit(solution)/shard_map/ppermute | solution.py:579
  231.8 4.8 %collective-permute-done.27 = bf16[12,48,384]{2,1,0:T(8,128)(2,1)S(1)} collective-permute-done((bf16[12,48,384]{2,1,0:T(8,128)(2,1)S(1)}, bf16[12,48,384]{2,1,0:T(8,128)(2,1)S(1)}, u32[]{:S(2)}, u32[]{:S(2)}) %collective-permute-start.27) | collective-permute-done | bytes 442400 | tf_op jit(solution)/shard_map/ppermute | solution.py:579
  236.7 1.5 collective-permute-start.22
  238.2 2.5 last.1
  240.8 1.3 collective-permute-start.28
  242.1 2.1 collective-permute-start.23
  244.1 1.3 collective-permute-start.35
  246.4 2.1 collective-permute-start.30
  249.3 6.0 %collective-permute-done.30 = bf16[2,48,384]{2,1,0:T(8,128)(2,1)S(1)} collective-permute-done((bf16[2,48,384]{2,1,0:T(8,128)(2,1)S(1)}, bf16[2,48,384]{2,1,0:T(8,128)(2,1)S(1)}, u32[]{:S(2)}, u32[]{:S(2)}) %collective-permute-start.30) | collective-permute-done | bytes 73760 | tf_op jit(solution)/shard_map/ppermute | solution.py:579
  255.4 1.2 collective-permute-start.32
  256.7 2.9 %collective-permute-start.34 = (bf16[192,768]{1,0:T(8,128)(2,1)S(1)}, bf16[192,768]{1,0:T(8,128)(2,1)S(1)}, u32[]{:S(2)}, u32[]{:S(2)}) collective-permute-start(bf16[192,768]{1,0:T(8,128)(2,1)S(1)} %bitcast.106), channel_id=1, source_target_pairs={{0,1},{1,0},{2,3},{3,2},{4,5},{5,4},{6,7},{7,6},{8,9},{9,8},{10,11... | collective-permute-start | bytes 884744 | tf_op jit(solution)/shard_map/ppermute | solution.py:579
  259.9 3.7 %collective-permute-start.33 = (bf16[2,5,48,384]{3,2,1,0:T(8,128)(2,1)S(1)}, bf16[2,5,48,384]{3,2,1,0:T(8,128)(2,1)S(1)}, u32[]{:S(2)}, u32[]{:S(2)}) collective-permute-start(bf16[2,5,48,384]{3,2,1,0:T(8,128)(2,1)S(1)} %pad_maximum_fusion.2.own), channel_id=1, source_target_pairs={{0,1},{1,0},{2,3},{3,2},{4,5},{5,4},{6,7},{7,6},{8,9},{9,8},{10,11... | collective-permute-start | bytes 1105928 | tf_op jit(solution)/shard_map/ppermute | solution.py:579
  264.5 2.1 fusion.25
  268.1 3.1 %finish.1 = (f32[96,3072]{1,0:T(8,128)}, f32[384,768]{1,0:T(8,128)}) custom-call(s32[3]{0:T(128)} %pad_add_fusion.1.sc.refs_0_, bf16[192,768]{1,0:T(8,128)(2,1)} %bitcast.104, bf16[192,768]{1,0:T(8,128)(2,1)} %copy-done.24, bf16[192,768]{1,0:T(8,128)(2,1)} %copy-done.23, bf16[192,768]{1,0:T(8,128)(2,1)} %copy-done.25), custom_call_target="tpu_custom_call" | custom-call | tf_op jit(solution)/shard_map/finish/pallas_call | solution.py:23
  271.9 2.4 finish_qkv.1
  (208 shorter events, 30.7 us)
Async XLA Ops:
  14.2 6.7 %copy-start.4 = (bf16[2,2,32,768]{3,2,1,0:T(8,128)(2,1)S(1)}, bf16[2,2,32,768]{3,2,1,0:T(8,128)(2,1)}, u32[]{:S(2)}) copy-start(bf16[2,2,32,768]{3,2,1,0:T(8,128)(2,1)} %grad.3) | copy-start | bytes 589828
  14.2 40.8 %copy-start.38 = (bf16[96,768]{1,0:T(8,128)(2,1)S(1)}, bf16[96,768]{1,0:T(8,128)(2,1)}, u32[]{:S(2)}) copy-start(bf16[96,768]{1,0:T(8,128)(2,1)} %param.21) | copy-start | bytes 442372
  14.2 40.8 %copy-start.41 = (s32[16]{0:T(128)S(1)}, s32[16]{0:T(128)}, u32[]{:S(2)}) copy-start(s32[16]{0:T(128)} %param.16) | copy-start | bytes 196
  14.2 40.9 %copy-start.40 = (s32[2,2048]{1,0:T(2,128)S(1)}, s32[2,2048]{1,0:T(2,128)}, u32[]{:S(2)}) copy-start(s32[2,2048]{1,0:T(2,128)} %param.17) | copy-start | bytes 49156
  14.2 40.7 %all-to-all-start = ((bf16[8,120,768]{2,1,0:T(8,128)(2,1)}), bf16[8,120,768]{2,1,0:T(8,128)(2,1)S(1)}, u32[]{:S(2)}, u32[]{:S(2)}) async-start(bf16[8,120,768]{2,1,0:T(8,128)(2,1)} %get-tuple-element.73), calls=%async_computation | async-start | bytes 2949120 | tf_op jit(solution)/shard_map/all_to_all | solution.py:619
  20.9 109.4 %all-gather.3.cloned.1.call-start = ((), (), s32[]{:S(2)}) async-start(), calls=%async_computation.7 | async-start | bytes 2654208 | tf_op jit(solution)/shard_map/all_gather | solution.py:720
  20.9 5.6 %collective-permute-start.1 = (bf16[2,2,32,768]{3,2,1,0:T(8,128)(2,1)S(1)}, bf16[2,2,32,768]{3,2,1,0:T(8,128)(2,1)S(1)}, u32[]{:S(2)}, u32[]{:S(2)}) collective-permute-start(bf16[2,2,32,768]{3,2,1,0:T(8,128)(2,1)S(1)} %copy-done.4), channel_id=1, source_target_pairs={{0,2},{1,3},{2,0},{3,1},{4,6},{5,7},{6,4},{7,5},{8,10},{9,11},{10,... | collective-permute-start | bytes 589832 | tf_op jit(solution)/shard_map/ppermute | solution.py:579
  22.1 6.2 %collective-permute-start = (bf16[2,2,32,768]{3,2,1,0:T(8,128)(2,1)S(1)}, bf16[2,2,32,768]{3,2,1,0:T(8,128)(2,1)S(1)}, u32[]{:S(2)}, u32[]{:S(2)}) collective-permute-start(bf16[2,2,32,768]{3,2,1,0:T(8,128)(2,1)S(1)} %copy-done.4), channel_id=1, source_target_pairs={{0,1},{1,0},{2,3},{3,2},{4,5},{5,4},{6,7},{7,6},{8,9},{9,8},{10,11... | collective-permute-start | bytes 589832 | tf_op jit(solution)/shard_map/ppermute | solution.py:579
  26.5 3.0 %collective-permute-start.2 = (bf16[2,2,32,768]{3,2,1,0:T(8,128)(2,1)S(1)}, bf16[2,2,32,768]{3,2,1,0:T(8,128)(2,1)}, u32[]{:S(2)}, u32[]{:S(2)}) collective-permute-start(bf16[2,2,32,768]{3,2,1,0:T(8,128)(2,1)S(1)} %collective-permute-done.1.g2), channel_id=1, source_target_pairs={{0,1},{1,0},{2,3},{3,2},{4,5},{5,4},{6,7},{7,6},{8,9},{9,8},{10,11... | collective-permute-start | bytes 589832 | tf_op jit(solution)/shard_map/ppermute | solution.py:579
  54.9 2.4 copy-start.1
  55.4 11.9 %copy-start.11 = (bf16[208,768]{1,0:T(8,128)(2,1)}, bf16[208,768]{1,0:T(8,128)(2,1)S(1)}, u32[]{:S(2)}) copy-start(bf16[208,768]{1,0:T(8,128)(2,1)S(1)} %pad_maximum_fusion.3.refs_6_) | copy-start | bytes 958468
  55.4 9.1 %collective-permute-start.4 = (bf16[208,768]{1,0:T(8,128)(2,1)S(1)}, bf16[208,768]{1,0:T(8,128)(2,1)S(1)}, u32[]{:S(2)}, u32[]{:S(2)}) collective-permute-start(bf16[208,768]{1,0:T(8,128)(2,1)S(1)} %pad_maximum_fusion.3.refs_6_), channel_id=1, source_target_pairs={{0,2},{1,3},{2,0},{3,1},{4,6},{5,7},{6,4},{7,5},{8,10},{9,11},{10,... | collective-permute-start | bytes 958472 | tf_op jit(solution)/shard_map/ppermute | solution.py:579
  57.4 27.8 %all-to-all-start.1 = ((bf16[8,48,768]{2,1,0:T(8,128)(2,1)}), bf16[8,48,768]{2,1,0:T(8,128)(2,1)S(1)}, u32[]{:S(2)}, u32[]{:S(2)}) async-start(bf16[8,48,768]{2,1,0:T(8,128)(2,1)} %broadcast_in_dim.56), calls=%async_computation.1 | async-start | bytes 1179648 | tf_op jit(solution)/shard_map/all_to_all | solution.py:619
  62.4 22.8 %copy-start.34 = (s32[2,16,4,32]{3,2,1,0:T(4,128)}, s32[2,16,4,32]{3,2,1,0:T(4,128)S(1)}, u32[]{:S(2)}) copy-start(s32[2,16,4,32]{3,2,1,0:T(4,128)S(1)} %reshape.173) | copy-start | bytes 49156
  63.4 3.8 %collective-permute-start.3 = (bf16[208,768]{1,0:T(8,128)(2,1)S(1)}, bf16[208,768]{1,0:T(8,128)(2,1)S(1)}, u32[]{:S(2)}, u32[]{:S(2)}) collective-permute-start(bf16[208,768]{1,0:T(8,128)(2,1)S(1)} %pad_maximum_fusion.3.refs_6_), channel_id=1, source_target_pairs={{0,1},{1,0},{2,3},{3,2},{4,5},{5,4},{6,7},{7,6},{8,9},{9,8},{10,11... | collective-permute-start | bytes 958472 | tf_op jit(solution)/shard_map/ppermute | solution.py:579
  64.4 2.8 %copy-start.18 = (bf16[208,768]{1,0:T(8,128)(2,1)}, bf16[208,768]{1,0:T(8,128)(2,1)S(1)}, u32[]{:S(2)}) copy-start(bf16[208,768]{1,0:T(8,128)(2,1)S(1)} %collective-permute-done.4.refs_8_) | copy-start | bytes 958468
  64.4 2.8 collective-permute-start.5
  73.4 11.1 %collective-permute-start.7 = (bf16[512,384]{1,0:T(8,128)(2,1)}, bf16[512,384]{1,0:T(8,128)(2,1)S(1)}, u32[]{:S(2)}, u32[]{:S(2)}) collective-permute-start(bf16[512,384]{1,0:T(8,128)(2,1)} %get-tuple-element.78.kv0), channel_id=1, source_target_pairs={{0,2},{1,3},{2,0},{3,1},{4,6},{5,7},{6,4},{7,5},{8,10},{9,11},{10,... | collective-permute-start | bytes 1179656 | tf_op jit(solution)/shard_map/ppermute | solution.py:579
  74.6 16.6 %copy-start.37 = (s32[1,512]{1,0:T(1,128)}, s32[1,512]{1,0:T(1,128)S(1)}, u32[]{:S(2)}) copy-start(s32[1,512]{1,0:T(1,128)S(1)} %stack_reshape.12.qid.ids_row) | copy-start | bytes 6148
  74.8 16.3 %collective-permute-start.6 = (bf16[512,384]{1,0:T(8,128)(2,1)}, bf16[512,384]{1,0:T(8,128)(2,1)S(1)}, u32[]{:S(2)}, u32[]{:S(2)}) collective-permute-start(bf16[512,384]{1,0:T(8,128)(2,1)} %get-tuple-element.78.kv0), channel_id=1, source_target_pairs={{0,1},{1,0},{2,3},{3,2},{4,5},{5,4},{6,7},{7,6},{8,9},{9,8},{10,11... | collective-permute-start | bytes 1179656 | tf_op jit(solution)/shard_map/ppermute | solution.py:579
  84.5 6.7 %copy-start.7 = (bf16[512,384]{1,0:T(8,128)(2,1)}, bf16[512,384]{1,0:T(8,128)(2,1)S(1)}, u32[]{:S(2)}) copy-start(bf16[512,384]{1,0:T(8,128)(2,1)S(1)} %collective-permute-done.7.kv2) | copy-start | bytes 1179652
  84.5 6.7 %collective-permute-start.8 = (bf16[512,384]{1,0:T(8,128)(2,1)S(1)}, bf16[512,384]{1,0:T(8,128)(2,1)S(1)}, u32[]{:S(2)}, u32[]{:S(2)}) collective-permute-start(bf16[512,384]{1,0:T(8,128)(2,1)S(1)} %collective-permute-done.7.kv2), channel_id=1, source_target_pairs={{0,1},{1,0},{2,3},{3,2},{4,5},{5,4},{6,7},{7,6},{8,9},{9,8},{10,11... | collective-permute-start | bytes 1179656 | tf_op jit(solution)/shard_map/ppermute | solution.py:579
  85.2 26.7 %collective-permute-start.9 = (bf16[8,48,768]{2,1,0:T(8,128)(2,1)S(1)}, bf16[8,48,768]{2,1,0:T(8,128)(2,1)S(1)}, u32[]{:S(2)}, u32[]{:S(2)}) collective-permute-start(bf16[8,48,768]{2,1,0:T(8,128)(2,1)S(1)} %all-to-all-done.1), channel_id=1, source_target_pairs={{0,1},{1,0},{2,3},{3,2},{4,5},{5,4},{6,7},{7,6},{8,9},{9,8},{10,11... | collective-permute-start | bytes 1769480 | tf_op jit(solution)/shard_map/ppermute | solution.py:579
  99.9 17.4 %all-to-all-start.2 = ((bf16[8,64,192]{2,1,0:T(8,128)(2,1)}), bf16[8,64,192]{2,1,0:T(8,128)(2,1)S(1)}, u32[]{:S(2)}, u32[]{:S(2)}) async-start(bf16[8,64,192]{2,1,0:T(8,128)(2,1)} %bitcast.108), calls=%async_computation.2 | async-start | bytes 524288 | tf_op jit(solution)/shard_map/all_to_all | solution.py:619
  103.5 137.1 %reduce-scatter.2.cloned.1.call-start = ((), (), s32[]{:S(2)}) async-start(), calls=%async_computation.6 | async-start | bytes 2654208 | tf_op jit(solution)/shard_map/reduce_scatter | solution.py:860
  121.5 4.7 %collective-permute-start.11 = (bf16[128,768]{1,0:T(8,128)(2,1)}, bf16[128,768]{1,0:T(8,128)(2,1)S(1)}, u32[]{:S(2)}, u32[]{:S(2)}) collective-permute-start(bf16[128,768]{1,0:T(8,128)(2,1)} %get-tuple-element.83.h0), channel_id=1, source_target_pairs={{0,2},{1,3},{2,0},{3,1},{4,6},{5,7},{6,4},{7,5},{8,10},{9,11},{10,... | collective-permute-start | bytes 589832 | tf_op jit(solution)/shard_map/ppermute | solution.py:579
  121.5 7.7 %collective-permute-start.10 = (bf16[128,768]{1,0:T(8,128)(2,1)}, bf16[128,768]{1,0:T(8,128)(2,1)S(1)}, u32[]{:S(2)}, u32[]{:S(2)}) collective-permute-start(bf16[128,768]{1,0:T(8,128)(2,1)} %get-tuple-element.83.h0), channel_id=1, source_target_pairs={{0,1},{1,0},{2,3},{3,2},{4,5},{5,4},{6,7},{7,6},{8,9},{9,8},{10,11... | collective-permute-start | bytes 589832 | tf_op jit(solution)/shard_map/ppermute | solution.py:579
  126.2 4.0 %copy-start.27 = (bf16[128,768]{1,0:T(8,128)(2,1)}, bf16[128,768]{1,0:T(8,128)(2,1)S(1)}, u32[]{:S(2)}) copy-start(bf16[128,768]{1,0:T(8,128)(2,1)S(1)} %collective-permute-done.11.h2) | copy-start | bytes 589828
  126.3 4.0 %collective-permute-start.12 = (bf16[128,768]{1,0:T(8,128)(2,1)S(1)}, bf16[128,768]{1,0:T(8,128)(2,1)S(1)}, u32[]{:S(2)}, u32[]{:S(2)}) collective-permute-start(bf16[128,768]{1,0:T(8,128)(2,1)S(1)} %collective-permute-done.11.h2), channel_id=1, source_target_pairs={{0,1},{1,0},{2,3},{3,2},{4,5},{5,4},{6,7},{7,6},{8,9},{9,8},{10,11... | collective-permute-start | bytes 589832 | tf_op jit(solution)/shard_map/ppermute | solution.py:579
  137.0 1.9 collective-permute-start.13
  138.9 7.3 %copy-start.12 = (bf16[2,128,768]{2,1,0:T(8,128)(2,1)}, bf16[2,128,768]{2,1,0:T(8,128)(2,1)S(1)}, u32[]{:S(2)}) copy-start(bf16[2,128,768]{2,1,0:T(8,128)(2,1)S(1)} %collective-permute-done.13.dh_recv) | copy-start | bytes 1179652
  140.1 6.2 %collective-permute-start.15 = (bf16[128,768]{1,0:T(8,128)(2,1)S(1)}, bf16[128,768]{1,0:T(8,128)(2,1)S(1)}, u32[]{:S(2)}, u32[]{:S(2)}) collective-permute-start(bf16[128,768]{1,0:T(8,128)(2,1)S(1)} %fusion.6), channel_id=1, source_target_pairs={{0,2},{1,3},{2,0},{3,1},{4,6},{5,7},{6,4},{7,5},{8,10},{9,11},{10,... | collective-permute-start | bytes 589832 | tf_op jit(solution)/shard_map/ppermute | solution.py:579
  181.1 6.9 %copy-start.5 = (bf16[2,512,384]{2,1,0:T(8,128)(2,1)S(1)}, bf16[2,512,384]{2,1,0:T(8,128)(2,1)}, u32[]{:S(2)}) copy-start(bf16[2,512,384]{2,1,0:T(8,128)(2,1)} %get-tuple-element.104.dkv_a) | copy-start | bytes 2359300
  181.1 6.8 %collective-permute-start.16 = (bf16[2,512,384]{2,1,0:T(8,128)(2,1)}, bf16[2,512,384]{2,1,0:T(8,128)(2,1)S(1)}, u32[]{:S(2)}, u32[]{:S(2)}) collective-permute-start(bf16[2,512,384]{2,1,0:T(8,128)(2,1)} %get-tuple-element.105), channel_id=1, source_target_pairs={{0,1},{1,0},{2,3},{3,2},{4,5},{5,4},{6,7},{7,6},{8,9},{9,8},{10,11... | collective-permute-start | bytes 2359304 | tf_op jit(solution)/shard_map/ppermute | solution.py:579
  187.9 2.2 collective-permute-start.25
  187.9 2.3 copy-start.6
  188.8 10.4 %collective-permute-start.17 = (bf16[512,384]{1,0:T(8,128)(2,1)}, bf16[512,384]{1,0:T(8,128)(2,1)S(1)}, u32[]{:S(2)}, u32[]{:S(2)}) collective-permute-start(bf16[512,384]{1,0:T(8,128)(2,1)} %fusion.2), channel_id=1, source_target_pairs={{0,2},{1,3},{2,0},{3,1},{4,6},{5,7},{6,4},{7,5},{8,10},{9,11},{10,... | collective-permute-start | bytes 1179656 | tf_op jit(solution)/shard_map/ppermute | solution.py:579
  188.8 16.1 %collective-permute-start.14 = (bf16[2,128,768]{2,1,0:T(8,128)(2,1)}, bf16[2,128,768]{2,1,0:T(8,128)(2,1)S(1)}, u32[]{:S(2)}, u32[]{:S(2)}) collective-permute-start(bf16[2,128,768]{2,1,0:T(8,128)(2,1)} %get-tuple-element.91), channel_id=1, source_target_pairs={{0,1},{1,0},{2,3},{3,2},{4,5},{5,4},{6,7},{7,6},{8,9},{9,8},{10,11... | collective-permute-start | bytes 1179656 | tf_op jit(solution)/shard_map/ppermute | solution.py:579
  190.3 24.1 %collective-permute-start.26 = (bf16[4,48,768]{2,1,0:T(8,128)(2,1)S(1)}, bf16[4,48,768]{2,1,0:T(8,128)(2,1)S(1)}, u32[]{:S(2)}, u32[]{:S(2)}) collective-permute-start(bf16[4,48,768]{2,1,0:T(8,128)(2,1)S(1)} %dynamic-slice_bitcast_fusion), channel_id=1, source_target_pairs={{0,4},{4,0},{8,12},{12,8},{16,20},{20,16},{24,28},{28,24},{1,5},{5... | collective-permute-start | bytes 884744 | tf_op jit(solution)/shard_map/ppermute | solution.py:579
  199.9 5.0 %copy-start.13 = (bf16[2,128,768]{2,1,0:T(8,128)(2,1)S(1)}, bf16[2,128,768]{2,1,0:T(8,128)(2,1)}, u32[]{:S(2)}) copy-start(bf16[2,128,768]{2,1,0:T(8,128)(2,1)} %get-tuple-element.87.z_keep) | copy-start | bytes 1179652
  199.9 5.2 %copy-start.35 = (f32[3,16,768]{2,1,0:T(8,128)S(1)}, f32[3,16,768]{2,1,0:T(8,128)}, u32[]{:S(2)}) copy-start(f32[3,16,768]{2,1,0:T(8,128)} %get-tuple-element.123) | copy-start | bytes 442372
  205.0 10.9 %collective-permute-start.18 = (bf16[128,768]{1,0:T(8,128)(2,1)S(1)}, bf16[128,768]{1,0:T(8,128)(2,1)S(1)}, u32[]{:S(2)}, u32[]{:S(2)}) collective-permute-start(bf16[128,768]{1,0:T(8,128)(2,1)S(1)} %fusion.7), channel_id=1, source_target_pairs={{0,2},{1,3},{2,0},{3,1},{4,6},{5,7},{6,4},{7,5},{8,10},{9,11},{10,... | collective-permute-start | bytes 589832 | tf_op jit(solution)/shard_map/ppermute | solution.py:579
  205.7 31.0 %all-to-all-start.4 = ((bf16[8,64,768]{2,1,0:T(8,128)(2,1)}), bf16[8,64,768]{2,1,0:T(8,128)(2,1)S(1)}, u32[]{:S(2)}, u32[]{:S(2)}) async-start(bf16[8,64,768]{2,1,0:T(8,128)(2,1)} %get-tuple-element.108), calls=%async_computation.4 | async-start | bytes 1572864 | tf_op jit(solution)/shard_map/all_to_all | solution.py:619
  214.4 8.4 %collective-permute-start.24 = (bf16[8,48,768]{2,1,0:T(8,128)(2,1)}, bf16[8,48,768]{2,1,0:T(8,128)(2,1)S(1)}, u32[]{:S(2)}, u32[]{:S(2)}) collective-permute-start(bf16[8,48,768]{2,1,0:T(8,128)(2,1)} %get-tuple-element.127), channel_id=1, source_target_pairs={{0,1},{1,0},{2,3},{3,2},{4,5},{5,4},{6,7},{7,6},{8,9},{9,8},{10,11... | collective-permute-start | bytes 1769480 | tf_op jit(solution)/shard_map/ppermute | solution.py:579
  219.3 3.6 %copy-start.15 = (bf16[8,48,768]{2,1,0:T(8,128)(2,1)S(1)}, bf16[8,48,768]{2,1,0:T(8,128)(2,1)}, u32[]{:S(2)}) copy-start(bf16[8,48,768]{2,1,0:T(8,128)(2,1)} %get-tuple-element.126) | copy-start | bytes 1769476
  220.1 1.4 collective-permute-start.19
  221.6 5.4 %collective-permute-start.20 = (bf16[6,16,768]{2,1,0:T(8,128)(2,1)S(1)}, bf16[6,16,768]{2,1,0:T(8,128)(2,1)S(1)}, u32[]{:S(2)}, u32[]{:S(2)}) collective-permute-start(bf16[6,16,768]{2,1,0:T(8,128)(2,1)S(1)} %add_convert_fusion.9), channel_id=1, source_target_pairs={{0,2},{1,3},{2,0},{3,1},{4,6},{5,7},{6,4},{7,5},{8,10},{9,11},{10,... | collective-permute-start | bytes 442376 | tf_op jit(solution)/shard_map/ppermute | solution.py:579
  223.1 13.4 %collective-permute-start.27 = (bf16[12,48,384]{2,1,0:T(8,128)(2,1)S(1)}, bf16[12,48,384]{2,1,0:T(8,128)(2,1)S(1)}, u32[]{:S(2)}, u32[]{:S(2)}) collective-permute-start(bf16[12,48,384]{2,1,0:T(8,128)(2,1)S(1)} %pad_maximum_fusion.1), channel_id=1, source_target_pairs={{0,2},{1,3},{2,0},{3,1},{4,6},{5,7},{6,4},{7,5},{8,10},{9,11},{10,... | collective-permute-start | bytes 1327112 | tf_op jit(solution)/shard_map/ppermute | solution.py:579
  227.0 4.7 %collective-permute-start.21 = (bf16[6,16,768]{2,1,0:T(8,128)(2,1)S(1)}, bf16[6,16,768]{2,1,0:T(8,128)(2,1)S(1)}, u32[]{:S(2)}, u32[]{:S(2)}) collective-permute-start(bf16[6,16,768]{2,1,0:T(8,128)(2,1)S(1)} %add_convert_fusion.8), channel_id=1, source_target_pairs={{0,4},{4,0},{8,12},{12,8},{16,20},{20,16},{24,28},{28,24},{1,5},{5... | collective-permute-start | bytes 442376 | tf_op jit(solution)/shard_map/ppermute | solution.py:579
  236.7 5.4 %collective-permute-start.22 = (bf16[6,16,768]{2,1,0:T(8,128)(2,1)S(1)}, bf16[6,16,768]{2,1,0:T(8,128)(2,1)S(1)}, u32[]{:S(2)}, u32[]{:S(2)}) collective-permute-start(bf16[6,16,768]{2,1,0:T(8,128)(2,1)S(1)} %convert_add_fusion.3), channel_id=1, source_target_pairs={{0,8},{4,12},{8,0},{12,4},{16,24},{20,28},{24,16},{28,20},{1,9},{5... | collective-permute-start | bytes 442376 | tf_op jit(solution)/shard_map/ppermute | solution.py:579
  240.7 3.5 %copy-start.22 = (bf16[1,192,768]{2,1,0:T(8,128)(2,1)S(1)}, bf16[1,192,768]{2,1,0:T(8,128)(2,1)}, u32[]{:S(2)}) copy-start(bf16[1,192,768]{2,1,0:T(8,128)(2,1)} %reduce-scatter.2.cloned.1.call-done) | copy-start | bytes 884740
  240.8 4.7 %collective-permute-start.28 = (bf16[4,48,384]{2,1,0:T(8,128)(2,1)S(1)}, bf16[4,48,384]{2,1,0:T(8,128)(2,1)S(1)}, u32[]{:S(2)}, u32[]{:S(2)}) collective-permute-start(bf16[4,48,384]{2,1,0:T(8,128)(2,1)S(1)} %dynamic-slice_bitcast_fusion.1), channel_id=1, source_target_pairs={{0,4},{4,0},{8,12},{12,8},{16,20},{20,16},{24,28},{28,24},{1,5},{5... | collective-permute-start | bytes 442376 | tf_op jit(solution)/shard_map/ppermute | solution.py:579
  242.1 14.6 %collective-permute-start.23 = (bf16[6,16,768]{2,1,0:T(8,128)(2,1)S(1)}, bf16[6,16,768]{2,1,0:T(8,128)(2,1)S(1)}, u32[]{:S(2)}, u32[]{:S(2)}) collective-permute-start(bf16[6,16,768]{2,1,0:T(8,128)(2,1)S(1)} %add_convert_fusion.7), channel_id=1, source_target_pairs={{0,16},{4,20},{8,24},{12,28},{16,0},{20,4},{24,8},{28,12},{1,17},{... | collective-permute-start | bytes 442376 | tf_op jit(solution)/shard_map/ppermute | solution.py:579
  244.1 15.5 %collective-permute-start.35 = (bf16[192,768]{1,0:T(8,128)(2,1)S(1)}, bf16[192,768]{1,0:T(8,128)(2,1)S(1)}, u32[]{:S(2)}, u32[]{:S(2)}) collective-permute-start(bf16[192,768]{1,0:T(8,128)(2,1)S(1)} %bitcast.105), channel_id=1, source_target_pairs={{0,2},{1,3},{2,0},{3,1},{4,6},{5,7},{6,4},{7,5},{8,10},{9,11},{10,... | collective-permute-start | bytes 884744 | tf_op jit(solution)/shard_map/ppermute | solution.py:579
  245.6 3.8 %collective-permute-start.29 = (bf16[2,48,384]{2,1,0:T(8,128)(2,1)S(1)}, bf16[2,48,384]{2,1,0:T(8,128)(2,1)S(1)}, u32[]{:S(2)}, u32[]{:S(2)}) collective-permute-start(bf16[2,48,384]{2,1,0:T(8,128)(2,1)S(1)} %pad_maximum_fusion.5), channel_id=1, source_target_pairs={{0,8},{4,12},{8,0},{12,4},{16,24},{20,28},{24,16},{28,20},{1,9},{5... | collective-permute-start | bytes 221192 | tf_op jit(solution)/shard_map/ppermute | solution.py:579
  246.4 8.9 %collective-permute-start.30 = (bf16[2,48,384]{2,1,0:T(8,128)(2,1)S(1)}, bf16[2,48,384]{2,1,0:T(8,128)(2,1)S(1)}, u32[]{:S(2)}, u32[]{:S(2)}) collective-permute-start(bf16[2,48,384]{2,1,0:T(8,128)(2,1)S(1)} %pad_maximum_fusion.6), channel_id=1, source_target_pairs={{0,16},{4,20},{8,24},{12,28},{16,0},{20,4},{24,8},{28,12},{1,17},{... | collective-permute-start | bytes 221192 | tf_op jit(solution)/shard_map/ppermute | solution.py:579
  248.5 6.9 %collective-permute-start.31 = (bf16[2,48,384]{2,1,0:T(8,128)(2,1)S(1)}, bf16[2,48,384]{2,1,0:T(8,128)(2,1)S(1)}, u32[]{:S(2)}, u32[]{:S(2)}) collective-permute-start(bf16[2,48,384]{2,1,0:T(8,128)(2,1)S(1)} %pad_maximum_fusion.7), channel_id=1, source_target_pairs={{0,24},{4,28},{8,16},{12,20},{16,8},{20,12},{24,0},{28,4},{1,25},{... | collective-permute-start | bytes 221192 | tf_op jit(solution)/shard_map/ppermute | solution.py:579
  255.4 9.1 %copy-start.39 = (bf16[16,96]{1,0:T(8,128)(2,1)S(1)}, bf16[16,96]{1,0:T(8,128)(2,1)}, u32[]{:S(2)}) copy-start(bf16[16,96]{1,0:T(8,128)(2,1)} %multiply_convert_fusion.cond) | copy-start | bytes 9220
  255.4 4.5 %collective-permute-start.32 = (bf16[5,48,384]{2,1,0:T(8,128)(2,1)S(1)}, bf16[5,48,384]{2,1,0:T(8,128)(2,1)S(1)}, u32[]{:S(2)}, u32[]{:S(2)}) collective-permute-start(bf16[5,48,384]{2,1,0:T(8,128)(2,1)S(1)} %fusion.8), channel_id=1, source_target_pairs={{0,2},{1,3},{2,0},{3,1},{4,6},{5,7},{6,4},{7,5},{8,10},{9,11},{10,... | collective-permute-start | bytes 552968 | tf_op jit(solution)/shard_map/ppermute | solution.py:579
  256.7 9.9 %collective-permute-start.34 = (bf16[192,768]{1,0:T(8,128)(2,1)S(1)}, bf16[192,768]{1,0:T(8,128)(2,1)S(1)}, u32[]{:S(2)}, u32[]{:S(2)}) collective-permute-start(bf16[192,768]{1,0:T(8,128)(2,1)S(1)} %bitcast.106), channel_id=1, source_target_pairs={{0,1},{1,0},{2,3},{3,2},{4,5},{5,4},{6,7},{7,6},{8,9},{9,8},{10,11... | collective-permute-start | bytes 884744 | tf_op jit(solution)/shard_map/ppermute | solution.py:579
  259.6 7.0 %copy-start.23 = (bf16[192,768]{1,0:T(8,128)(2,1)}, bf16[192,768]{1,0:T(8,128)(2,1)S(1)}, u32[]{:S(2)}) copy-start(bf16[192,768]{1,0:T(8,128)(2,1)S(1)} %collective-permute-done.35.p2) | copy-start | bytes 884740
  259.6 7.0 %collective-permute-start.36 = (bf16[192,768]{1,0:T(8,128)(2,1)S(1)}, bf16[192,768]{1,0:T(8,128)(2,1)S(1)}, u32[]{:S(2)}, u32[]{:S(2)}) collective-permute-start(bf16[192,768]{1,0:T(8,128)(2,1)S(1)} %collective-permute-done.35.p2), channel_id=1, source_target_pairs={{0,1},{1,0},{2,3},{3,2},{4,5},{5,4},{6,7},{7,6},{8,9},{9,8},{10,11... | collective-permute-start | bytes 884744 | tf_op jit(solution)/shard_map/ppermute | solution.py:579
  259.9 6.6 %copy-start.10 = (bf16[2,5,48,384]{3,2,1,0:T(8,128)(2,1)}, bf16[2,5,48,384]{3,2,1,0:T(8,128)(2,1)S(1)}, u32[]{:S(2)}) copy-start(bf16[2,5,48,384]{3,2,1,0:T(8,128)(2,1)S(1)} %pad_maximum_fusion.2.own) | copy-start | bytes 1105924
  259.9 11.2 %collective-permute-start.33 = (bf16[2,5,48,384]{3,2,1,0:T(8,128)(2,1)S(1)}, bf16[2,5,48,384]{3,2,1,0:T(8,128)(2,1)S(1)}, u32[]{:S(2)}, u32[]{:S(2)}) collective-permute-start(bf16[2,5,48,384]{3,2,1,0:T(8,128)(2,1)S(1)} %pad_maximum_fusion.2.own), channel_id=1, source_target_pairs={{0,1},{1,0},{2,3},{3,2},{4,5},{5,4},{6,7},{7,6},{8,9},{9,8},{10,11... | collective-permute-start | bytes 1105928 | tf_op jit(solution)/shard_map/ppermute | solution.py:579
  (21 other events, 21.7 us)
Sparse Core Ops, SparseCore 0:
  55.1 65.1 all-gather.2
  167.5 72.2 reduce-scatter.1

commit v3 on v2

--- a/solution.py
+++ b/solution.py
@@ -667,9 +667,8 @@
     cond = jax.nn.silu(
         jnp.dot(pick_time, table_part, precision=lax.Precision.HIGHEST)
     ).astype(BF)
-    bias = lax.dynamic_update_slice(
-        jnp.zeros((1, 6 * width), F32), b_ada.astype(F32)[None, :], (0, b_ada.shape[0] * r)
-    )
+    owner = jnp.arange(6 * width, dtype=jnp.int32) // b_ada.shape[0]
+    bias = jnp.where(owner == r, jnp.tile(b_ada.astype(F32), cp), 0.0)[None, :]
 
     if fast:
         quarter_rows = part_rows // 4
@@ -755,7 +754,6 @@
     key_col = key_ids[:, :, None]
     kvs = gather_sp(kv, key_col)
     if fast:
-        kvs[0] = after(kvs[0], w_proj)
         w_proj = jnp.stack([w_proj, swap(w_proj, "sp", 1, 4)])
     query_row = query_ids[None, :]
     part = kv.shape[0]

time: 282 us -> 282 us (level)
    unnamed x87 -> x85, local copies, waits for them, and re-layouts: 9.29 us -> 8.72 us
where the time goes in v3:
time: 282 us; the launch traced here: 281 us
  waiting for transfers between devices  80.1 us (28%)
  Pallas kernels  74.3 us (26%)
  starting transfers between devices  65.7 us (23%)
  local copies, waits for them, and re-layouts  21.4 us (8%)
  between operations  14.7 us (5%)
  blocking collectives  12.1 us (4%)
  other arithmetic  9.77 us (3%)
  matrix products  3.1 us (1%)
    pallas_call x16, Pallas kernels, call(): pl.pallas_call(kernel, out_shape=[jax.ShapeDtypeStruct(shape, kind) for s...  74.3 us
    ppermute x37, waiting for transfers between devices, swap(): return lax.ppermute(x, axis, [(i, i ^ k) for i in range(size)])  50.5 us
    ppermute x37, starting transfers between devices, swap(): return lax.ppermute(x, axis, [(i, i ^ k) for i in range(size)])  46.8 us
    all_to_all x4, waiting for transfers between devices, all_to_all(): lax.all_to_all(x, 'cp', split_axis=0, concat_axis=0, tiled=True, axis_ind...  29.5 us
    all_to_all x4, starting transfers between devices, all_to_all(): lax.all_to_all(x, 'cp', split_axis=0, concat_axis=0, tiled=True, axis_ind...  18.7 us
    all_to_all x1, blocking collectives, all_to_all(): lax.all_to_all(x, 'cp', split_axis=0, concat_axis=0, tiled=True, axis_ind...  12.1 us
    unnamed x85, local copies, waits for them, and re-layouts  8.72 us
  transfers between devices with their start and end apart: 43, of which 17 were waited for; matrix products, arithmetic and copies ran while one was open for 7% of the time, Pallas kernels for 19%

profile of v3, /device:TPU:1, one launch (start us, length us, event | category | flops | bytes accessed | tf_op | source)
XLA Modules:
  0.0 281.1 jit_solution(8069506878222254339)
XLA Ops:
  10.9 3.3 %pack.1 = (bf16[8,120,768]{2,1,0:T(8,128)(2,1)}, bf16[192,768]{1,0:T(8,128)(2,1)}) custom-call(s32[3]{0:T(128)} %pad_add_fusion.1.sc.refs_0_, bf16[2,2,32,768]{3,2,1,0:T(8,128)(2,1)} %tok.5, bf16[16,96]{1,0:T(8,128)(2,1)} %multiply_convert_fusion.cond, bf16[96,4608]{1,0:T(8,128)(2,1)} %w_ada.1, f32[1,4608]{1,0:T(1,128)} %compare_select_fusion.bias, ...), custom_call_target="tpu_custom_call" | custom-call | tf_op jit(solution)/shard_map/pack/pallas_call | solution.py:23
  14.2 6.5 %all-to-all-start = ((bf16[8,120,768]{2,1,0:T(8,128)(2,1)}), bf16[8,120,768]{2,1,0:T(8,128)(2,1)S(1)}, u32[]{:S(2)}, u32[]{:S(2)}) async-start(bf16[8,120,768]{2,1,0:T(8,128)(2,1)} %get-tuple-element.72), calls=%async_computation | async-start | bytes 2949120 | tf_op jit(solution)/shard_map/all_to_all | solution.py:619
  20.8 1.2 collective-permute-start.1
  22.0 1.3 collective-permute-start
  23.3 3.1 %collective-permute-done.1.g2 = bf16[2,2,32,768]{3,2,1,0:T(8,128)(2,1)S(1)} collective-permute-done((bf16[2,2,32,768]{3,2,1,0:T(8,128)(2,1)S(1)}, bf16[2,2,32,768]{3,2,1,0:T(8,128)(2,1)S(1)}, u32[]{:S(2)}, u32[]{:S(2)}) %collective-permute-start.1) | collective-permute-done | bytes 196640 | tf_op jit(solution)/shard_map/ppermute | solution.py:579
  26.4 1.8 collective-permute-start.2
  29.4 25.4 %all-to-all-done.refs_1_.refs_2_ = bf16[8,120,768]{2,1,0:T(8,128)(2,1)S(1)} async-done(((bf16[8,120,768]{2,1,0:T(8,128)(2,1)}), bf16[8,120,768]{2,1,0:T(8,128)(2,1)S(1)}, u32[]{:S(2)}, u32[]{:S(2)}) %all-to-all-start) | async-done | bytes 1474592 | tf_op jit(solution)/shard_map/all_to_all | solution.py:619
  55.3 1.1 collective-permute-start.4
  57.2 4.7 %all-to-all-start.2 = ((bf16[8,48,768]{2,1,0:T(8,128)(2,1)}), bf16[8,48,768]{2,1,0:T(8,128)(2,1)S(1)}, u32[]{:S(2)}, u32[]{:S(2)}) async-start(bf16[8,48,768]{2,1,0:T(8,128)(2,1)} %broadcast_in_dim.52), calls=%async_computation.2 | async-start | bytes 1179648 | tf_op jit(solution)/shard_map/all_to_all | solution.py:619
  65.3 1.8 fusion.5
  68.0 5.3 %qkv.1 = (bf16[512,192]{1,0:T(8,128)(2,1)}, bf16[512,384]{1,0:T(8,128)(2,1)}, bf16[512,768]{1,0:T(8,128)(2,1)}, bf16[512,768]{1,0:T(8,128)(2,1)}, bf16[768,576]{1,0:T(8,128)(2,1)}, /*index=5*/bf16[16,768]{1,0:T(8,128)(2,1)}) custom-call(s32[3]{0:T(128)} %pad_add_fusion.1.sc.refs_0_, bf16[8,120,768]{2,1,0:T(8,128)(2,1)} %copy-done.1, ...), custom_call_target="tpu_custom_call" | custom-call | tf_op jit(solution)/shard_map/qkv/pallas_call | solution.py:23
  73.3 1.1 collective-permute-start.7
  75.1 9.3 %collective-permute-done.7.kv2 = bf16[512,384]{1,0:T(8,128)(2,1)S(1)} collective-permute-done((bf16[512,384]{1,0:T(8,128)(2,1)}, bf16[512,384]{1,0:T(8,128)(2,1)S(1)}, u32[]{:S(2)}, u32[]{:S(2)}) %collective-permute-start.7) | collective-permute-done | bytes 393248 | tf_op jit(solution)/shard_map/ppermute | solution.py:579
  85.1 3.2 %collective-permute-start.9 = (bf16[8,48,768]{2,1,0:T(8,128)(2,1)S(1)}, bf16[8,48,768]{2,1,0:T(8,128)(2,1)S(1)}, u32[]{:S(2)}, u32[]{:S(2)}) collective-permute-start(bf16[8,48,768]{2,1,0:T(8,128)(2,1)S(1)} %all-to-all-done.2), channel_id=1, source_target_pairs={{0,1},{1,0},{2,3},{3,2},{4,5},{5,4},{6,7},{7,6},{8,9},{9,8},{10,11... | collective-permute-start | bytes 1769480 | tf_op jit(solution)/shard_map/ppermute | solution.py:579
  88.3 1.4 copy.35.kid
  92.0 7.8 %attend.1 = (bf16[512,192]{1,0:T(8,128)(2,1)}, f32[512,192]{1,0:T(8,128)}, f32[8,512]{1,0:T(8,128)}) custom-call(s32[3]{0:T(128)} %pad_add_fusion.1.sc.refs_0_, bf16[512,192]{1,0:T(8,128)(2,1)} %get-tuple-element.74.q, bf16[512,384]{1,0:T(8,128)(2,1)} %get-tuple-element.75.kv0, bf16[512,384]{1,0:T(8,128)(2,1)} %copy-done.8, bf16[512,384]{1,0:T(8,128)(2,1)} %copy-done.7, ...), custom_call_target="tpu_custom_call" | custom-call | tf_op jit(solution)/shard_map/attend/pallas_call | solution.py:23
  99.8 3.7 %all-to-all-start.1 = ((bf16[8,64,192]{2,1,0:T(8,128)(2,1)}), bf16[8,64,192]{2,1,0:T(8,128)(2,1)S(1)}, u32[]{:S(2)}, u32[]{:S(2)}) async-start(bf16[8,64,192]{2,1,0:T(8,128)(2,1)} %bitcast.108), calls=%async_computation.1 | async-start | bytes 524288 | tf_op jit(solution)/shard_map/all_to_all | solution.py:619
  104.6 1.4 slice.77.rest2
  106.0 1.3 slice.76.rest1
  107.3 1.3 slice.78.rest3
  108.7 3.2 %expand.1 = (f32[4,128,768]{2,1,0:T(8,128)}, bf16[512,768]{1,0:T(8,128)(2,1)}) custom-call(s32[3]{0:T(128)} %pad_add_fusion.1.sc.refs_0_, bf16[16,768]{1,0:T(8,128)(2,1)} %copy-done.26, bf16[16,768]{1,0:T(8,128)(2,1)} %slice.76.rest1, bf16[16,768]{1,0:T(8,128)(2,1)} %slice.77.rest2, bf16[16,768]{1,0:T(8,128)(2,1)} %slice.78.rest3, s32[512,1]{1,0:T(8,128)} %copy.40.ids, ...), custom_call_target="tpu_custom_call" | custom-call | tf_op jit(solution)/shard_map/expand/pallas_call | solution.py:23
  111.9 1.1 pad_maximum_fusion.weights
  113.0 4.1 %all-to-all-done.1.attn = bf16[8,64,192]{2,1,0:T(8,128)(2,1)S(1)} async-done(((bf16[8,64,192]{2,1,0:T(8,128)(2,1)}), bf16[8,64,192]{2,1,0:T(8,128)(2,1)S(1)}, u32[]{:S(2)}, u32[]{:S(2)}) %all-to-all-start.1) | async-done | bytes 196640 | tf_op jit(solution)/shard_map/all_to_all | solution.py:619
  117.8 3.5 %project.1 = (f32[128,768]{1,0:T(8,128)}, f32[128,768]{1,0:T(8,128)}, f32[128,768]{1,0:T(8,128)}, f32[128,1]{1,0:T(8,128)}, bf16[128,768]{1,0:T(8,128)(2,1)}, /*index=5*/bf16[768,768]{1,0:T(8,128)(2,1)}) custom-call(s32[3]{0:T(128)} %pad_add_fusion.1.sc.refs_0_, bf16[8,64,192]{2,1,0:T(8,128)(2,1)} %copy-done.3, bf16[2,2,32,768]{3,2,1,0:T(8,128)(2,1)} %tok.5, ...), custom_call_target="tpu_custom_call" | custom-call | tf_op jit(solution)/shard_map/project/pallas_call | solution.py:23
  121.3 2.6 collective-permute-start.10
  123.9 2.1 collective-permute-done.11.h2
  126.0 3.1 %collective-permute-start.12 = (bf16[128,768]{1,0:T(8,128)(2,1)S(1)}, bf16[128,768]{1,0:T(8,128)(2,1)S(1)}, u32[]{:S(2)}, u32[]{:S(2)}) collective-permute-start(bf16[128,768]{1,0:T(8,128)(2,1)S(1)} %collective-permute-done.11.h2), channel_id=1, source_target_pairs={{0,1},{1,0},{2,3},{3,2},{4,5},{5,4},{6,7},{7,6},{8,9},{9,8},{10,11... | collective-permute-start | bytes 589832 | tf_op jit(solution)/shard_map/ppermute | solution.py:579
  129.1 1.1 collective-permute-done.12.h3
  130.9 6.1 %feed.1 = (bf16[2,128,768]{2,1,0:T(8,128)(2,1)}, bf16[2,128,768]{2,1,0:T(8,128)(2,1)}, bf16[2,128,768]{2,1,0:T(8,128)(2,1)}, bf16[2,128,768]{2,1,0:T(8,128)(2,1)...) custom-call(s32[3]{0:T(128)} %pad_add_fusion.1.sc.refs_0_, ...), custom_call_target="tpu_custom_call" | custom-call | tf_op jit(solution)/shard_map/feed/pallas_call | solution.py:23
  137.3 1.6 collective-permute-done.13.dh_recv
  138.9 1.1 fusion.6
  140.5 5.7 %collective-permute-done.15.dh_far = bf16[128,768]{1,0:T(8,128)(2,1)S(1)} collective-permute-done((bf16[128,768]{1,0:T(8,128)(2,1)S(1)}, bf16[128,768]{1,0:T(8,128)(2,1)S(1)}, u32[]{:S(2)}, u32[]{:S(2)}) %collective-permute-start.15) | collective-permute-done | bytes 196640 | tf_op jit(solution)/shard_map/ppermute | solution.py:579
  146.8 3.7 %middle.1 = (f32[128,768]{1,0:T(8,128)}, f32[128,768]{1,0:T(8,128)}, bf16[128,768]{1,0:T(8,128)(2,1)}, bf16[8,64,192]{2,1,0:T(8,128)(2,1)}) custom-call(s32[3]{0:T(128)} %pad_add_fusion.1.sc.refs_0_, bf16[2,128,768]{2,1,0:T(8,128)(2,1)} %get-tuple-element.87.dh_keep, bf16[2,128,768]{2,1,0:T(8,128)(2,1)} %copy-done.12, bf16[128,768]{1,0:T(8,128)(2,1)} %copy-done.30, ...), custom_call_target="tpu_custom_call" | custom-call | tf_op jit(solution)/shard_map/middle/pallas_call | solution.py:23
  150.6 12.1 %all_to_all.25 = bf16[8,64,192]{2,1,0:T(8,128)(2,1)} all-to-all(bf16[8,64,192]{2,1,0:T(8,128)(2,1)} %get-tuple-element.95), channel_id=1, replica_groups=mesh['cp'=8,'sp'=4] {'cp'}, dimensions={0} | all-to-all | bytes 393216 | tf_op jit(solution)/shard_map/all_to_all | solution.py:619
  162.7 4.7 %feed_grad.1 = bf16[8,192,768]{2,1,0:T(8,128)(2,1)} custom-call(s32[3]{0:T(128)} %pad_add_fusion.1.sc.refs_0_, bf16[512,768]{1,0:T(8,128)(2,1)} %get-tuple-element.96.h, bf16[512,768]{1,0:T(8,128)(2,1)} %get-tuple-element.82.dz_in.dz, bf16[512,768]{1,0:T(8,128)(2,1)} %get-tuple-element.98.act, bf16[512,768]{1,0:T(8,128)(2,1)} %get-tuple-element.99.du), custom_call_target="tpu_custom_call" | custom-call | tf_op jit(solution)/shard_map/feed_grad/pallas_call | solution.py:23
  167.3 13.7 %attend_back.1 = (f32[512,192]{1,0:T(8,128)}, bf16[2,512,384]{2,1,0:T(8,128)(2,1)}, bf16[2,512,384]{2,1,0:T(8,128)(2,1)}) custom-call(s32[3]{0:T(128)} %pad_add_fusion.1.sc.refs_0_, bf16[512,192]{1,0:T(8,128)(2,1)} %get-tuple-element.74.q, bf16[512,384]{1,0:T(8,128)(2,1)} %get-tuple-element.75.kv0, bf16[512,384]{1,0:T(8,128)(2,1)} %copy-done.8, ...), custom_call_target="tpu_custom_call" | custom-call | tf_op jit(solution)/shard_map/attend_back/pallas_call | solution.py:23
  181.1 2.8 %collective-permute-start.16 = (bf16[2,512,384]{2,1,0:T(8,128)(2,1)}, bf16[2,512,384]{2,1,0:T(8,128)(2,1)S(1)}, u32[]{:S(2)}, u32[]{:S(2)}) collective-permute-start(bf16[2,512,384]{2,1,0:T(8,128)(2,1)} %get-tuple-element.103), channel_id=1, source_target_pairs={{0,1},{1,0},{2,3},{3,2},{4,5},{5,4},{6,7},{7,6},{8,9},{9,8},{10,11... | collective-permute-start | bytes 2359304 | tf_op jit(solution)/shard_map/ppermute | solution.py:579
  184.6 3.3 %middle_grad.1 = (f32[3,16,768]{2,1,0:T(8,128)}, bf16[8,48,768]{2,1,0:T(8,128)(2,1)}, bf16[8,48,768]{2,1,0:T(8,128)(2,1)}) custom-call(s32[3]{0:T(128)} %pad_add_fusion.1.sc.refs_0_, f32[128,768]{1,0:T(8,128)} %get-tuple-element.111.dx, f32[128,768]{1,0:T(8,128)} %get-tuple-element.117.dh, bf16[128,768]{1,0:T(8,128)(2,1)} %get-tuple-element.118.dy, ...), custom_call_target="tpu_custom_call" | custom-call | tf_op jit(solution)/shard_map/middle_grad/pallas_call | solution.py:23
  190.3 1.1 collective-permute-start.26
  191.4 7.8 %collective-permute-done.17.dkv_c = bf16[512,384]{1,0:T(8,128)(2,1)S(1)} collective-permute-done((bf16[512,384]{1,0:T(8,128)(2,1)}, bf16[512,384]{1,0:T(8,128)(2,1)S(1)}, u32[]{:S(2)}, u32[]{:S(2)}) %collective-permute-start.17) | collective-permute-done | bytes 393248 | tf_op jit(solution)/shard_map/ppermute | solution.py:579
  200.0 5.0 %qkv_back.1 = (bf16[8,64,768]{2,1,0:T(8,128)(2,1)}, bf16[512,768]{1,0:T(8,128)(2,1)}, bf16[512,576]{1,0:T(8,128)(2,1)}) custom-call(s32[3]{0:T(128)} %pad_add_fusion.1.sc.refs_0_, f32[512,192]{1,0:T(8,128)} %get-tuple-element.101.dq, bf16[2,512,384]{2,1,0:T(8,128)(2,1)} %get-tuple-element.102.dkv_a, bf16[2,512,384]{2,1,0:T(8,128)(2,1)} %copy-done.6, ...), custom_call_target="tpu_custom_call" | custom-call | tf_op jit(solution)/shard_map/qkv_back/pallas_call | solution.py:23
  205.7 3.8 %all-to-all-start.4 = ((bf16[8,64,768]{2,1,0:T(8,128)(2,1)}), bf16[8,64,768]{2,1,0:T(8,128)(2,1)S(1)}, u32[]{:S(2)}, u32[]{:S(2)}) async-start(bf16[8,64,768]{2,1,0:T(8,128)(2,1)} %get-tuple-element.106), calls=%async_computation.4 | async-start | bytes 1572864 | tf_op jit(solution)/shard_map/all_to_all | solution.py:619
  209.5 4.1 %qkv_grad.1 = (f32[2,16,768]{2,1,0:T(8,128)}, bf16[8,48,768]{2,1,0:T(8,128)(2,1)}, bf16[8,48,768]{2,1,0:T(8,128)(2,1)}) custom-call(s32[3]{0:T(128)} %pad_add_fusion.1.sc.refs_0_, bf16[512,576]{1,0:T(8,128)(2,1)} %get-tuple-element.112.d, bf16[512,768]{1,0:T(8,128)(2,1)} %get-tuple-element.113.dh, bf16[512,768]{1,0:T(8,128)(2,1)} %get-tuple-element.114.h, ...), custom_call_target="tpu_custom_call" | custom-call | tf_op jit(solution)/shard_map/qkv_grad/pallas_call | solution.py:23
  214.5 1.4 collective-permute-start.24
  216.6 2.7 block.1
  220.4 1.2 collective-permute-done.19
  221.7 1.2 collective-permute-start.20
  223.5 3.5 %collective-permute-done.20 = bf16[6,16,768]{2,1,0:T(8,128)(2,1)S(1)} collective-permute-done((bf16[6,16,768]{2,1,0:T(8,128)(2,1)S(1)}, bf16[6,16,768]{2,1,0:T(8,128)(2,1)S(1)}, u32[]{:S(2)}, u32[]{:S(2)}) %collective-permute-start.20) | collective-permute-done | bytes 147488 | tf_op jit(solution)/shard_map/ppermute | solution.py:579
  227.1 1.6 collective-permute-start.21
  228.7 3.1 %collective-permute-done.21 = bf16[6,16,768]{2,1,0:T(8,128)(2,1)S(1)} collective-permute-done((bf16[6,16,768]{2,1,0:T(8,128)(2,1)S(1)}, bf16[6,16,768]{2,1,0:T(8,128)(2,1)S(1)}, u32[]{:S(2)}, u32[]{:S(2)}) %collective-permute-start.21) | collective-permute-done | bytes 147488 | tf_op jit(solution)/shard_map/ppermute | solution.py:579
  231.8 4.8 %collective-permute-done.27 = bf16[12,48,384]{2,1,0:T(8,128)(2,1)S(1)} collective-permute-done((bf16[12,48,384]{2,1,0:T(8,128)(2,1)S(1)}, bf16[12,48,384]{2,1,0:T(8,128)(2,1)S(1)}, u32[]{:S(2)}, u32[]{:S(2)}) %collective-permute-start.27) | collective-permute-done | bytes 442400 | tf_op jit(solution)/shard_map/ppermute | solution.py:579
  236.7 1.5 collective-permute-start.22
  238.2 2.5 last.1
  240.8 1.3 collective-permute-start.28
  242.1 2.1 collective-permute-start.23
  244.2 1.3 collective-permute-start.35
  246.5 2.1 collective-permute-start.30
  249.4 6.0 %collective-permute-done.30 = bf16[2,48,384]{2,1,0:T(8,128)(2,1)S(1)} collective-permute-done((bf16[2,48,384]{2,1,0:T(8,128)(2,1)S(1)}, bf16[2,48,384]{2,1,0:T(8,128)(2,1)S(1)}, u32[]{:S(2)}, u32[]{:S(2)}) %collective-permute-start.30) | collective-permute-done | bytes 73760 | tf_op jit(solution)/shard_map/ppermute | solution.py:579
  255.5 1.2 collective-permute-start.32
  256.7 2.9 %collective-permute-start.34 = (bf16[192,768]{1,0:T(8,128)(2,1)S(1)}, bf16[192,768]{1,0:T(8,128)(2,1)S(1)}, u32[]{:S(2)}, u32[]{:S(2)}) collective-permute-start(bf16[192,768]{1,0:T(8,128)(2,1)S(1)} %bitcast.106), channel_id=1, source_target_pairs={{0,1},{1,0},{2,3},{3,2},{4,5},{5,4},{6,7},{7,6},{8,9},{9,8},{10,11... | collective-permute-start | bytes 884744 | tf_op jit(solution)/shard_map/ppermute | solution.py:579
  260.0 3.7 %collective-permute-start.33 = (bf16[2,5,48,384]{3,2,1,0:T(8,128)(2,1)S(1)}, bf16[2,5,48,384]{3,2,1,0:T(8,128)(2,1)S(1)}, u32[]{:S(2)}, u32[]{:S(2)}) collective-permute-start(bf16[2,5,48,384]{3,2,1,0:T(8,128)(2,1)S(1)} %pad_maximum_fusion.2.own), channel_id=1, source_target_pairs={{0,1},{1,0},{2,3},{3,2},{4,5},{5,4},{6,7},{7,6},{8,9},{9,8},{10,11... | collective-permute-start | bytes 1105928 | tf_op jit(solution)/shard_map/ppermute | solution.py:579
  264.5 2.1 fusion.25
  268.1 3.1 %finish.1 = (f32[96,3072]{1,0:T(8,128)}, f32[384,768]{1,0:T(8,128)}) custom-call(s32[3]{0:T(128)} %pad_add_fusion.1.sc.refs_0_, bf16[192,768]{1,0:T(8,128)(2,1)} %bitcast.104, bf16[192,768]{1,0:T(8,128)(2,1)} %copy-done.24, bf16[192,768]{1,0:T(8,128)(2,1)} %copy-done.23, bf16[192,768]{1,0:T(8,128)(2,1)} %copy-done.25), custom_call_target="tpu_custom_call" | custom-call | tf_op jit(solution)/shard_map/finish/pallas_call | solution.py:23
  271.9 2.4 finish_qkv.1
  (206 shorter events, 31.3 us)
Async XLA Ops:
  7.2 2.9 %copy-start = (f32[64,768]{1,0:T(8,128)S(1)}, f32[64,768]{1,0:T(8,128)}, u32[]{:S(2)}) copy-start(f32[64,768]{1,0:T(8,128)} %param.14) | copy-start | bytes 589828
  14.2 6.6 %copy-start.4 = (bf16[2,2,32,768]{3,2,1,0:T(8,128)(2,1)S(1)}, bf16[2,2,32,768]{3,2,1,0:T(8,128)(2,1)}, u32[]{:S(2)}) copy-start(bf16[2,2,32,768]{3,2,1,0:T(8,128)(2,1)} %grad.3) | copy-start | bytes 589828
  14.2 40.7 %copy-start.37 = (bf16[96,768]{1,0:T(8,128)(2,1)S(1)}, bf16[96,768]{1,0:T(8,128)(2,1)}, u32[]{:S(2)}) copy-start(bf16[96,768]{1,0:T(8,128)(2,1)} %param.21) | copy-start | bytes 442372
  14.2 40.7 %copy-start.40 = (s32[16]{0:T(128)S(1)}, s32[16]{0:T(128)}, u32[]{:S(2)}) copy-start(s32[16]{0:T(128)} %param.16) | copy-start | bytes 196
  14.2 40.7 %copy-start.39 = (s32[2,2048]{1,0:T(2,128)S(1)}, s32[2,2048]{1,0:T(2,128)}, u32[]{:S(2)}) copy-start(s32[2,2048]{1,0:T(2,128)} %param.17) | copy-start | bytes 49156
  14.2 40.6 %all-to-all-start = ((bf16[8,120,768]{2,1,0:T(8,128)(2,1)}), bf16[8,120,768]{2,1,0:T(8,128)(2,1)S(1)}, u32[]{:S(2)}, u32[]{:S(2)}) async-start(bf16[8,120,768]{2,1,0:T(8,128)(2,1)} %get-tuple-element.72), calls=%async_computation | async-start | bytes 2949120 | tf_op jit(solution)/shard_map/all_to_all | solution.py:619
  20.7 109.5 %all-gather.3.cloned.1.call-start = ((), (), s32[]{:S(2)}) async-start(), calls=%async_computation.7 | async-start | bytes 2654208 | tf_op jit(solution)/shard_map/all_gather | solution.py:719
  20.8 5.6 %collective-permute-start.1 = (bf16[2,2,32,768]{3,2,1,0:T(8,128)(2,1)S(1)}, bf16[2,2,32,768]{3,2,1,0:T(8,128)(2,1)S(1)}, u32[]{:S(2)}, u32[]{:S(2)}) collective-permute-start(bf16[2,2,32,768]{3,2,1,0:T(8,128)(2,1)S(1)} %copy-done.4), channel_id=1, source_target_pairs={{0,2},{1,3},{2,0},{3,1},{4,6},{5,7},{6,4},{7,5},{8,10},{9,11},{10,... | collective-permute-start | bytes 589832 | tf_op jit(solution)/shard_map/ppermute | solution.py:579
  22.0 6.2 %collective-permute-start = (bf16[2,2,32,768]{3,2,1,0:T(8,128)(2,1)S(1)}, bf16[2,2,32,768]{3,2,1,0:T(8,128)(2,1)S(1)}, u32[]{:S(2)}, u32[]{:S(2)}) collective-permute-start(bf16[2,2,32,768]{3,2,1,0:T(8,128)(2,1)S(1)} %copy-done.4), channel_id=1, source_target_pairs={{0,1},{1,0},{2,3},{3,2},{4,5},{5,4},{6,7},{7,6},{8,9},{9,8},{10,11... | collective-permute-start | bytes 589832 | tf_op jit(solution)/shard_map/ppermute | solution.py:579
  26.4 3.0 %collective-permute-start.2 = (bf16[2,2,32,768]{3,2,1,0:T(8,128)(2,1)S(1)}, bf16[2,2,32,768]{3,2,1,0:T(8,128)(2,1)}, u32[]{:S(2)}, u32[]{:S(2)}) collective-permute-start(bf16[2,2,32,768]{3,2,1,0:T(8,128)(2,1)S(1)} %collective-permute-done.1.g2), channel_id=1, source_target_pairs={{0,1},{1,0},{2,3},{3,2},{4,5},{5,4},{6,7},{7,6},{8,9},{9,8},{10,11... | collective-permute-start | bytes 589832 | tf_op jit(solution)/shard_map/ppermute | solution.py:579
  54.8 2.4 copy-start.1
  55.2 11.9 %copy-start.11 = (bf16[208,768]{1,0:T(8,128)(2,1)}, bf16[208,768]{1,0:T(8,128)(2,1)S(1)}, u32[]{:S(2)}) copy-start(bf16[208,768]{1,0:T(8,128)(2,1)S(1)} %pad_maximum_fusion.3.refs_6_) | copy-start | bytes 958468
  55.3 9.1 %collective-permute-start.4 = (bf16[208,768]{1,0:T(8,128)(2,1)S(1)}, bf16[208,768]{1,0:T(8,128)(2,1)S(1)}, u32[]{:S(2)}, u32[]{:S(2)}) collective-permute-start(bf16[208,768]{1,0:T(8,128)(2,1)S(1)} %pad_maximum_fusion.3.refs_6_), channel_id=1, source_target_pairs={{0,2},{1,3},{2,0},{3,1},{4,6},{5,7},{6,4},{7,5},{8,10},{9,11},{10,... | collective-permute-start | bytes 958472 | tf_op jit(solution)/shard_map/ppermute | solution.py:579
  57.2 27.8 %all-to-all-start.2 = ((bf16[8,48,768]{2,1,0:T(8,128)(2,1)}), bf16[8,48,768]{2,1,0:T(8,128)(2,1)S(1)}, u32[]{:S(2)}, u32[]{:S(2)}) async-start(bf16[8,48,768]{2,1,0:T(8,128)(2,1)} %broadcast_in_dim.52), calls=%async_computation.2 | async-start | bytes 1179648 | tf_op jit(solution)/shard_map/all_to_all | solution.py:619
  62.2 22.8 %copy-start.34 = (s32[2,16,4,32]{3,2,1,0:T(4,128)}, s32[2,16,4,32]{3,2,1,0:T(4,128)S(1)}, u32[]{:S(2)}) copy-start(s32[2,16,4,32]{3,2,1,0:T(4,128)S(1)} %reshape.221) | copy-start | bytes 49156
  63.3 3.9 %collective-permute-start.3 = (bf16[208,768]{1,0:T(8,128)(2,1)S(1)}, bf16[208,768]{1,0:T(8,128)(2,1)S(1)}, u32[]{:S(2)}, u32[]{:S(2)}) collective-permute-start(bf16[208,768]{1,0:T(8,128)(2,1)S(1)} %pad_maximum_fusion.3.refs_6_), channel_id=1, source_target_pairs={{0,1},{1,0},{2,3},{3,2},{4,5},{5,4},{6,7},{7,6},{8,9},{9,8},{10,11... | collective-permute-start | bytes 958472 | tf_op jit(solution)/shard_map/ppermute | solution.py:579
  64.3 2.9 %copy-start.18 = (bf16[208,768]{1,0:T(8,128)(2,1)}, bf16[208,768]{1,0:T(8,128)(2,1)S(1)}, u32[]{:S(2)}) copy-start(bf16[208,768]{1,0:T(8,128)(2,1)S(1)} %collective-permute-done.4.refs_8_) | copy-start | bytes 958468
  64.3 2.8 %collective-permute-start.5 = (bf16[208,768]{1,0:T(8,128)(2,1)S(1)}, bf16[208,768]{1,0:T(8,128)(2,1)S(1)}, u32[]{:S(2)}, u32[]{:S(2)}) collective-permute-start(bf16[208,768]{1,0:T(8,128)(2,1)S(1)} %collective-permute-done.4.refs_8_), channel_id=1, source_target_pairs={{0,1},{1,0},{2,3},{3,2},{4,5},{5,4},{6,7},{7,6},{8,9},{9,8},{10,11... | collective-permute-start | bytes 958472 | tf_op jit(solution)/shard_map/ppermute | solution.py:579
  73.3 11.1 %collective-permute-start.7 = (bf16[512,384]{1,0:T(8,128)(2,1)}, bf16[512,384]{1,0:T(8,128)(2,1)S(1)}, u32[]{:S(2)}, u32[]{:S(2)}) collective-permute-start(bf16[512,384]{1,0:T(8,128)(2,1)} %get-tuple-element.75.kv0), channel_id=1, source_target_pairs={{0,2},{1,3},{2,0},{3,1},{4,6},{5,7},{6,4},{7,5},{8,10},{9,11},{10,... | collective-permute-start | bytes 1179656 | tf_op jit(solution)/shard_map/ppermute | solution.py:579
  74.5 16.6 %copy-start.36 = (s32[1,512]{1,0:T(1,128)}, s32[1,512]{1,0:T(1,128)S(1)}, u32[]{:S(2)}) copy-start(s32[1,512]{1,0:T(1,128)S(1)} %stack_reshape.12.qid.ids_row) | copy-start | bytes 6148
  74.7 16.4 %collective-permute-start.6 = (bf16[512,384]{1,0:T(8,128)(2,1)}, bf16[512,384]{1,0:T(8,128)(2,1)S(1)}, u32[]{:S(2)}, u32[]{:S(2)}) collective-permute-start(bf16[512,384]{1,0:T(8,128)(2,1)} %get-tuple-element.75.kv0), channel_id=1, source_target_pairs={{0,1},{1,0},{2,3},{3,2},{4,5},{5,4},{6,7},{7,6},{8,9},{9,8},{10,11... | collective-permute-start | bytes 1179656 | tf_op jit(solution)/shard_map/ppermute | solution.py:579
  84.4 6.7 %copy-start.7 = (bf16[512,384]{1,0:T(8,128)(2,1)}, bf16[512,384]{1,0:T(8,128)(2,1)S(1)}, u32[]{:S(2)}) copy-start(bf16[512,384]{1,0:T(8,128)(2,1)S(1)} %collective-permute-done.7.kv2) | copy-start | bytes 1179652
  84.4 6.7 %collective-permute-start.8 = (bf16[512,384]{1,0:T(8,128)(2,1)S(1)}, bf16[512,384]{1,0:T(8,128)(2,1)S(1)}, u32[]{:S(2)}, u32[]{:S(2)}) collective-permute-start(bf16[512,384]{1,0:T(8,128)(2,1)S(1)} %collective-permute-done.7.kv2), channel_id=1, source_target_pairs={{0,1},{1,0},{2,3},{3,2},{4,5},{5,4},{6,7},{7,6},{8,9},{9,8},{10,11... | collective-permute-start | bytes 1179656 | tf_op jit(solution)/shard_map/ppermute | solution.py:579
  85.1 26.8 %collective-permute-start.9 = (bf16[8,48,768]{2,1,0:T(8,128)(2,1)S(1)}, bf16[8,48,768]{2,1,0:T(8,128)(2,1)S(1)}, u32[]{:S(2)}, u32[]{:S(2)}) collective-permute-start(bf16[8,48,768]{2,1,0:T(8,128)(2,1)S(1)} %all-to-all-done.2), channel_id=1, source_target_pairs={{0,1},{1,0},{2,3},{3,2},{4,5},{5,4},{6,7},{7,6},{8,9},{9,8},{10,11... | collective-permute-start | bytes 1769480 | tf_op jit(solution)/shard_map/ppermute | solution.py:579
  99.8 17.2 %all-to-all-start.1 = ((bf16[8,64,192]{2,1,0:T(8,128)(2,1)}), bf16[8,64,192]{2,1,0:T(8,128)(2,1)S(1)}, u32[]{:S(2)}, u32[]{:S(2)}) async-start(bf16[8,64,192]{2,1,0:T(8,128)(2,1)} %bitcast.108), calls=%async_computation.1 | async-start | bytes 524288 | tf_op jit(solution)/shard_map/all_to_all | solution.py:619
  103.5 137.2 %reduce-scatter.2.cloned.1.call-start = ((), (), s32[]{:S(2)}) async-start(), calls=%async_computation.6 | async-start | bytes 2654208 | tf_op jit(solution)/shard_map/reduce_scatter | solution.py:858
  121.3 4.7 %collective-permute-start.11 = (bf16[128,768]{1,0:T(8,128)(2,1)}, bf16[128,768]{1,0:T(8,128)(2,1)S(1)}, u32[]{:S(2)}, u32[]{:S(2)}) collective-permute-start(bf16[128,768]{1,0:T(8,128)(2,1)} %get-tuple-element.81.h0), channel_id=1, source_target_pairs={{0,2},{1,3},{2,0},{3,1},{4,6},{5,7},{6,4},{7,5},{8,10},{9,11},{10,... | collective-permute-start | bytes 589832 | tf_op jit(solution)/shard_map/ppermute | solution.py:579
  121.3 7.8 %collective-permute-start.10 = (bf16[128,768]{1,0:T(8,128)(2,1)}, bf16[128,768]{1,0:T(8,128)(2,1)S(1)}, u32[]{:S(2)}, u32[]{:S(2)}) collective-permute-start(bf16[128,768]{1,0:T(8,128)(2,1)} %get-tuple-element.81.h0), channel_id=1, source_target_pairs={{0,1},{1,0},{2,3},{3,2},{4,5},{5,4},{6,7},{7,6},{8,9},{9,8},{10,11... | collective-permute-start | bytes 589832 | tf_op jit(solution)/shard_map/ppermute | solution.py:579
  126.0 4.2 %copy-start.27 = (bf16[128,768]{1,0:T(8,128)(2,1)}, bf16[128,768]{1,0:T(8,128)(2,1)S(1)}, u32[]{:S(2)}) copy-start(bf16[128,768]{1,0:T(8,128)(2,1)S(1)} %collective-permute-done.11.h2) | copy-start | bytes 589828
  126.0 4.2 %collective-permute-start.12 = (bf16[128,768]{1,0:T(8,128)(2,1)S(1)}, bf16[128,768]{1,0:T(8,128)(2,1)S(1)}, u32[]{:S(2)}, u32[]{:S(2)}) collective-permute-start(bf16[128,768]{1,0:T(8,128)(2,1)S(1)} %collective-permute-done.11.h2), channel_id=1, source_target_pairs={{0,1},{1,0},{2,3},{3,2},{4,5},{5,4},{6,7},{7,6},{8,9},{9,8},{10,11... | collective-permute-start | bytes 589832 | tf_op jit(solution)/shard_map/ppermute | solution.py:579
  136.9 1.9 collective-permute-start.13
  138.9 7.3 %copy-start.12 = (bf16[2,128,768]{2,1,0:T(8,128)(2,1)}, bf16[2,128,768]{2,1,0:T(8,128)(2,1)S(1)}, u32[]{:S(2)}) copy-start(bf16[2,128,768]{2,1,0:T(8,128)(2,1)S(1)} %collective-permute-done.13.dh_recv) | copy-start | bytes 1179652
  140.0 6.2 %collective-permute-start.15 = (bf16[128,768]{1,0:T(8,128)(2,1)S(1)}, bf16[128,768]{1,0:T(8,128)(2,1)S(1)}, u32[]{:S(2)}, u32[]{:S(2)}) collective-permute-start(bf16[128,768]{1,0:T(8,128)(2,1)S(1)} %fusion.6), channel_id=1, source_target_pairs={{0,2},{1,3},{2,0},{3,1},{4,6},{5,7},{6,4},{7,5},{8,10},{9,11},{10,... | collective-permute-start | bytes 589832 | tf_op jit(solution)/shard_map/ppermute | solution.py:579
  181.1 6.9 %copy-start.5 = (bf16[2,512,384]{2,1,0:T(8,128)(2,1)S(1)}, bf16[2,512,384]{2,1,0:T(8,128)(2,1)}, u32[]{:S(2)}) copy-start(bf16[2,512,384]{2,1,0:T(8,128)(2,1)} %get-tuple-element.102.dkv_a) | copy-start | bytes 2359300
  181.1 6.9 %collective-permute-start.16 = (bf16[2,512,384]{2,1,0:T(8,128)(2,1)}, bf16[2,512,384]{2,1,0:T(8,128)(2,1)S(1)}, u32[]{:S(2)}, u32[]{:S(2)}) collective-permute-start(bf16[2,512,384]{2,1,0:T(8,128)(2,1)} %get-tuple-element.103), channel_id=1, source_target_pairs={{0,1},{1,0},{2,3},{3,2},{4,5},{5,4},{6,7},{7,6},{8,9},{9,8},{10,11... | collective-permute-start | bytes 2359304 | tf_op jit(solution)/shard_map/ppermute | solution.py:579
  187.9 2.2 collective-permute-start.25
  188.8 10.4 %collective-permute-start.17 = (bf16[512,384]{1,0:T(8,128)(2,1)}, bf16[512,384]{1,0:T(8,128)(2,1)S(1)}, u32[]{:S(2)}, u32[]{:S(2)}) collective-permute-start(bf16[512,384]{1,0:T(8,128)(2,1)} %fusion.2), channel_id=1, source_target_pairs={{0,2},{1,3},{2,0},{3,1},{4,6},{5,7},{6,4},{7,5},{8,10},{9,11},{10,... | collective-permute-start | bytes 1179656 | tf_op jit(solution)/shard_map/ppermute | solution.py:579
  188.8 16.2 %collective-permute-start.14 = (bf16[2,128,768]{2,1,0:T(8,128)(2,1)}, bf16[2,128,768]{2,1,0:T(8,128)(2,1)S(1)}, u32[]{:S(2)}, u32[]{:S(2)}) collective-permute-start(bf16[2,128,768]{2,1,0:T(8,128)(2,1)} %get-tuple-element.89), channel_id=1, source_target_pairs={{0,1},{1,0},{2,3},{3,2},{4,5},{5,4},{6,7},{7,6},{8,9},{9,8},{10,11... | collective-permute-start | bytes 1179656 | tf_op jit(solution)/shard_map/ppermute | solution.py:579
  190.3 24.1 %collective-permute-start.26 = (bf16[4,48,768]{2,1,0:T(8,128)(2,1)S(1)}, bf16[4,48,768]{2,1,0:T(8,128)(2,1)S(1)}, u32[]{:S(2)}, u32[]{:S(2)}) collective-permute-start(bf16[4,48,768]{2,1,0:T(8,128)(2,1)S(1)} %dynamic-slice_bitcast_fusion), channel_id=1, source_target_pairs={{0,4},{4,0},{8,12},{12,8},{16,20},{20,16},{24,28},{28,24},{1,5},{5... | collective-permute-start | bytes 884744 | tf_op jit(solution)/shard_map/ppermute | solution.py:579
  200.0 5.0 %copy-start.13 = (bf16[2,128,768]{2,1,0:T(8,128)(2,1)S(1)}, bf16[2,128,768]{2,1,0:T(8,128)(2,1)}, u32[]{:S(2)}) copy-start(bf16[2,128,768]{2,1,0:T(8,128)(2,1)} %get-tuple-element.85.z_keep) | copy-start | bytes 1179652
  200.0 5.2 %copy-start.35 = (f32[3,16,768]{2,1,0:T(8,128)S(1)}, f32[3,16,768]{2,1,0:T(8,128)}, u32[]{:S(2)}) copy-start(f32[3,16,768]{2,1,0:T(8,128)} %get-tuple-element.121) | copy-start | bytes 442372
  205.1 10.9 %collective-permute-start.18 = (bf16[128,768]{1,0:T(8,128)(2,1)S(1)}, bf16[128,768]{1,0:T(8,128)(2,1)S(1)}, u32[]{:S(2)}, u32[]{:S(2)}) collective-permute-start(bf16[128,768]{1,0:T(8,128)(2,1)S(1)} %fusion.7), channel_id=1, source_target_pairs={{0,2},{1,3},{2,0},{3,1},{4,6},{5,7},{6,4},{7,5},{8,10},{9,11},{10,... | collective-permute-start | bytes 589832 | tf_op jit(solution)/shard_map/ppermute | solution.py:579
  205.7 31.0 %all-to-all-start.4 = ((bf16[8,64,768]{2,1,0:T(8,128)(2,1)}), bf16[8,64,768]{2,1,0:T(8,128)(2,1)S(1)}, u32[]{:S(2)}, u32[]{:S(2)}) async-start(bf16[8,64,768]{2,1,0:T(8,128)(2,1)} %get-tuple-element.106), calls=%async_computation.4 | async-start | bytes 1572864 | tf_op jit(solution)/shard_map/all_to_all | solution.py:619
  214.5 8.4 %collective-permute-start.24 = (bf16[8,48,768]{2,1,0:T(8,128)(2,1)}, bf16[8,48,768]{2,1,0:T(8,128)(2,1)S(1)}, u32[]{:S(2)}, u32[]{:S(2)}) collective-permute-start(bf16[8,48,768]{2,1,0:T(8,128)(2,1)} %get-tuple-element.125), channel_id=1, source_target_pairs={{0,1},{1,0},{2,3},{3,2},{4,5},{5,4},{6,7},{7,6},{8,9},{9,8},{10,11... | collective-permute-start | bytes 1769480 | tf_op jit(solution)/shard_map/ppermute | solution.py:579
  219.3 3.6 %copy-start.15 = (bf16[8,48,768]{2,1,0:T(8,128)(2,1)S(1)}, bf16[8,48,768]{2,1,0:T(8,128)(2,1)}, u32[]{:S(2)}) copy-start(bf16[8,48,768]{2,1,0:T(8,128)(2,1)} %get-tuple-element.124) | copy-start | bytes 1769476
  220.2 1.4 collective-permute-start.19
  221.7 5.4 %collective-permute-start.20 = (bf16[6,16,768]{2,1,0:T(8,128)(2,1)S(1)}, bf16[6,16,768]{2,1,0:T(8,128)(2,1)S(1)}, u32[]{:S(2)}, u32[]{:S(2)}) collective-permute-start(bf16[6,16,768]{2,1,0:T(8,128)(2,1)S(1)} %add_convert_fusion.9), channel_id=1, source_target_pairs={{0,2},{1,3},{2,0},{3,1},{4,6},{5,7},{6,4},{7,5},{8,10},{9,11},{10,... | collective-permute-start | bytes 442376 | tf_op jit(solution)/shard_map/ppermute | solution.py:579
  223.2 13.4 %collective-permute-start.27 = (bf16[12,48,384]{2,1,0:T(8,128)(2,1)S(1)}, bf16[12,48,384]{2,1,0:T(8,128)(2,1)S(1)}, u32[]{:S(2)}, u32[]{:S(2)}) collective-permute-start(bf16[12,48,384]{2,1,0:T(8,128)(2,1)S(1)} %pad_maximum_fusion.1), channel_id=1, source_target_pairs={{0,2},{1,3},{2,0},{3,1},{4,6},{5,7},{6,4},{7,5},{8,10},{9,11},{10,... | collective-permute-start | bytes 1327112 | tf_op jit(solution)/shard_map/ppermute | solution.py:579
  227.1 4.7 %collective-permute-start.21 = (bf16[6,16,768]{2,1,0:T(8,128)(2,1)S(1)}, bf16[6,16,768]{2,1,0:T(8,128)(2,1)S(1)}, u32[]{:S(2)}, u32[]{:S(2)}) collective-permute-start(bf16[6,16,768]{2,1,0:T(8,128)(2,1)S(1)} %add_convert_fusion.8), channel_id=1, source_target_pairs={{0,4},{4,0},{8,12},{12,8},{16,20},{20,16},{24,28},{28,24},{1,5},{5... | collective-permute-start | bytes 442376 | tf_op jit(solution)/shard_map/ppermute | solution.py:579
  236.7 5.4 %collective-permute-start.22 = (bf16[6,16,768]{2,1,0:T(8,128)(2,1)S(1)}, bf16[6,16,768]{2,1,0:T(8,128)(2,1)S(1)}, u32[]{:S(2)}, u32[]{:S(2)}) collective-permute-start(bf16[6,16,768]{2,1,0:T(8,128)(2,1)S(1)} %convert_add_fusion.3), channel_id=1, source_target_pairs={{0,8},{4,12},{8,0},{12,4},{16,24},{20,28},{24,16},{28,20},{1,9},{5... | collective-permute-start | bytes 442376 | tf_op jit(solution)/shard_map/ppermute | solution.py:579
  240.7 3.5 %copy-start.22 = (bf16[1,192,768]{2,1,0:T(8,128)(2,1)S(1)}, bf16[1,192,768]{2,1,0:T(8,128)(2,1)}, u32[]{:S(2)}) copy-start(bf16[1,192,768]{2,1,0:T(8,128)(2,1)} %reduce-scatter.2.cloned.1.call-done) | copy-start | bytes 884740
  240.8 4.7 %collective-permute-start.28 = (bf16[4,48,384]{2,1,0:T(8,128)(2,1)S(1)}, bf16[4,48,384]{2,1,0:T(8,128)(2,1)S(1)}, u32[]{:S(2)}, u32[]{:S(2)}) collective-permute-start(bf16[4,48,384]{2,1,0:T(8,128)(2,1)S(1)} %dynamic-slice_bitcast_fusion.1), channel_id=1, source_target_pairs={{0,4},{4,0},{8,12},{12,8},{16,20},{20,16},{24,28},{28,24},{1,5},{5... | collective-permute-start | bytes 442376 | tf_op jit(solution)/shard_map/ppermute | solution.py:579
  242.1 14.6 %collective-permute-start.23 = (bf16[6,16,768]{2,1,0:T(8,128)(2,1)S(1)}, bf16[6,16,768]{2,1,0:T(8,128)(2,1)S(1)}, u32[]{:S(2)}, u32[]{:S(2)}) collective-permute-start(bf16[6,16,768]{2,1,0:T(8,128)(2,1)S(1)} %add_convert_fusion.7), channel_id=1, source_target_pairs={{0,16},{4,20},{8,24},{12,28},{16,0},{20,4},{24,8},{28,12},{1,17},{... | collective-permute-start | bytes 442376 | tf_op jit(solution)/shard_map/ppermute | solution.py:579
  244.2 15.5 %collective-permute-start.35 = (bf16[192,768]{1,0:T(8,128)(2,1)S(1)}, bf16[192,768]{1,0:T(8,128)(2,1)S(1)}, u32[]{:S(2)}, u32[]{:S(2)}) collective-permute-start(bf16[192,768]{1,0:T(8,128)(2,1)S(1)} %bitcast.105), channel_id=1, source_target_pairs={{0,2},{1,3},{2,0},{3,1},{4,6},{5,7},{6,4},{7,5},{8,10},{9,11},{10,... | collective-permute-start | bytes 884744 | tf_op jit(solution)/shard_map/ppermute | solution.py:579
  245.6 3.8 %collective-permute-start.29 = (bf16[2,48,384]{2,1,0:T(8,128)(2,1)S(1)}, bf16[2,48,384]{2,1,0:T(8,128)(2,1)S(1)}, u32[]{:S(2)}, u32[]{:S(2)}) collective-permute-start(bf16[2,48,384]{2,1,0:T(8,128)(2,1)S(1)} %pad_maximum_fusion.5), channel_id=1, source_target_pairs={{0,8},{4,12},{8,0},{12,4},{16,24},{20,28},{24,16},{28,20},{1,9},{5... | collective-permute-start | bytes 221192 | tf_op jit(solution)/shard_map/ppermute | solution.py:579
  246.5 8.9 %collective-permute-start.30 = (bf16[2,48,384]{2,1,0:T(8,128)(2,1)S(1)}, bf16[2,48,384]{2,1,0:T(8,128)(2,1)S(1)}, u32[]{:S(2)}, u32[]{:S(2)}) collective-permute-start(bf16[2,48,384]{2,1,0:T(8,128)(2,1)S(1)} %pad_maximum_fusion.6), channel_id=1, source_target_pairs={{0,16},{4,20},{8,24},{12,28},{16,0},{20,4},{24,8},{28,12},{1,17},{... | collective-permute-start | bytes 221192 | tf_op jit(solution)/shard_map/ppermute | solution.py:579
  248.6 6.9 %collective-permute-start.31 = (bf16[2,48,384]{2,1,0:T(8,128)(2,1)S(1)}, bf16[2,48,384]{2,1,0:T(8,128)(2,1)S(1)}, u32[]{:S(2)}, u32[]{:S(2)}) collective-permute-start(bf16[2,48,384]{2,1,0:T(8,128)(2,1)S(1)} %pad_maximum_fusion.7), channel_id=1, source_target_pairs={{0,24},{4,28},{8,16},{12,20},{16,8},{20,12},{24,0},{28,4},{1,25},{... | collective-permute-start | bytes 221192 | tf_op jit(solution)/shard_map/ppermute | solution.py:579
  255.5 9.1 %copy-start.38 = (bf16[16,96]{1,0:T(8,128)(2,1)S(1)}, bf16[16,96]{1,0:T(8,128)(2,1)}, u32[]{:S(2)}) copy-start(bf16[16,96]{1,0:T(8,128)(2,1)} %multiply_convert_fusion.cond) | copy-start | bytes 9220
  255.5 4.5 %collective-permute-start.32 = (bf16[5,48,384]{2,1,0:T(8,128)(2,1)S(1)}, bf16[5,48,384]{2,1,0:T(8,128)(2,1)S(1)}, u32[]{:S(2)}, u32[]{:S(2)}) collective-permute-start(bf16[5,48,384]{2,1,0:T(8,128)(2,1)S(1)} %fusion.8), channel_id=1, source_target_pairs={{0,2},{1,3},{2,0},{3,1},{4,6},{5,7},{6,4},{7,5},{8,10},{9,11},{10,... | collective-permute-start | bytes 552968 | tf_op jit(solution)/shard_map/ppermute | solution.py:579
  256.7 9.9 %collective-permute-start.34 = (bf16[192,768]{1,0:T(8,128)(2,1)S(1)}, bf16[192,768]{1,0:T(8,128)(2,1)S(1)}, u32[]{:S(2)}, u32[]{:S(2)}) collective-permute-start(bf16[192,768]{1,0:T(8,128)(2,1)S(1)} %bitcast.106), channel_id=1, source_target_pairs={{0,1},{1,0},{2,3},{3,2},{4,5},{5,4},{6,7},{7,6},{8,9},{9,8},{10,11... | collective-permute-start | bytes 884744 | tf_op jit(solution)/shard_map/ppermute | solution.py:579
  259.6 7.0 %copy-start.23 = (bf16[192,768]{1,0:T(8,128)(2,1)}, bf16[192,768]{1,0:T(8,128)(2,1)S(1)}, u32[]{:S(2)}) copy-start(bf16[192,768]{1,0:T(8,128)(2,1)S(1)} %collective-permute-done.35.p2) | copy-start | bytes 884740
  259.6 7.0 %collective-permute-start.36 = (bf16[192,768]{1,0:T(8,128)(2,1)S(1)}, bf16[192,768]{1,0:T(8,128)(2,1)S(1)}, u32[]{:S(2)}, u32[]{:S(2)}) collective-permute-start(bf16[192,768]{1,0:T(8,128)(2,1)S(1)} %collective-permute-done.35.p2), channel_id=1, source_target_pairs={{0,1},{1,0},{2,3},{3,2},{4,5},{5,4},{6,7},{7,6},{8,9},{9,8},{10,11... | collective-permute-start | bytes 884744 | tf_op jit(solution)/shard_map/ppermute | solution.py:579
  260.0 6.6 %copy-start.10 = (bf16[2,5,48,384]{3,2,1,0:T(8,128)(2,1)}, bf16[2,5,48,384]{3,2,1,0:T(8,128)(2,1)S(1)}, u32[]{:S(2)}) copy-start(bf16[2,5,48,384]{3,2,1,0:T(8,128)(2,1)S(1)} %pad_maximum_fusion.2.own) | copy-start | bytes 1105924
  260.0 11.2 %collective-permute-start.33 = (bf16[2,5,48,384]{3,2,1,0:T(8,128)(2,1)S(1)}, bf16[2,5,48,384]{3,2,1,0:T(8,128)(2,1)S(1)}, u32[]{:S(2)}, u32[]{:S(2)}) collective-permute-start(bf16[2,5,48,384]{3,2,1,0:T(8,128)(2,1)S(1)} %pad_maximum_fusion.2.own), channel_id=1, source_target_pairs={{0,1},{1,0},{2,3},{3,2},{4,5},{5,4},{6,7},{7,6},{8,9},{9,8},{10,11... | collective-permute-start | bytes 1105928 | tf_op jit(solution)/shard_map/ppermute | solution.py:579
  (20 other events, 21.4 us)
Sparse Core Ops, SparseCore 0:
  55.0 65.1 all-gather.2
  167.5 72.3 reduce-scatter.1
